TPU v7x, 32 devices: a whole 2x2x4 slice. The times are simulated.
32 devices in a mesh: dp: 8 (over y, x, core), seq: 4 (over z).
Axes of the slice: x: 2, y: 2, z: 4, core: 2. Of those that a mesh axis runs over, the one named last changes fastest.
Arguments:
- hidden_in: bfloat16 [2, 8, 512, 768], P(None, 'dp', 'seq'), may hold values from -6 to 6
- boxes: int32 [2, 2, 8, 512], P(None, None, 'dp', 'seq'), may hold values from 0 to 999
- lengths: int32 [2, 8], P(None, 'dp'), may hold values from 64 to 512, as said below
- w_query: bfloat16 [768, 768], replicated, may hold values from -0.21875 to 0.21875
- w_key: bfloat16 [768, 768], replicated, may hold values from -0.21875 to 0.21875
- w_value: bfloat16 [768, 768], replicated, may hold values from -0.21875 to 0.21875
- w_out: bfloat16 [768, 768], replicated, may hold values from -1.75 to 1.75
- w_rel: bfloat16 [768, 768], replicated, may hold values from -0.21875 to 0.21875
- w_up: bfloat16 [768, 3072], replicated, may hold values from -0.21875 to 0.21875
- b_up: bfloat16 [3072], replicated, may hold values from -3 to 3
- w_down: bfloat16 [3072, 768], replicated, may hold values from -0.109375 to 0.109375
- gain_attn: bfloat16 [768], replicated, may hold values from 0.5 to 1.5
- bias_attn: bfloat16 [768], replicated, may hold values from -2 to 2
- gain_ffn: bfloat16 [768], replicated, may hold values from 0.5 to 1.5
- bias_ffn: bfloat16 [768], replicated, may hold values from -2 to 2
- cotangent: bfloat16 [2, 8, 512, 768], P(None, 'dp', 'seq'), may hold values from -6 to 6
Outputs:
- hidden_out: bfloat16 [2, 8, 512, 768], P(None, 'dp', 'seq')
- input_grad: bfloat16 [2, 8, 512, 768], P(None, 'dp', 'seq')
- grad_w_query: float32 [768, 768], P('dp')
- grad_w_key: float32 [768, 768], P('dp')
- grad_w_value: float32 [768, 768], P('dp')
- grad_w_out: float32 [768, 768], P('dp')
- grad_w_rel: float32 [768, 768], P('dp')
- grad_w_up: float32 [768, 3072], P('dp')
- grad_b_up: float32 [3072], P('dp')
- grad_w_down: float32 [3072, 768], P('dp')
- grad_gain_attn: float32 [768], P('dp')
- grad_bias_attn: float32 [768], P('dp')
- grad_gain_ffn: float32 [768], P('dp')
- grad_bias_ffn: float32 [768], P('dp')
Inputs may be any that keep to these rules, and one draw needn't show every extreme that they name: `lengths`: live tokens of each page; slots at or after it are padding; the first page of each micro-batch is full. `boxes`: quantized box centre coordinates.
All inputs are finite; a program needn't handle non-finite values.
Results may differ from a plain program's by a relative error of at most 0.018.
Values may be sent and summed in bfloat16 or wider, within the bound.
A program may use at most 192 MiB of HBM per device.

v0:
```python
import jax
import jax.numpy as jnp
from jax import lax
from jax.sharding import PartitionSpec as P

HEADS = 12


norm_epsilon = 1e-05


def layer_norm(row_block, gain_vec, shift_vec):
    center = row_block - jnp.mean(row_block, axis=-1, keepdims=True)
    spread = jnp.mean(center * center, axis=-1, keepdims=True)
    return center * lax.rsqrt(spread + norm_epsilon) * gain_vec + shift_vec


def exact_gelu(values_in):
    return jax.nn.gelu(values_in, approximate=False)


def sines(coords, freq_count):
    frequency = 10000.0 ** (-jnp.arange(freq_count, dtype=jnp.float32) / freq_count)
    angles = coords.astype(jnp.float32)[..., None] * frequency
    return (jnp.sin(angles), jnp.cos(angles))


def rotate(rel_in, sine_x, cosine_x, sine_y, cosine_y):
    quarter = sine_x.shape[-1]
    part_one = rel_in[..., 0:quarter]
    part_two = rel_in[..., quarter : 2 * quarter]
    part_three = rel_in[..., 2 * quarter : 3 * quarter]
    part_four = rel_in[..., 3 * quarter : 4 * quarter]
    return jnp.concatenate(
        [
            part_one * sine_x + part_two * cosine_x,
            part_two * sine_x - part_one * cosine_x,
            part_three * sine_y + part_four * cosine_y,
            part_four * sine_y - part_three * cosine_y,
        ],
        axis=-1,
    )


def row_product(left_rows, right_rows):
    return jnp.einsum("rd,rf->df", left_rows, right_rows, preferred_element_type=jnp.float32)


def shards(
    hidden_in,
    boxes,
    lengths,
    w_query,
    w_key,
    w_value,
    w_out,
    w_rel,
    w_up,
    b_up,
    w_down,
    gain_attn,
    bias_attn,
    gain_ffn,
    bias_ffn,
    cotangent,
):
    micro_count, page_count, slab_rows, model_width = hidden_in.shape
    head_dim = model_width // HEADS
    rel_width = w_rel.shape[0]
    quarter = rel_width // 4
    score_scale = head_dim ** (-0.5)
    row_count = page_count * slab_rows
    all_boxes = lax.all_gather(boxes, "seq", axis=3, tiled=True)
    seq_len = all_boxes.shape[3]
    weights = (
        w_query,
        w_key,
        w_value,
        w_out,
        w_rel,
        w_up,
        b_up,
        w_down,
        gain_attn,
        bias_attn,
        gain_ffn,
        bias_ffn,
    )
    totals = [jnp.zeros(item.shape, jnp.float32) for item in weights]
    rel_heads = w_rel.reshape(rel_width, HEADS, head_dim)
    outputs = []
    input_grads = []
    for micro_step in range(micro_count):
        tokens = hidden_in[micro_step].reshape(row_count, model_width)
        query_rows = jnp.dot(tokens, w_query, preferred_element_type=jnp.float32).astype(
            jnp.bfloat16
        )
        key_rows = jnp.dot(tokens, w_key, preferred_element_type=jnp.float32).astype(jnp.bfloat16)
        value_rows = jnp.dot(tokens, w_value, preferred_element_type=jnp.float32).astype(
            jnp.bfloat16
        )
        key_all, value_all = (
            lax.all_gather(
                key_rows.reshape(page_count, slab_rows, model_width), "seq", axis=1, tiled=True
            ),
            lax.all_gather(
                value_rows.reshape(page_count, slab_rows, model_width), "seq", axis=1, tiled=True
            ),
        )
        key_heads = key_all.reshape(page_count, seq_len, HEADS, head_dim)
        value_heads = value_all.reshape(page_count, seq_len, HEADS, head_dim)
        query_heads = query_rows.reshape(page_count, slab_rows, HEADS, head_dim)
        query_sin_x, query_cos_x = sines(boxes[0, micro_step], quarter)
        query_sin_y, query_cos_y = sines(boxes[1, micro_step], quarter)
        key_sin_x, key_cos_x = sines(all_boxes[0, micro_step], quarter)
        key_sin_y, key_cos_y = sines(all_boxes[1, micro_step], quarter)
        key_feat = jnp.concatenate([key_cos_x, key_sin_x, key_cos_y, key_sin_y], axis=-1).astype(
            jnp.bfloat16
        )
        rel_proj = jnp.einsum(
            "pihe,che->pihc", query_heads, rel_heads, preferred_element_type=jnp.float32
        )

        def turn_rel(rel_in):
            return rotate(
                rel_in,
                query_sin_x[:, :, None, :],
                query_cos_x[:, :, None, :],
                query_sin_y[:, :, None, :],
                query_cos_y[:, :, None, :],
            )

        rel_full, turn_pull = jax.vjp(turn_rel, rel_proj)
        rel_query = rel_full.astype(jnp.bfloat16)
        live_keys = jnp.arange(seq_len)[None, :] < lengths[micro_step][:, None]

        def logits_of():
            plain = jnp.einsum(
                "pihe,pjhe->phij", query_heads, key_heads, preferred_element_type=jnp.float32
            )
            extra = jnp.einsum(
                "pihc,pjc->phij", rel_query, key_feat, preferred_element_type=jnp.float32
            )
            return jnp.where(live_keys[:, None, None, :], (plain + extra) * score_scale, -1e30)

        logits = logits_of()
        row_max = jnp.max(logits, axis=-1, keepdims=True)
        log_total = row_max + jnp.log(jnp.sum(jnp.exp(logits - row_max), axis=-1, keepdims=True))
        probs_low = jnp.exp(logits - log_total).astype(jnp.bfloat16)
        attended = jnp.einsum(
            "phij,pjhe->pihe", probs_low, value_heads, preferred_element_type=jnp.float32
        )
        attended = attended.reshape(row_count, model_width).astype(jnp.bfloat16)
        branch = jnp.dot(attended, w_out, preferred_element_type=jnp.float32)
        residual = tokens.astype(jnp.float32) + branch
        normed, norm_pull = jax.vjp(
            layer_norm, residual, gain_attn.astype(jnp.float32), bias_attn.astype(jnp.float32)
        )
        normed_low = normed.astype(jnp.bfloat16)
        up_proj = jnp.dot(normed_low, w_up, preferred_element_type=jnp.float32) + b_up.astype(
            jnp.float32
        )
        active, gelu_pull = jax.vjp(exact_gelu, up_proj)
        active_low = active.astype(jnp.bfloat16)
        down_proj = jnp.dot(active_low, w_down, preferred_element_type=jnp.float32)
        result_rows, final_pull = jax.vjp(
            layer_norm,
            normed + down_proj,
            gain_ffn.astype(jnp.float32),
            bias_ffn.astype(jnp.float32),
        )
        outputs.append(result_rows.astype(jnp.bfloat16).reshape(page_count, slab_rows, model_width))
        d_final = cotangent[micro_step].reshape(row_count, model_width).astype(jnp.float32)
        d_res_two, d_gain_two, d_bias_two = final_pull(d_final)
        d_down = d_res_two.astype(jnp.bfloat16)
        grad_down = row_product(active_low, d_down)
        (d_up_full,) = gelu_pull(jnp.dot(d_down, w_down.T, preferred_element_type=jnp.float32))
        d_up = d_up_full.astype(jnp.bfloat16)
        grad_bias_up = jnp.sum(d_up.astype(jnp.float32), axis=0)
        grad_up = row_product(normed_low, d_up)
        d_normed = d_res_two + jnp.dot(d_up, w_up.T, preferred_element_type=jnp.float32)
        d_res_one, d_gain_one, d_bias_one = norm_pull(d_normed)
        d_branch = d_res_one.astype(jnp.bfloat16)
        grad_out = row_product(attended, d_branch)
        d_attended = jnp.dot(d_branch, w_out.T, preferred_element_type=jnp.float32).astype(
            jnp.bfloat16
        )
        d_attended = d_attended.reshape(page_count, slab_rows, HEADS, head_dim)
        probs_again = jnp.exp(logits_of() - log_total)
        again_low = probs_again.astype(jnp.bfloat16)
        d_value_part = jnp.einsum(
            "phij,pihe->pjhe", again_low, d_attended, preferred_element_type=jnp.float32
        )
        d_prob = jnp.einsum(
            "pihe,pjhe->phij", d_attended, value_heads, preferred_element_type=jnp.float32
        )
        d_logit = probs_again * (d_prob - jnp.sum(probs_again * d_prob, axis=-1, keepdims=True))
        d_logit = d_logit.astype(jnp.bfloat16)
        d_query_att = (
            jnp.einsum("phij,pjhe->pihe", d_logit, key_heads, preferred_element_type=jnp.float32)
            * score_scale
        )
        d_key_part = (
            jnp.einsum("phij,pihe->pjhe", d_logit, query_heads, preferred_element_type=jnp.float32)
            * score_scale
        )
        d_rel_query = (
            jnp.einsum("phij,pjc->pihc", d_logit, key_feat, preferred_element_type=jnp.float32)
            * score_scale
        )
        (d_rel_full,) = turn_pull(d_rel_query)
        d_rel_proj = d_rel_full.astype(jnp.bfloat16)
        grad_rel = jnp.einsum(
            "pihc,pihe->che", d_rel_proj, query_heads, preferred_element_type=jnp.float32
        )
        grad_rel = grad_rel.reshape(rel_width, model_width)
        d_query_full = d_query_att + jnp.einsum(
            "pihc,che->pihe", d_rel_proj, rel_heads, preferred_element_type=jnp.float32
        )
        d_query = d_query_full.reshape(row_count, model_width).astype(jnp.bfloat16)
        d_key_sum, d_value_sum = (
            lax.psum_scatter(
                d_key_part.reshape(page_count, seq_len, model_width).astype(jnp.bfloat16),
                "seq",
                scatter_dimension=1,
                tiled=True,
            ).astype(jnp.float32),
            lax.psum_scatter(
                d_value_part.reshape(page_count, seq_len, model_width).astype(jnp.bfloat16),
                "seq",
                scatter_dimension=1,
                tiled=True,
            ).astype(jnp.float32),
        )
        d_key = d_key_sum.reshape(row_count, model_width).astype(jnp.bfloat16)
        d_value = d_value_sum.reshape(row_count, model_width).astype(jnp.bfloat16)
        grad_query = row_product(tokens, d_query)
        grad_key = row_product(tokens, d_key)
        grad_value = row_product(tokens, d_value)
        d_tokens = (
            d_res_one
            + jnp.dot(d_query, w_query.T, preferred_element_type=jnp.float32)
            + jnp.dot(d_key, w_key.T, preferred_element_type=jnp.float32)
            + jnp.dot(d_value, w_value.T, preferred_element_type=jnp.float32)
        )
        input_grads.append(
            d_tokens.astype(jnp.bfloat16).reshape(page_count, slab_rows, model_width)
        )
        micro_terms = (
            grad_query,
            grad_key,
            grad_value,
            grad_out,
            grad_rel,
            grad_up,
            grad_bias_up,
            grad_down,
            d_gain_one,
            d_bias_one,
            d_gain_two,
            d_bias_two,
        )
        totals = [older + newer for older, newer in zip(totals, micro_terms)]
    group_count = lax.axis_size("dp")
    by_group = jnp.concatenate([item.reshape(group_count, -1) for item in totals], axis=1)
    share_part = lax.psum_scatter(
        by_group.reshape(-1), ("dp", "seq"), scatter_dimension=0, tiled=True
    )
    summed = lax.all_gather(share_part.astype(jnp.bfloat16), "seq", axis=0, tiled=True).astype(
        share_part.dtype
    )
    pieces = []
    offset_at = 0
    for item in totals:
        piece_size = item.size // group_count
        local_shape = (item.shape[0] // group_count,) + tuple(item.shape[1:])
        pieces.append(summed[offset_at : offset_at + piece_size].reshape(local_shape))
        offset_at = offset_at + piece_size
    return (jnp.stack(outputs), jnp.stack(input_grads)) + tuple(pieces)


def solution(mesh):
    placed = (
        P(None, "dp", "seq", None),
        P(None, None, "dp", "seq"),
        P(None, "dp"),
        P(),
        P(),
        P(),
        P(),
        P(),
        P(),
        P(),
        P(),
        P(),
        P(),
        P(),
        P(),
        P(None, "dp", "seq", None),
    )
    return jax.shard_map(
        shards,
        mesh=mesh,
        in_specs=placed,
        out_specs=(
            P(None, "dp", "seq", None),
            P(None, "dp", "seq", None),
            P("dp", None),
            P("dp", None),
            P("dp", None),
            P("dp", None),
            P("dp", None),
            P("dp", None),
            P("dp"),
            P("dp", None),
            P("dp"),
            P("dp"),
            P("dp"),
            P("dp"),
        ),
        check_vma=False,
    )
```

profile of v0, /device:TPU:0, one launch (start us, length us, event | category | flops | bytes accessed | tf_op | source)
XLA Modules:
  0.0 1015.1 jit_solution(5928028593304300660)
XLA Ops:
  9.1 12.9 %all_gather.20 = s32[2,2,1,512]{3,2,1,0:T(1,128)S(1)} all-gather(s32[2,2,1,128]{3,2,1,0:T(1,128)} %param.17), channel_id=1, replica_groups=mesh['dp'=8,'seq'=4] {'seq'}, dimensions={3}, use_global_device_ids=true | all-gather | bytes 10240 | tf_op jit(solution)/shard_map/all_gather | solution.py:73
  22.0 2.5 convolution_convert_fusion.6
  32.0 17.3 %all-gather.3 = bf16[512,768]{1,0:T(8,128)(2,1)} all-gather(bf16[128,768]{1,0:T(8,128)(2,1)S(1)} %convolution_convert_fusion.5), channel_id=5, replica_groups=mesh['dp'=8,'seq'=4] {'seq'}, dimensions={0}, use_global_device_ids=true | all-gather | bytes 983040 | tf_op jit(solution)/shard_map/all_gather | solution.py:103
  54.6 2.9 multiply_sine_fusion.7
  57.5 8.9 fusion.62
  72.2 17.2 %all-gather.2 = bf16[512,768]{1,0:T(8,128)(2,1)} all-gather(bf16[128,768]{1,0:T(8,128)(2,1)S(1)} %copy-done.95), channel_id=4, replica_groups=mesh['dp'=8,'seq'=4] {'seq'}, dimensions={0}, use_global_device_ids=true | all-gather | bytes 983040 | tf_op jit(solution)/shard_map/all_gather | solution.py:106
  90.8 2.9 convolution_convert_fusion.4
  95.2 8.5 multiply_convert_fusion.2
  108.3 4.0 convolution_bitcast_fusion.1
  112.2 17.4 %all-gather.1 = bf16[512,768]{1,0:T(8,128)(2,1)} all-gather(bf16[128,768]{1,0:T(8,128)(2,1)S(1)} %copy-done.94), channel_id=3, replica_groups=mesh['dp'=8,'seq'=4] {'seq'}, dimensions={0}, use_global_device_ids=true | all-gather | bytes 983040 | tf_op jit(solution)/shard_map/all_gather | solution.py:103
  131.9 4.5 fusion.54
  140.6 16.6 %all-gather = bf16[512,768]{1,0:T(8,128)(2,1)} all-gather(bf16[128,768]{1,0:T(8,128)(2,1)S(1)} %copy-done.93), channel_id=2, replica_groups=mesh['dp'=8,'seq'=4] {'seq'}, dimensions={0}, use_global_device_ids=true | all-gather | bytes 983040 | tf_op jit(solution)/shard_map/all_gather | solution.py:106
  158.5 2.7 convolution_convert_fusion.8
  161.9 6.3 multiply_convert_fusion.3
  171.9 2.5 convert_reduce_fusion
  176.1 2.5 convert_reduce_fusion.1
  178.7 2.4 multiply_reduce_fusion.1
  183.5 3.6 convolution_convert_fusion.1
  187.0 4.8 copy.108
  191.8 2.4 copy.124
  195.8 2.6 convolution_convert_fusion
  198.5 3.0 copy.112
  201.4 2.4 copy.122
  203.9 3.1 fusion.7
  208.3 2.9 copy.106
  211.2 2.5 copy.125
  213.8 3.1 fusion.5
  219.2 2.9 copy.110
  222.2 2.5 copy.123
  228.0 3.7 multiply_bitcast_fusion
  231.7 1.9 fusion.135
  237.1 2.5 fusion.144
  239.7 4.4 convolution_bitcast_fusion.3
  244.2 5.1 fusion.133
  249.4 5.1 convolution_add_fusion.1
  256.0 2.2 convolution_bitcast_fusion.2
  258.2 2.9 add_bitcast_fusion
  263.7 1.8 add_bitcast_fusion.3
  265.6 3.2 copy.94
  268.8 3.5 reshape.1173
  272.3 3.3 constant_dynamic-update-slice_fusion.7
  275.6 9.1 convolution_add_fusion
  284.7 1.9 convolution_add_fusion.4
  286.6 8.9 reshape.1177
  295.6 6.5 copy.97
  302.0 5.7 add.302
  307.8 3.6 reshape.1176
  311.5 9.0 reshape.1178
  325.9 1.9 add_bitcast_fusion.1
  327.7 3.0 copy.96
  330.8 3.5 reshape.1175
  336.0 1.8 fusion.97
  339.4 3.6 add_bitcast_fusion.2
  343.0 3.0 copy.95
  346.0 3.5 reshape.1174
  349.6 3.4 constant_dynamic-update-slice_fusion.6
  353.0 3.4 constant_dynamic-update-slice_fusion.5
  360.3 4.9 constant_dynamic-update-slice_fusion.2
  366.5 3.8 constant_dynamic-update-slice_fusion
  375.8 37.2 %reshape.1179 = f32[7673856]{0:T(1024)} reshape(f32[8,959232]{1,0:T(8,128)} %dynamic-update-slice.12) | data formatting | bytes 61390848 | tf_op jit(solution)/shard_map/reshape | solution.py:267
  413.0 492.6 %all-reduce.14 = bf16[7673856]{0:T(1024)(128)(2,1)} all-reduce(f32[7673856]{0:T(1024)} %reshape.1179), channel_id=10, replica_groups=mesh['dp'=8,'seq'=4] {'dp','seq'}, use_global_device_ids=true, to_apply=%region_36.37.clone | all-reduce | flops 7673856 | bytes 46043136
  907.1 4.4 dynamic-update-slice
  912.8 1.9 pad_maximum_fusion
  921.7 72.0 %all-reduce.13.cloned.1.call-done = bf16[959232]{0:T(1024)(128)(2,1)} async-done(((bf16[959232]{0:T(1024)(128)(2,1)}), bf16[959232]{0:T(1024)(128)(2,1)}) %all-reduce.13.cloned.1.call-update) | async-done | bytes 1918480
  (503 shorter events, 101.8 us)
Async XLA Ops:
  7.2 86.6 %copy-start = (bf16[768,768]{1,0:T(8,128)(2,1)S(1)}, bf16[768,768]{1,0:T(8,128)(2,1)}, u32[]{:S(2)}) copy-start(bf16[768,768]{1,0:T(8,128)(2,1)} %param.22) | copy-start | bytes 3538948
  7.2 17.3 %copy-start.6 = (bf16[2,1,128,768]{3,2,1,0:T(8,128)(2,1)S(1)}, bf16[2,1,128,768]{3,2,1,0:T(8,128)(2,1)}, u32[]{:S(2)}) copy-start(bf16[2,1,128,768]{3,2,1,0:T(8,128)(2,1)} %param.16) | copy-start | bytes 1179652
  7.2 17.3 %copy-start.7 = (bf16[768,768]{1,0:T(8,128)(2,1)S(1)}, bf16[768,768]{1,0:T(8,128)(2,1)}, u32[]{:S(2)}) copy-start(bf16[768,768]{1,0:T(8,128)(2,1)} %param.19) | copy-start | bytes 3538948
  7.2 315.0 %reduce-scatter.15.cloned.1.call-start = ((), (), s32[]{:S(2)}) async-start(), calls=%async_computation.6 | async-start | bytes 983040
  30.4 77.9 %copy-start.17 = (bf16[768,768]{0,1:T(8,128)(2,1)}, bf16[768,768]{0,1:T(8,128)(2,1)S(1)}, u32[]{:S(2)}) copy-start(bf16[768,768]{0,1:T(8,128)(2,1)S(1)} %copy.82) | copy-start | bytes 3538948
  50.7 19.0 %copy-start.26 = (bf16[512,768]{0,1:T(8,128)(2,1)}, bf16[512,768]{0,1:T(8,128)(2,1)S(1)}, u32[]{:S(2)}) copy-start(bf16[512,768]{0,1:T(8,128)(2,1)S(1)} %copy.86) | copy-start | bytes 2359300
  52.8 4.7 copy-start.135
  52.8 4.7 copy-start.136
  57.5 10.5 %copy-start.76 = (f32[128,192]{1,0:T(8,128)}, f32[128,192]{1,0:T(8,128)S(1)}, u32[]{:S(2)}) copy-start(f32[128,192]{1,0:T(8,128)S(1)} %get-tuple-element.117) | copy-start | bytes 294916
  57.5 10.5 %copy-start.78 = (f32[128,192]{1,0:T(8,128)}, f32[128,192]{1,0:T(8,128)S(1)}, u32[]{:S(2)}) copy-start(f32[128,192]{1,0:T(8,128)S(1)} %get-tuple-element.118) | copy-start | bytes 294916
  57.5 10.5 %copy-start.80 = (f32[128,192]{1,0:T(8,128)}, f32[128,192]{1,0:T(8,128)S(1)}, u32[]{:S(2)}) copy-start(f32[128,192]{1,0:T(8,128)S(1)} %get-tuple-element.119) | copy-start | bytes 294916
  57.5 10.5 %copy-start.82 = (f32[128,192]{1,0:T(8,128)}, f32[128,192]{1,0:T(8,128)S(1)}, u32[]{:S(2)}) copy-start(f32[128,192]{1,0:T(8,128)S(1)} %get-tuple-element.120) | copy-start | bytes 294916
  93.8 9.9 slice-start.8
  94.3 86.9 %copy-start.15 = (f32[128,768]{1,0:T(8,128)}, f32[128,768]{1,0:T(8,128)S(1)}, u32[]{:S(2)}) copy-start(f32[128,768]{1,0:T(8,128)S(1)} %get-tuple-element.133) | copy-start | bytes 1179652
  94.3 9.4 copy-start.123
  95.1 8.7 copy-start.132
  95.2 8.6 copy-start.128
  95.2 8.6 slice-start.9
  104.7 7.5 copy-start.39
  112.2 19.5 %copy-start.84 = (f32[128,192]{1,0:T(8,128)S(1)}, f32[128,192]{1,0:T(8,128)}, u32[]{:S(2)}) copy-start(f32[128,192]{1,0:T(8,128)} %get-tuple-element.101) | copy-start | bytes 294916
  112.2 19.5 %copy-start.86 = (f32[128,192]{1,0:T(8,128)S(1)}, f32[128,192]{1,0:T(8,128)}, u32[]{:S(2)}) copy-start(f32[128,192]{1,0:T(8,128)} %get-tuple-element.102) | copy-start | bytes 294916
  112.2 19.6 %copy-start.88 = (f32[128,192]{1,0:T(8,128)S(1)}, f32[128,192]{1,0:T(8,128)}, u32[]{:S(2)}) copy-start(f32[128,192]{1,0:T(8,128)} %get-tuple-element.115) | copy-start | bytes 294916
  131.1 7.0 copy-start.28
  140.6 20.6 %copy-start.113 = (f32[12,128]{1,0:T(8,128)}, f32[12,128]{1,0:T(8,128)S(1)}, u32[]{:S(2)}) copy-start(f32[12,128]{1,0:T(8,128)S(1)} %log_add_fusion.1) | copy-start | bytes 18436
  161.2 7.0 slice-start.10
  161.7 19.5 %copy-start.115 = (f32[128]{0:T(128)}, f32[128]{0:T(128)S(1)}, u32[]{:S(2)}) copy-start(f32[128]{0:T(128)S(1)} %broadcast_multiply_fusion.3) | copy-start | bytes 1540
  161.9 19.2 %copy-start.126 = (f32[128]{0:T(128)}, f32[128]{0:T(128)S(1)}, u32[]{:S(2)}) copy-start(f32[128]{0:T(128)S(1)} %fusion.125) | copy-start | bytes 1540
  161.9 6.3 slice-start.11
  171.8 6.9 copy-start.49
  171.8 6.8 copy-start.151
  182.0 12.6 %copy-start.36 = (f32[128,768]{1,0:T(8,128)}, f32[128,768]{1,0:T(8,128)S(1)}, u32[]{:S(2)}) copy-start(f32[128,768]{1,0:T(8,128)S(1)} %get-tuple-element.85) | copy-start | bytes 1179652
  194.3 129.5 %reduce-scatter.19.cloned.1.call-start = ((), (), s32[]{:S(2)}) async-start(), calls=%async_computation.8 | async-start | bytes 983040
  203.9 130.4 %reduce-scatter.13.cloned.1.call-start = ((), (), s32[]{:S(2)}) async-start(), calls=%async_computation.5 | async-start | bytes 983040
  213.8 124.1 %reduce-scatter.17.cloned.1.call-start = ((), (), s32[]{:S(2)}) async-start(), calls=%async_computation.7 | async-start | bytes 983040
  224.6 769.1 %all-reduce.13.cloned.1.call-start = ((), (), s32[]{:S(2)}) async-start(), calls=%async_computation.4 | async-start | bytes 3837952
  244.2 5.2 copy-start.16
  244.2 5.2 copy-start.56
  244.2 5.2 copy-start.125
  244.2 5.2 copy-start.134
  244.2 10.3 %slice-start.12 = ((s8[4718592]{0:T(1024)(128)(4,1)}), s8[4194304]{0:T(1024)(128)(4,1)S(1)}, s32[]{:S(2)}) async-start(s8[4718592]{0:T(1024)(128)(4,1)} %bitcast.400), calls=%async_computation.21 | async-start | bytes 8388608
  249.4 5.2 slice-start.13
  249.4 5.2 copy-start.77
  249.4 5.2 copy-start.79
  249.4 5.2 copy-start.81
  249.4 5.2 copy-start.83
  275.6 9.1 copy-start.21
  275.6 9.1 copy-start.37
  275.6 9.1 copy-start.62
  275.6 9.1 copy-start.143
  311.4 9.1 copy-start.121
  311.4 9.1 copy-start.122
  311.4 9.2 copy-start.119
  311.4 9.2 copy-start.120
  311.4 9.2 copy-start.117
  311.4 9.2 copy-start.118
  311.5 9.3 copy-start.52
  311.5 9.5 copy-start.163
  346.0 13.7 %slice-start = ((s8[9437184]{0:T(1024)(128)(4,1)}), s8[1048576]{0:T(1024)(128)(4,1)S(1)}, s32[]{:S(2)}) async-start(s8[9437184]{0:T(1024)(128)(4,1)} %bitcast.386), calls=%async_computation.9 | async-start | bytes 2097152
  349.6 10.1 slice-start.1
  353.0 5.0 copy-start.20
  358.0 7.8 slice-start.3
  360.3 5.7 slice-start.4
  360.3 6.2 slice-start.5
  998.3 9.9 copy-start.1
  (121 other events, 265.0 us)
Sparse Core Ops, SparseCore 0:
  194.4 23.7 reduce-scatter.14
  220.5 22.6 reduce-scatter.18
  245.6 22.6 reduce-scatter.12
  271.0 22.6 reduce-scatter.16
  912.9 80.7 all-reduce.12
where the time goes:
time: 1020 us
  blocking collectives  574 us (56%)
  local copies, waits for them, and re-layouts  196 us (19%)
  matrix products  121 us (12%)
  waiting for transfers between devices  72.1 us (7%)
  other arithmetic  34.6 us (3%)
  between operations  17.2 us (2%)
    unnamed x1, blocking collectives  493 us
    unnamed x392, local copies, waits for them, and re-layouts  79.7 us
    unnamed x10, waiting for transfers between devices  72.1 us
    reshape x1, local copies, waits for them, and re-layouts, shards(): by_group.reshape(-1)  37.2 us
    all_gather x2, blocking collectives, shards(): lax.all_gather(key_rows.reshape(page_count, slab_rows, model_width), 'seq...  34.7 us
    dot_general x12, matrix products, row_product(): jnp.einsum('rd,rf->df', left_rows, right_rows, preferred_element_type=jnp...  34.6 us
    all_gather x2, blocking collectives, shards(): lax.all_gather(value_rows.reshape(page_count, slab_rows, model_width), 's...  33.7 us
    reshape x6, local copies, waits for them, and re-layouts, shards(): item.reshape(group_count, -1)  32 us
  transfers between devices with their start and end apart: 5, of which 1 were waited for; matrix products, arithmetic and copies ran while one was open for 14% of the time, Pallas kernels for 0%

commit v1 on v0

v1 whole, which is shorter than its diff:
```python
import functools

import jax
import jax.numpy as jnp
import numpy as np
from jax import lax
from jax.experimental import pallas as pl
from jax.experimental.pallas import tpu as pltpu
from jax.sharding import PartitionSpec as P

HEADS = 12
EPS = 1e-05
BF = jnp.bfloat16
F32 = jnp.float32
PAIRS = HEADS // 2
VMEM_LIMIT = 67043328


def nn(a, b):
    return lax.dot_general(a, b, (((1,), (0,)), ((), ())), preferred_element_type=F32)


def nt(a, b):
    return lax.dot_general(a, b, (((1,), (1,)), ((), ())), preferred_element_type=F32)


def tn(a, b):
    return lax.dot_general(a, b, (((0,), (0,)), ((), ())), preferred_element_type=F32)


def trig_tables(quarter):
    freq = 10000.0 ** (-np.arange(quarter) / quarter)
    tables = []
    for step in (32.0, 1.0):
        angle = step * np.arange(32)[:, None] * freq[None, :]
        rest = np.concatenate([np.sin(angle), np.cos(angle)], axis=1).astype(np.float32)
        parts = []
        for _ in range(3):
            part = rest.astype(BF)
            parts.append(part)
            rest = rest - part.astype(np.float32)
        tables.append(np.concatenate(parts, axis=0))
    return tables


def features(bx_ref, hi_ref, lo_ref, sin_ref, cos_ref, feat_ref):
    quarter = hi_ref.shape[1] // 2
    half = 2 * quarter
    iota = lax.broadcasted_iota(jnp.int32, (32, 128), 0)
    hi_tab, lo_tab = hi_ref[...], lo_ref[...]
    for slot in range(4):
        sines, cosines = [], []
        for axis in range(2):
            where = bx_ref[slot, axis : axis + 1, :]
            pick_hi = (iota == lax.shift_right_logical(where, 5)).astype(F32).astype(BF)
            pick_lo = (iota == (where & 31)).astype(F32).astype(BF)
            hi = tn(jnp.concatenate([pick_hi] * 3, axis=0), hi_tab)
            lo = tn(jnp.concatenate([pick_lo] * 3, axis=0), lo_tab)
            sin_hi, cos_hi = hi[:, :quarter], hi[:, quarter:]
            sin_lo, cos_lo = lo[:, :quarter], lo[:, quarter:]
            sines.append(sin_hi * cos_lo + cos_hi * sin_lo)
            cosines.append(cos_hi * cos_lo - sin_hi * sin_lo)
        sine = jnp.concatenate(sines, axis=1)
        cosine = jnp.concatenate(cosines, axis=1)
        rows = pl.ds(128 * slot, 128)
        feat_ref[rows, 0:half] = cosine.astype(BF)
        feat_ref[rows, half : 2 * half] = sine.astype(BF)
        if slot < 2:
            sin_ref[rows, :] = sine
            cos_ref[rows, :] = cosine


def head_stack(pair):
    first = lax.broadcasted_iota(jnp.int32, pair.shape, 1) < 64
    zero = jnp.zeros_like(pair)
    return jnp.concatenate([jnp.where(first, pair, zero), jnp.where(first, zero, pair)], axis=0)


def head_join(stack):
    half = stack.shape[0] // 2
    first = lax.broadcasted_iota(jnp.int32, (half, 128), 1) < 64
    return jnp.where(first, stack[:half], stack[half:])


def attend_pair(pair, live, r):
    cols = pl.ds(pl.multiple_of(128 * pair, 128), 128)
    stack = head_stack(r.q[:, cols].astype(F32) * 0.125).astype(BF)
    sine, cosine = r.sine, r.cosine
    for head in range(2):
        rows = slice(256 * head, 256 * head + 256)
        left = nt(stack[rows], r.wr[0:384, cols])
        right = nt(stack[rows], r.wr[384:768, cols])
        sin, cos = sine[...], cosine[...]
        r.relq[rows, 0:384] = (left * sin + right * cos).astype(BF)
        r.relq[rows, 384:768] = (right * sin - left * cos).astype(BF)
    r.relq[:, 768:896] = stack
    r.feat[:, 768:896] = r.k[:, cols]
    r.score[...] = nt(r.relq[...], r.feat[...])

    for block in range(8):
        rows = pl.ds(64 * block, 64)
        score = jnp.where(live, r.score[rows, :], -1e30)
        top = jnp.max(score, axis=-1, keepdims=True)
        weight = jnp.exp(score - top)
        total = jnp.sum(weight, axis=-1, keepdims=True)
        r.probs[pair, rows, :] = (weight * (1.0 / total)).astype(BF)
    r.att[:, cols] = head_join(nn(r.probs[pair], r.v[:, cols])).astype(BF)


def attend_pair_back(pair, r):
    cols = pl.ds(pl.multiple_of(128 * pair, 128), 128)
    given = head_stack(r.datt[:, cols].astype(F32)).astype(BF)
    stack = head_stack(r.q[:, cols].astype(F32)).astype(BF)
    r.score[...] = nt(given, r.v[:, cols])

    for block in range(8):
        rows = pl.ds(64 * block, 64)
        prob = r.probs[pair, rows, :].astype(F32)
        push = prob * r.score[rows, :]
        mean = jnp.sum(push, axis=-1, keepdims=True)
        r.dlog[rows, :] = ((push - prob * mean) * 0.125).astype(BF)
    r.dv[:, cols] = tn(r.probs[pair], given).astype(BF)
    r.dk[:, cols] = tn(r.dlog[...], stack).astype(BF)
    r.feat[:, 768:896] = r.k[:, cols]
    for head in range(2):
        rows = slice(256 * head, 256 * head + 256)
        first = nn(r.dlog[rows, :], r.feat[:, 0:384])
        second = nn(r.dlog[rows, :], r.feat[:, 384:768])
        sin, cos = r.sine[...], r.cosine[...]
        r.relq[rows, 0:384] = (first * sin - second * cos).astype(BF)
        r.relq[rows, 384:768] = (first * cos + second * sin).astype(BF)
    dq = nn(r.dlog[...], r.feat[:, 768:896]) + nn(r.relq[:, 0:768], r.wr[:, cols])
    r.dq[:, cols] = head_join(dq).astype(BF)
    part = tn(r.relq[:, 0:768], stack).astype(BF)
    for piece, share in enumerate((0, 1, 4, 5, 2, 3, 6, 7)):
        r.g[share % 2, share // 2, 864:960, cols] = part[96 * piece : 96 * piece + 96]


def norm_back(given, hat, scale, gain):
    push = given * gain
    mean = jnp.mean(push, axis=-1, keepdims=True)
    lean = jnp.mean(push * hat, axis=-1, keepdims=True)
    return scale * (push - mean - hat * lean)


def put_shares(g_ref, base, cols, part):
    for share in range(8):
        g_ref[share % 2, share // 2, base : base + 96, cols] = part[
            96 * share : 96 * share + 96
        ].astype(BF)


class Refs:
    pass


def layer_kernel(names, *refs):
    r = Refs()
    for name, ref in zip(names, refs):
        setattr(r, name, ref)
    z = r.info[0]
    length = r.info[1]
    quarter = 192
    for dst, src in ((0, 0), (192, 384), (384, 192), (576, 576)):
        r.wr[dst : dst + 192, :] = r.w_rel[src : src + 192, :]
    features(r.bx, r.hi, r.lo, r.sine, r.cosine, r.feat)

    for tile in range(3):
        cols = slice(256 * tile, 256 * tile + 256)
        r.q[:, cols] = nn(r.x[0:256, :], r.w_query[:, cols]).astype(BF)
        r.k[:, cols] = nn(r.x[...], r.w_key[:, cols]).astype(BF)
        r.v[:, cols] = nn(r.x[...], r.w_value[:, cols]).astype(BF)

    lane = lax.broadcasted_iota(jnp.int32, (1, 128), 1)
    live = jnp.concatenate(
        [lane + 128 * block < length for block in (z, 3 - z, z + 1 - 2 * (z % 2), (z + 2) % 4)],
        axis=1,
    )

    def attend(pair, carry):
        attend_pair(pair, live, r)
        return carry

    lax.fori_loop(0, PAIRS, attend, 0)

    for tile in range(3):
        cols = slice(256 * tile, 256 * tile + 256)
        r.res[:, cols] = r.x[0:256, cols].astype(F32) + nn(r.att[...], r.w_out[:, cols])

    gain1, bias1 = r.gain_attn[...].astype(F32), r.bias_attn[...].astype(F32)
    gain2, bias2 = r.gain_ffn[...].astype(F32), r.bias_ffn[...].astype(F32)
    for block in range(4):
        rows = slice(64 * block, 64 * block + 64)
        res = r.res[rows, :]
        center = res - jnp.mean(res, axis=-1, keepdims=True)
        scale = lax.rsqrt(jnp.mean(center * center, axis=-1, keepdims=True) + EPS)
        hat = center * scale
        r.hat[rows, :] = hat
        r.scale[rows, :] = jnp.broadcast_to(scale, (64, 128))
        normed = hat * gain1 + bias1
        r.res[rows, :] = normed
        r.low[rows, :] = normed.astype(BF)

    def up(tile, carry):
        cols = pl.ds(pl.multiple_of(256 * tile, 256), 256)
        value = nn(r.low[...], r.w_up[:, cols]) + r.b_up[:, cols].astype(F32)
        below = 0.5 * (1.0 + lax.erf(value * np.float32(np.sqrt(0.5))))
        dense = jnp.exp(value * value * -0.5) * np.float32(1.0 / np.sqrt(2.0 * np.pi))
        r.act[:, cols] = (value * below).astype(BF)
        r.slope[:, cols] = below + value * dense
        return carry

    lax.fori_loop(0, 12, up, 0)
    for tile in range(3):
        cols = slice(256 * tile, 256 * tile + 256)
        r.res[:, cols] = r.res[:, cols] + nn(r.act[...], r.w_down[:, cols])

    sums = [jnp.zeros((1, 768), F32) for _ in range(4)]
    for block in range(4):
        rows = slice(64 * block, 64 * block + 64)
        res = r.res[rows, :]
        center = res - jnp.mean(res, axis=-1, keepdims=True)
        scale = lax.rsqrt(jnp.mean(center * center, axis=-1, keepdims=True) + EPS)
        hat = center * scale
        r.out[rows, :] = (hat * gain2 + bias2).astype(BF)
        given = r.cot[rows, :].astype(F32)
        sums[2] = sums[2] + jnp.sum(given * hat, axis=0, keepdims=True)
        sums[3] = sums[3] + jnp.sum(given, axis=0, keepdims=True)
        dres = norm_back(given, hat, scale, gain2)
        r.res[rows, :] = dres
        r.dlow[rows, :] = dres.astype(BF)

    def up_back(tile, carry):
        cols = pl.ds(pl.multiple_of(256 * tile, 256), 256)
        push = nt(r.dlow[...], r.w_down[cols, :]) * r.slope[:, cols]
        low = push.astype(BF)
        r.dup[:, cols] = low
        r.upsum[:, cols] = jnp.sum(low.astype(F32), axis=0, keepdims=True)
        return carry

    lax.fori_loop(0, 12, up_back, 0)
    for row in range(4):
        r.small[row : row + 1, :] = r.upsum[:, 768 * row : 768 * row + 768]

    def grad_down(share, carry):
        cols = pl.ds(pl.multiple_of(384 * share, 128), 384)
        r.g[share % 2, share // 2, 384:768, :] = tn(r.act[:, cols], r.dlow[...]).astype(BF)
        return carry

    lax.fori_loop(0, 8, grad_down, 0)

    def grad_up(tile, carry):
        cols = pl.ds(pl.multiple_of(256 * tile, 256), 256)
        part = tn(r.low[...], r.dup[:, cols])
        base = pl.multiple_of(96 * (tile // 3), 32)
        dest = pl.ds(pl.multiple_of(256 * (tile % 3), 256), 256)
        for share in range(8):
            r.g[share % 2, share // 2, pl.ds(base, 96), dest] = part[
                96 * share : 96 * share + 96
            ].astype(BF)
        return carry

    lax.fori_loop(0, 12, grad_up, 0)
    for tile in range(3):
        cols = slice(256 * tile, 256 * tile + 256)
        r.res[:, cols] = r.res[:, cols] + nt(r.dup[...], r.w_up[cols, :])
    for block in range(4):
        rows = slice(64 * block, 64 * block + 64)
        given, hat = r.res[rows, :], r.hat[rows, :]
        sums[0] = sums[0] + jnp.sum(given * hat, axis=0, keepdims=True)
        sums[1] = sums[1] + jnp.sum(given, axis=0, keepdims=True)
        dres = norm_back(given, hat, r.scale[rows, 0:1], gain1)
        r.res[rows, :] = dres
        r.dlow[rows, :] = dres.astype(BF)
    for row in range(4):
        r.small[4 + row : 5 + row, :] = sums[row]
    for tile in range(3):
        cols = slice(256 * tile, 256 * tile + 256)
        r.datt[:, cols] = nt(r.dlow[...], r.w_out[cols, :]).astype(BF)
        put_shares(r.g, 768, cols, tn(r.att[...], r.dlow[:, cols]))

    def attend_back(pair, carry):
        attend_pair_back(pair, r)
        return carry

    lax.fori_loop(0, PAIRS, attend_back, 0)

    for tile in range(3):
        cols = slice(256 * tile, 256 * tile + 256)
        tail = nt(r.dk[...], r.w_key[cols, :]) + nt(r.dv[...], r.w_value[cols, :])
        r.dx[256:512, cols] = tail[256:512].astype(BF)
        r.dx[0:256, cols] = (
            tail[0:256] + r.res[:, cols] + nt(r.dq[...], r.w_query[cols, :])
        ).astype(BF)
    for tile in range(3):
        cols = slice(256 * tile, 256 * tile + 256)
        put_shares(r.g, 960, cols, tn(r.x[0:256, :], r.dq[:, cols]))
        put_shares(r.g, 1056, cols, tn(r.x[...], r.dk[:, cols]))
        put_shares(r.g, 1152, cols, tn(r.x[...], r.dv[:, cols]))


G_ROWS = 1248

SCRATCH = (
    ("wr", (768, 768), BF),
    ("sine", (256, 384), F32),
    ("cosine", (256, 384), F32),
    ("feat", (512, 896), BF),
    ("q", (256, 768), BF),
    ("k", (512, 768), BF),
    ("v", (512, 768), BF),
    ("att", (256, 768), BF),
    ("relq", (512, 896), BF),
    ("score", (512, 512), F32),
    ("dlog", (512, 512), BF),
    ("probs", (PAIRS, 512, 512), BF),
    ("res", (256, 768), F32),
    ("hat", (256, 768), F32),
    ("scale", (256, 128), F32),
    ("low", (256, 768), BF),
    ("act", (256, 3072), BF),
    ("slope", (256, 3072), F32),
    ("dlow", (256, 768), BF),
    ("dup", (256, 3072), BF),
    ("upsum", (1, 3072), F32),
    ("datt", (256, 768), BF),
    ("dq", (256, 768), BF),
    ("dk", (512, 768), BF),
    ("dv", (512, 768), BF),
)

WEIGHTS = (
    "w_query",
    "w_key",
    "w_value",
    "w_out",
    "w_rel",
    "w_up",
    "b_up",
    "w_down",
    "gain_attn",
    "bias_attn",
    "gain_ffn",
    "bias_ffn",
)


def layer(info, x, bx, cot, weights):
    hi, lo = trig_tables(192)
    rows = [w if w.ndim == 2 else w.reshape(1, -1) for w in weights]
    names_in = ("info", "x", "bx", "cot", "hi", "lo") + WEIGHTS
    outs = (
        ("out", (256, 768), BF),
        ("dx", (512, 768), BF),
        ("g", (2, 4, G_ROWS, 768), BF),
        ("small", (8, 768), F32),
    )
    names = names_in + tuple(o[0] for o in outs) + tuple(s[0] for s in SCRATCH)
    vmem = pl.BlockSpec(memory_space=pltpu.VMEM)
    return pl.pallas_call(
        functools.partial(layer_kernel, names),
        out_shape=[jax.ShapeDtypeStruct(o[1], o[2]) for o in outs],
        in_specs=[pl.BlockSpec(memory_space=pltpu.SMEM)] + [vmem] * (len(names_in) - 1),
        out_specs=[vmem] * len(outs),
        scratch_shapes=[pltpu.VMEM(s[1], s[2]) for s in SCRATCH],
        compiler_params=pltpu.CompilerParams(vmem_limit_bytes=VMEM_LIMIT),
        name="layer",
    )(info, x, bx, cot, jnp.asarray(hi), jnp.asarray(lo), *rows)


def swap(value, axis, count, bit):
    return lax.ppermute(value, axis, [(i, i ^ bit) for i in range(count)])


def pick(stacked, index):
    return lax.dynamic_index_in_dim(stacked, index, 0, keepdims=False)


def reduce_grads(g, small):
    dp = lax.axis_index("dp")
    core, xbit, ybit = dp % 2, (dp // 2) % 2, dp // 4
    got = swap(pick(g, 1 - core), "dp", 8, 1)
    mine = (pick(g, core) + got).reshape(2, 2, G_ROWS, 768)
    cut = G_ROWS // 2
    a, b = mine[:, :, :cut], mine[:, :, cut:]
    a_x = jnp.swapaxes(a, 0, 1)
    got_a = swap(pick(a_x, 1 - xbit), "dp", 8, 2)
    got_b = swap(pick(b, 1 - ybit), "dp", 8, 4)
    a = pick(a_x, xbit) + got_a
    b = pick(b, ybit) + got_b
    got_a = swap(pick(a, 1 - ybit), "dp", 8, 4)
    got_b = swap(pick(b, 1 - xbit), "dp", 8, 2)
    share = jnp.concatenate([pick(a, ybit) + got_a, pick(b, xbit) + got_b], axis=0)
    z = lax.axis_index("seq")
    low = z % 2
    halves = share.reshape(2, cut, 768)
    part = pick(halves, low) + swap(pick(halves, 1 - low), "seq", 4, 1)
    part = part + swap(part, "seq", 4, 2)
    other = swap(part, "seq", 4, 1)
    share = jnp.where(low == 0, jnp.concatenate([part, other]), jnp.concatenate([other, part]))
    for axis, count, bit in (
        ("dp", 8, 1),
        ("dp", 8, 2),
        ("dp", 8, 4),
        ("seq", 4, 1),
        ("seq", 4, 2),
    ):
        small = small + swap(small, axis, count, bit)
    return share.astype(F32), small


def reduce_grads_any(g, small):
    order = g.transpose(1, 0, 2, 3).reshape(8, G_ROWS, 768)

    def weight(base):
        return order[:, base : base + 96].reshape(768, 768)

    up = jnp.concatenate([weight(96 * j) for j in range(4)], axis=1)
    down = order[:, 384:768].reshape(3072, 768)
    full = [weight(960), weight(1056), weight(1152), weight(768), weight(864), up, down]
    scattered = [
        lax.psum(lax.psum_scatter(w, "dp", scatter_dimension=0, tiled=True), "seq").astype(F32)
        for w in full
    ]
    return scattered, lax.psum(small, ("dp", "seq"))


def shards(hidden_in, boxes, lengths, *rest):
    weights, cotangent = rest[:-1], rest[-1]
    micro_count, _, rows, width = hidden_in.shape
    x, cot = hidden_in[:, 0], cotangent[:, 0]
    box = boxes[:, :, 0].transpose(1, 0, 2)
    z = lax.axis_index("seq")
    micro = z // 2
    got_x, got_box = [pick(x, micro)], [pick(box, micro)]
    for bit in (3, 1, 2):
        peer = (z ^ bit) // 2
        got_x.append(swap(pick(x, peer), "seq", 4, bit))
        got_box.append(swap(pick(box, peer), "seq", 4, bit))
    got_cot = [pick(cot, micro), swap(pick(cot, 1 - micro), "seq", 4, 3)]
    info = jnp.stack([z, pick(lengths[:, 0], micro)]).astype(jnp.int32)
    out, dx, g, small = layer(
        info, jnp.concatenate(got_x), jnp.stack(got_box), jnp.concatenate(got_cot), weights
    )
    other_out = swap(out[rows:], "seq", 4, 3)
    own_dx = dx[:rows].astype(F32) + swap(dx[2 * rows : 3 * rows], "seq", 4, 1).astype(F32)
    other_dx = swap(dx[rows : 2 * rows], "seq", 4, 3).astype(F32) + swap(
        dx[3 * rows :], "seq", 4, 2
    ).astype(F32)

    def by_micro(own, other):
        own, other = own.astype(BF), other.astype(BF)
        both = jnp.where(micro == 0, jnp.stack([own, other]), jnp.stack([other, own]))
        return both[:, None]

    hidden = by_micro(out[:rows], other_out)
    dinput = by_micro(own_dx, other_dx)
    dp_count = lax.axis_size("dp")
    if dp_count == 8:
        share, small = reduce_grads(g, small)
        up = jnp.concatenate([share[96 * j : 96 * j + 96] for j in range(4)], axis=1)
        grads = [
            share[960:1056],
            share[1056:1152],
            share[1152:1248],
            share[768:864],
            share[864:960],
            up,
            share[384:768],
        ]
    else:
        grads, small = reduce_grads_any(g, small)
    dp = lax.axis_index("dp")

    def own_part(vector):
        size = vector.shape[0] // dp_count
        return lax.dynamic_slice_in_dim(vector, dp * size, size)

    small = [own_part(small[0:4].reshape(-1))] + [own_part(small[4 + i]) for i in range(4)]
    return (hidden, dinput, *grads[:6], small[0], grads[6], *small[1:])


def solution(mesh):
    rows = P(None, "dp", "seq", None)
    placed = (rows, P(None, None, "dp", "seq"), P(None, "dp")) + (P(),) * 12 + (rows,)
    matrix, vector = P("dp", None), P("dp")
    return jax.shard_map(
        shards,
        mesh=mesh,
        in_specs=placed,
        out_specs=(rows, rows) + (matrix,) * 6 + (vector, matrix) + (vector,) * 4,
        check_vma=False,
    )
```

time: 1020 us -> 322 us (0.32)
  blocking collectives: 574 us -> 0 us
  local copies, waits for them, and re-layouts: 196 us -> 33 us
  matrix products: 121 us -> 0 us
  waiting for transfers between devices: 72.1 us -> 166 us
  Pallas kernels: 0 us -> 60.8 us
  starting transfers between devices: 0.42 us -> 34.7 us
  between operations: 17.2 us -> 0.97 us
    unnamed x1 -> x0, blocking collectives: 493 us -> none
    ppermute x0 -> x24, waiting for transfers between devices: none -> 166 us  [swap(): return lax.ppermute(value, axis, [(i, i ^ bit) for i in range(count)])]
    dot_general x58 -> x0, matrix products: 121 us -> none  [the longest x12 34.6 us: row_product(): jnp.einsum('rd,rf->df', left_rows, right_rows, preferred_element_type=jnp...]
    all_gather x5 -> x0, blocking collectives: 81.3 us -> none  [the longest x2 34.7 us: shards(): lax.all_gather(key_rows.reshape(page_count, slab_rows, model_width), 'seq...]
    unnamed x392 -> x24, local copies, waits for them, and re-layouts: 79.7 us -> 3.07 us
    unnamed x10 -> x0, waiting for transfers between devices: 72.1 us -> none
    reshape x9 -> x6, local copies, waits for them, and re-layouts: 71.6 us -> 2.96 us  [the longest x5 2.95 us: layer(): rows = [w if w.ndim == 2 else w.reshape(1, -1) for w in weights]]
    pallas_call x0 -> x1, Pallas kernels: none -> 60.8 us  [layer(): pl.pallas_call(functools.partial(layer_kernel, names), out_shape=[jax.Sha...]
  transfers between devices with their start and end apart: 5 -> 24, of which waited for: 1 -> 13; matrix products, arithmetic and copies ran while one was open for 14% -> 8% of each run, Pallas kernels for 0% -> 0%
where the time goes in v1:
time: 322 us
  waiting for transfers between devices  166 us (52%)
  Pallas kernels  60.8 us (19%)
  starting transfers between devices  34.7 us (11%)
  local copies, waits for them, and re-layouts  33 us (10%)
  other arithmetic  26.6 us (8%)
    ppermute x24, waiting for transfers between devices, swap(): return lax.ppermute(value, axis, [(i, i ^ bit) for i in range(count)])  166 us
    pallas_call x1, Pallas kernels, layer(): pl.pallas_call(functools.partial(layer_kernel, names), out_shape=[jax.Sha...  60.8 us
    ppermute x24, starting transfers between devices, swap(): return lax.ppermute(value, axis, [(i, i ^ bit) for i in range(count)])  34.7 us
    squeeze x8, local copies, waits for them, and re-layouts, pick(): return lax.dynamic_index_in_dim(stacked, index, 0, keepdims=False)  14.3 us
    add x1, other arithmetic, reduce_grads(): mine = (pick(g, core) + got).reshape(2, 2, G_ROWS, 768)  9.25 us
  transfers between devices with their start and end apart: 24, of which 13 were waited for; matrix products, arithmetic and copies ran while one was open for 8% of the time, Pallas kernels for 0%

profile of v1, /device:TPU:0, one launch (start us, length us, event | category | flops | bytes accessed | tf_op | source)
XLA Modules:
  0.0 321.9 jit_solution(18102140852128222941)
XLA Ops:
  0.8 0.8 constant_dynamic-slice_fusion.7
  1.6 5.1 %collective-permute-start.3 = (s32[2,128]{1,0:T(2,128)S(1)}, s32[2,128]{1,0:T(2,128)S(1)}, u32[]{:S(2)}, u32[]{:S(2)}) collective-permute-start(s32[2,128]{1,0:T(2,128)S(1)} %bitcast.68), channel_id=1, source_target_pairs={{0,3},{1,2},{2,1},{3,0},{4,7},{5,6},{6,5},{7,4},{8,11},{9,10},{10,... | collective-permute-start | bytes 3080 | tf_op jit(solution)/shard_map/ppermute | solution.py:372
  7.2 1.0 dynamic-slice_bitcast_fusion.7
  8.3 3.9 %collective-permute-start.6 = (bf16[128,768]{1,0:T(8,128)(2,1)S(1)}, bf16[128,768]{1,0:T(8,128)(2,1)S(1)}, u32[]{:S(2)}, u32[]{:S(2)}) collective-permute-start(bf16[128,768]{1,0:T(8,128)(2,1)S(1)} %get-tuple-element.39), channel_id=1, source_target_pairs={{0,3},{1,2},{2,1},{3,0},{4,7},{5,6},{6,5},{7,4},{8,11},{9,10},{10,... | collective-permute-start | bytes 589832 | tf_op jit(solution)/shard_map/ppermute | solution.py:372
  12.2 1.3 dynamic-slice_bitcast_fusion.11
  13.5 0.6 constant_dynamic-slice_fusion.8
  14.1 1.2 pad_add_fusion.1.refs_0_
  17.1 0.6 reshape.210.refs_17_
  17.7 0.6 reshape.206.refs_12_
  18.9 3.8 %collective-permute-start.1 = (bf16[128,768]{1,0:T(8,128)(2,1)S(1)}, bf16[128,768]{1,0:T(8,128)(2,1)S(1)}, u32[]{:S(2)}, u32[]{:S(2)}) collective-permute-start(bf16[128,768]{1,0:T(8,128)(2,1)S(1)} %get-tuple-element.43), channel_id=1, source_target_pairs={{0,1},{1,0},{2,3},{3,2},{4,5},{5,4},{6,7},{7,6},{8,9},{9,8},{10,11... | collective-permute-start | bytes 589832 | tf_op jit(solution)/shard_map/ppermute | solution.py:372
  22.7 0.6 pad_add_fusion.refs_2_
  23.3 0.8 pad_maximum_fusion.3.refs_3_
  24.1 12.3 %collective-permute-done.2 = bf16[128,768]{1,0:T(8,128)(2,1)S(1)} collective-permute-done((bf16[128,768]{1,0:T(8,128)(2,1)S(1)}, bf16[128,768]{1,0:T(8,128)(2,1)S(1)}, u32[]{:S(2)}, u32[]{:S(2)}) %collective-permute-start.2) | collective-permute-done | bytes 196640 | tf_op jit(solution)/shard_map/ppermute | solution.py:372
  36.4 0.9 pad_maximum_fusion.2.refs_1_
  37.3 60.8 %layer.1 = (bf16[256,768]{1,0:T(8,128)(2,1)}, bf16[512,768]{1,0:T(8,128)(2,1)}, bf16[2,4,1248,768]{3,2,1,0:T(8,128)(2,1)}, f32[8,768]{1,0:T(8,128)}) custom-call(s32[2]{0:T(128)} %pad_add_fusion.1.refs_0_, bf16[512,768]{1,0:T(8,128)(2,1)} %pad_maximum_fusion.2.refs_1_, s32[4,2,128]{2,1,0:T(2,128)} %pad_add_fusion.refs_2_, ...), custom_call_target="tpu_custom_call" | custom-call | tf_op jit(solution)/shard_map/layer/pallas_call | solution.py:360
  98.1 6.8 %dynamic-slice_bitcast_fusion = bf16[4,1248,768]{2,1,0:T(8,128)(2,1)} fusion(bf16[2,4,1248,768]{3,2,1,0:T(8,128)(2,1)} %get-tuple-element.20, s32[]{:T(128)S(6)} %select_n.148), kind=kLoop, calls=%fused_computation.1 | loop fusion | bytes 15335428 | tf_op jit(solution)/shard_map/jit(dynamic_index_in_dim)/squeeze | solution.py:376
  104.9 12.5 %collective-permute-done.11 = bf16[4,1248,768]{2,1,0:T(8,128)(2,1)} collective-permute-done((bf16[4,1248,768]{2,1,0:T(8,128)(2,1)}, bf16[4,1248,768]{2,1,0:T(8,128)(2,1)}, u32[]{:S(2)}, u32[]{:S(2)}) %collective-permute-start.11) | collective-permute-done | bytes 7667744 | tf_op jit(solution)/shard_map/ppermute | solution.py:372
  117.4 9.3 %bitcast_add_fusion = bf16[4,1248,768]{2,1,0:T(8,128)(2,1)} fusion(bf16[4,1248,768]{2,1,0:T(8,128)(2,1)} %collective-permute-done.11, bf16[2,4,1248,768]{3,2,1,0:T(8,128)(2,1)} %get-tuple-element.20, s32[]{:T(128)S(6)} %select_n.147), kind=kLoop, calls=%fused_computation | loop fusion | flops 3833856 | bytes 23003140 | tf_op jit(solution)/shard_map/add | solution.py:383
  126.7 4.8 %fusion.7 = (bf16[2,2,624,768]{3,2,1,0:T(8,128)(2,1)}, bf16[2,2,624,768]{3,2,1,0:T(8,128)(2,1)S(1)}) fusion(bf16[2,2,1248,768]{3,2,1,0:T(8,128)(2,1)} %bitcast.62), kind=kLoop, calls=%fused_computation.46 | loop fusion | bytes 15335424 | tf_op jit(solution)/shard_map/slice | solution.py:385
  131.6 1.7 copy-done.1
  133.3 1.5 collective-permute-start.14
  134.8 3.0 dynamic-slice_bitcast_fusion.2
  137.8 1.5 collective-permute-start.12
  139.3 37.9 %collective-permute-done.14 = bf16[2,624,768]{2,1,0:T(8,128)(2,1)} collective-permute-done((bf16[2,624,768]{2,1,0:T(8,128)(2,1)S(1)}, bf16[2,624,768]{2,1,0:T(8,128)(2,1)}, u32[]{:S(2)}, u32[]{:S(2)}) %collective-permute-start.14) | collective-permute-done | bytes 1916960 | tf_op jit(solution)/shard_map/ppermute | solution.py:372
  177.2 2.4 bitcast_add_fusion.1
  179.7 1.0 dynamic-slice_bitcast_fusion.4
  180.7 1.5 collective-permute-start.15
  182.2 1.8 bitcast_add_fusion.2
  184.0 1.3 copy-done.2
  185.3 1.0 dynamic-slice_bitcast_fusion.5
  186.3 1.5 collective-permute-start.13
  187.8 15.5 %collective-permute-done.15 = bf16[624,768]{1,0:T(8,128)(2,1)S(1)} collective-permute-done((bf16[624,768]{1,0:T(8,128)(2,1)}, bf16[624,768]{1,0:T(8,128)(2,1)S(1)}, u32[]{:S(2)}, u32[]{:S(2)}) %collective-permute-start.15) | collective-permute-done | bytes 958496 | tf_op jit(solution)/shard_map/ppermute | solution.py:372
  203.4 5.3 %collective-permute-done.13 = bf16[624,768]{1,0:T(8,128)(2,1)} collective-permute-done((bf16[624,768]{1,0:T(8,128)(2,1)}, bf16[624,768]{1,0:T(8,128)(2,1)}, u32[]{:S(2)}, u32[]{:S(2)}) %collective-permute-start.13) | collective-permute-done | bytes 958496 | tf_op jit(solution)/shard_map/ppermute | solution.py:372
  208.7 1.3 bitcast_add_fusion.5
  210.4 21.4 %collective-permute-done.16 = bf16[624,768]{1,0:T(8,128)(2,1)} collective-permute-done((bf16[624,768]{1,0:T(8,128)(2,1)S(1)}, bf16[624,768]{1,0:T(8,128)(2,1)}, u32[]{:S(2)}, u32[]{:S(2)}) %collective-permute-start.16) | collective-permute-done | bytes 958496 | tf_op jit(solution)/shard_map/ppermute | solution.py:372
  231.7 1.3 bitcast_add_fusion.3
  233.0 1.2 collective-permute-start.17
  234.3 1.2 collective-permute-done.19
  235.5 0.9 collective-permute-start.20
  236.4 2.9 collective-permute-done.20
  239.3 1.5 collective-permute-start.21
  240.8 2.3 collective-permute-done.21
  243.1 1.8 collective-permute-start.22
  244.9 0.7 slice_bitcast_fusion
  245.6 1.4 collective-permute-start.7
  247.0 9.3 %collective-permute-done.22 = f32[8,768]{1,0:T(8,128)S(1)} collective-permute-done((f32[8,768]{1,0:T(8,128)S(1)}, f32[8,768]{1,0:T(8,128)S(1)}, u32[]{:S(2)}, u32[]{:S(2)}) %collective-permute-start.22) | collective-permute-done | bytes 24608 | tf_op jit(solution)/shard_map/ppermute | solution.py:372
  256.4 1.7 collective-permute-start.23
  258.0 1.8 fusion.9
  259.9 0.8 collective-permute-start.8
  260.7 2.9 collective-permute-start.10
  263.6 25.3 %collective-permute-done.23 = f32[8,768]{1,0:T(8,128)S(1)} collective-permute-done((f32[8,768]{1,0:T(8,128)S(1)}, f32[8,768]{1,0:T(8,128)S(1)}, u32[]{:S(2)}, u32[]{:S(2)}) %collective-permute-start.23) | collective-permute-done | bytes 24608 | tf_op jit(solution)/shard_map/ppermute | solution.py:372
  288.8 2.3 collective-permute-start.9
  291.6 0.7 dynamic_slice.109
  292.2 0.6 fusion.5
  292.8 0.6 fusion.3
  293.4 1.8 maximum_select_fusion.1
  295.2 1.1 fusion.1
  296.3 2.2 collective-permute-done.9
  298.5 1.1 fusion.2
  299.6 0.8 maximum_select_fusion.2
  300.4 17.6 %collective-permute-done.18 = bf16[624,768]{1,0:T(8,128)(2,1)S(1)} collective-permute-done((bf16[624,768]{1,0:T(8,128)(2,1)S(1)}, bf16[624,768]{1,0:T(8,128)(2,1)S(1)}, u32[]{:S(2)}, u32[]{:S(2)}) %collective-permute-start.18) | collective-permute-done | bytes 958496 | tf_op jit(solution)/shard_map/ppermute | solution.py:372
  318.5 1.1 slice.104
  319.6 1.1 fusion.8
  320.7 1.1 pad_maximum_fusion.1
  (58 shorter events, 4.5 us)
Async XLA Ops:
  0.6 12.9 %copy-start.11 = (s32[2,1]{0,1:T(1,128)S(1)}, s32[2,1]{0,1:T(1,128)}, u32[]{:S(2)}) copy-start(s32[2,1]{0,1:T(1,128)} %param.20) | copy-start | bytes 28
  0.7 14.7 %copy-start.7 = (bf16[768]{0:T(1024)(128)(2,1)S(1)}, bf16[768]{0:T(1024)(128)(2,1)}, u32[]{:S(2)}) copy-start(bf16[768]{0:T(1024)(128)(2,1)} %param.29) | copy-start | bytes 4612
  0.7 15.3 %copy-start.8 = (bf16[768]{0:T(1024)(128)(2,1)S(1)}, bf16[768]{0:T(1024)(128)(2,1)}, u32[]{:S(2)}) copy-start(bf16[768]{0:T(1024)(128)(2,1)} %param.30) | copy-start | bytes 4612
  0.7 15.8 %copy-start.9 = (bf16[768]{0:T(1024)(128)(2,1)S(1)}, bf16[768]{0:T(1024)(128)(2,1)}, u32[]{:S(2)}) copy-start(bf16[768]{0:T(1024)(128)(2,1)} %param.31) | copy-start | bytes 4612
  0.7 16.4 %copy-start.10 = (bf16[768]{0:T(1024)(128)(2,1)S(1)}, bf16[768]{0:T(1024)(128)(2,1)}, u32[]{:S(2)}) copy-start(bf16[768]{0:T(1024)(128)(2,1)} %param.32) | copy-start | bytes 4612
  0.7 17.0 %copy-start.6 = (bf16[3072]{0:T(1024)(128)(2,1)S(1)}, bf16[3072]{0:T(1024)(128)(2,1)}, u32[]{:S(2)}) copy-start(bf16[3072]{0:T(1024)(128)(2,1)} %param.27) | copy-start | bytes 18436
  1.6 16.7 %collective-permute-start.3 = (s32[2,128]{1,0:T(2,128)S(1)}, s32[2,128]{1,0:T(2,128)S(1)}, u32[]{:S(2)}, u32[]{:S(2)}) collective-permute-start(s32[2,128]{1,0:T(2,128)S(1)} %bitcast.68), channel_id=1, source_target_pairs={{0,3},{1,2},{2,1},{3,0},{4,7},{5,6},{6,5},{7,4},{8,11},{9,10},{10,... | collective-permute-start | bytes 3080 | tf_op jit(solution)/shard_map/ppermute | solution.py:372
  6.7 12.2 %collective-permute-start.5 = (s32[2,128]{1,0:T(2,128)S(1)}, s32[2,128]{1,0:T(2,128)S(1)}, u32[]{:S(2)}, u32[]{:S(2)}) collective-permute-start(s32[2,128]{1,0:T(2,128)S(1)} %bitcast.67), channel_id=1, source_target_pairs={{0,2},{1,3},{2,0},{3,1},{4,6},{5,7},{6,4},{7,5},{8,10},{9,11},{10,... | collective-permute-start | bytes 3080 | tf_op jit(solution)/shard_map/ppermute | solution.py:372
  6.7 16.0 %collective-permute-start.4 = (s32[2,128]{1,0:T(2,128)S(1)}, s32[2,128]{1,0:T(2,128)S(1)}, u32[]{:S(2)}, u32[]{:S(2)}) collective-permute-start(s32[2,128]{1,0:T(2,128)S(1)} %bitcast.66), channel_id=1, source_target_pairs={{0,1},{1,0},{2,3},{3,2},{4,5},{5,4},{6,7},{7,6},{8,9},{9,8},{10,11... | collective-permute-start | bytes 3080 | tf_op jit(solution)/shard_map/ppermute | solution.py:372
  8.3 15.0 %collective-permute-start.6 = (bf16[128,768]{1,0:T(8,128)(2,1)S(1)}, bf16[128,768]{1,0:T(8,128)(2,1)S(1)}, u32[]{:S(2)}, u32[]{:S(2)}) collective-permute-start(bf16[128,768]{1,0:T(8,128)(2,1)S(1)} %get-tuple-element.39), channel_id=1, source_target_pairs={{0,3},{1,2},{2,1},{3,0},{4,7},{5,6},{6,5},{7,4},{8,11},{9,10},{10,... | collective-permute-start | bytes 589832 | tf_op jit(solution)/shard_map/ppermute | solution.py:372
  13.4 10.6 %collective-permute-start = (bf16[128,768]{1,0:T(8,128)(2,1)S(1)}, bf16[128,768]{1,0:T(8,128)(2,1)S(1)}, u32[]{:S(2)}, u32[]{:S(2)}) collective-permute-start(bf16[128,768]{1,0:T(8,128)(2,1)S(1)} %get-tuple-element.41), channel_id=1, source_target_pairs={{0,3},{1,2},{2,1},{3,0},{4,7},{5,6},{6,5},{7,4},{8,11},{9,10},{10,... | collective-permute-start | bytes 589832 | tf_op jit(solution)/shard_map/ppermute | solution.py:372
  18.3 18.1 %collective-permute-start.2 = (bf16[128,768]{1,0:T(8,128)(2,1)S(1)}, bf16[128,768]{1,0:T(8,128)(2,1)S(1)}, u32[]{:S(2)}, u32[]{:S(2)}) collective-permute-start(bf16[128,768]{1,0:T(8,128)(2,1)S(1)} %get-tuple-element.42), channel_id=1, source_target_pairs={{0,2},{1,3},{2,0},{3,1},{4,6},{5,7},{6,4},{7,5},{8,10},{9,11},{10,... | collective-permute-start | bytes 589832 | tf_op jit(solution)/shard_map/ppermute | solution.py:372
  18.9 17.5 %collective-permute-start.1 = (bf16[128,768]{1,0:T(8,128)(2,1)S(1)}, bf16[128,768]{1,0:T(8,128)(2,1)S(1)}, u32[]{:S(2)}, u32[]{:S(2)}) collective-permute-start(bf16[128,768]{1,0:T(8,128)(2,1)S(1)} %get-tuple-element.43), channel_id=1, source_target_pairs={{0,1},{1,0},{2,3},{3,2},{4,5},{5,4},{6,7},{7,6},{8,9},{9,8},{10,11... | collective-permute-start | bytes 589832 | tf_op jit(solution)/shard_map/ppermute | solution.py:372
  104.9 12.5 %collective-permute-start.11 = (bf16[4,1248,768]{2,1,0:T(8,128)(2,1)}, bf16[4,1248,768]{2,1,0:T(8,128)(2,1)}, u32[]{:S(2)}, u32[]{:S(2)}) collective-permute-start(bf16[4,1248,768]{2,1,0:T(8,128)(2,1)} %dynamic-slice_bitcast_fusion), channel_id=1, source_target_pairs={{0,4},{4,0},{8,12},{12,8},{16,20},{20,16},{24,28},{28,24},{1,5},{5... | collective-permute-start | bytes 23003144 | tf_op jit(solution)/shard_map/ppermute | solution.py:372
  131.4 1.9 copy-start.1
  133.3 43.9 %collective-permute-start.14 = (bf16[2,624,768]{2,1,0:T(8,128)(2,1)S(1)}, bf16[2,624,768]{2,1,0:T(8,128)(2,1)}, u32[]{:S(2)}, u32[]{:S(2)}) collective-permute-start(bf16[2,624,768]{2,1,0:T(8,128)(2,1)S(1)} %dynamic-slice_bitcast_fusion.1), channel_id=1, source_target_pairs={{0,16},{4,20},{8,24},{12,28},{16,0},{20,4},{24,8},{28,12},{1,17},{... | collective-permute-start | bytes 5750792 | tf_op jit(solution)/shard_map/ppermute | solution.py:372
  137.8 44.4 %collective-permute-start.12 = (bf16[2,624,768]{2,1,0:T(8,128)(2,1)}, bf16[2,624,768]{2,1,0:T(8,128)(2,1)}, u32[]{:S(2)}, u32[]{:S(2)}) collective-permute-start(bf16[2,624,768]{2,1,0:T(8,128)(2,1)} %dynamic-slice_bitcast_fusion.2), channel_id=1, source_target_pairs={{0,8},{4,12},{8,0},{12,4},{16,24},{20,28},{24,16},{28,20},{1,9},{5... | collective-permute-start | bytes 5750792 | tf_op jit(solution)/shard_map/ppermute | solution.py:372
  177.2 5.0 %copy-start = (bf16[2,2,624,768]{3,2,1,0:T(8,128)(2,1)S(1)}, bf16[2,2,624,768]{3,2,1,0:T(8,128)(2,1)}, u32[]{:S(2)}) copy-start(bf16[2,2,624,768]{3,2,1,0:T(8,128)(2,1)} %get-tuple-element.22) | copy-start | bytes 11501572
  180.7 22.6 %collective-permute-start.15 = (bf16[624,768]{1,0:T(8,128)(2,1)}, bf16[624,768]{1,0:T(8,128)(2,1)S(1)}, u32[]{:S(2)}, u32[]{:S(2)}) collective-permute-start(bf16[624,768]{1,0:T(8,128)(2,1)} %dynamic-slice_bitcast_fusion.4), channel_id=1, source_target_pairs={{0,8},{4,12},{8,0},{12,4},{16,24},{20,28},{24,16},{28,20},{1,9},{5... | collective-permute-start | bytes 2875400 | tf_op jit(solution)/shard_map/ppermute | solution.py:372
  184.0 1.3 copy-start.2
  186.3 22.5 %collective-permute-start.13 = (bf16[624,768]{1,0:T(8,128)(2,1)}, bf16[624,768]{1,0:T(8,128)(2,1)}, u32[]{:S(2)}, u32[]{:S(2)}) collective-permute-start(bf16[624,768]{1,0:T(8,128)(2,1)} %dynamic-slice_bitcast_fusion.5), channel_id=1, source_target_pairs={{0,16},{4,20},{8,24},{12,28},{16,0},{20,4},{24,8},{28,12},{1,17},{... | collective-permute-start | bytes 2875400 | tf_op jit(solution)/shard_map/ppermute | solution.py:372
  187.8 20.9 %copy-start.3 = (bf16[2,624,768]{2,1,0:T(8,128)(2,1)S(1)}, bf16[2,624,768]{2,1,0:T(8,128)(2,1)}, u32[]{:S(2)}) copy-start(bf16[2,624,768]{2,1,0:T(8,128)(2,1)} %copy-done.2) | copy-start | bytes 5750788
  210.2 24.0 %copy-start.5 = (f32[8,768]{1,0:T(8,128)S(1)}, f32[8,768]{1,0:T(8,128)}, u32[]{:S(2)}) copy-start(f32[8,768]{1,0:T(8,128)} %get-tuple-element.21) | copy-start | bytes 73732
  210.3 34.6 %copy-start.4 = (bf16[256,768]{1,0:T(8,128)(2,1)S(1)}, bf16[256,768]{1,0:T(8,128)(2,1)}, u32[]{:S(2)}) copy-start(bf16[256,768]{1,0:T(8,128)(2,1)} %get-tuple-element.18) | copy-start | bytes 1179652
  210.3 21.4 %collective-permute-start.16 = (bf16[624,768]{1,0:T(8,128)(2,1)S(1)}, bf16[624,768]{1,0:T(8,128)(2,1)}, u32[]{:S(2)}, u32[]{:S(2)}) collective-permute-start(bf16[624,768]{1,0:T(8,128)(2,1)S(1)} %dynamic-slice_bitcast_fusion.3), channel_id=1, source_target_pairs={{0,1},{1,0},{2,3},{3,2},{4,5},{5,4},{6,7},{7,6},{8,9},{9,8},{10,11... | collective-permute-start | bytes 2875400 | tf_op jit(solution)/shard_map/ppermute | solution.py:372
  233.0 58.2 %collective-permute-start.17 = (bf16[624,768]{1,0:T(8,128)(2,1)S(1)}, bf16[624,768]{1,0:T(8,128)(2,1)S(1)}, u32[]{:S(2)}, u32[]{:S(2)}) collective-permute-start(bf16[624,768]{1,0:T(8,128)(2,1)S(1)} %bitcast_add_fusion.3), channel_id=1, source_target_pairs={{0,2},{1,3},{2,0},{3,1},{4,6},{5,7},{6,4},{7,5},{8,10},{9,11},{10,... | collective-permute-start | bytes 2875400 | tf_op jit(solution)/shard_map/ppermute | solution.py:372
  234.3 1.2 collective-permute-start.19
  235.5 3.8 %collective-permute-start.20 = (f32[8,768]{1,0:T(8,128)S(1)}, f32[8,768]{1,0:T(8,128)S(1)}, u32[]{:S(2)}, u32[]{:S(2)}) collective-permute-start(f32[8,768]{1,0:T(8,128)S(1)} %add.152), channel_id=1, source_target_pairs={{0,8},{4,12},{8,0},{12,4},{16,24},{20,28},{24,16},{28,20},{1,9},{5... | collective-permute-start | bytes 73736 | tf_op jit(solution)/shard_map/ppermute | solution.py:372
  239.3 3.8 %collective-permute-start.21 = (f32[8,768]{1,0:T(8,128)S(1)}, f32[8,768]{1,0:T(8,128)S(1)}, u32[]{:S(2)}, u32[]{:S(2)}) collective-permute-start(f32[8,768]{1,0:T(8,128)S(1)} %add.153), channel_id=1, source_target_pairs={{0,16},{4,20},{8,24},{12,28},{16,0},{20,4},{24,8},{28,12},{1,17},{... | collective-permute-start | bytes 73736 | tf_op jit(solution)/shard_map/ppermute | solution.py:372
  243.1 13.2 %collective-permute-start.22 = (f32[8,768]{1,0:T(8,128)S(1)}, f32[8,768]{1,0:T(8,128)S(1)}, u32[]{:S(2)}, u32[]{:S(2)}) collective-permute-start(f32[8,768]{1,0:T(8,128)S(1)} %add.154), channel_id=1, source_target_pairs={{0,1},{1,0},{2,3},{3,2},{4,5},{5,4},{6,7},{7,6},{8,9},{9,8},{10,11... | collective-permute-start | bytes 73736 | tf_op jit(solution)/shard_map/ppermute | solution.py:372
  245.6 47.8 %collective-permute-start.7 = (bf16[128,768]{1,0:T(8,128)(2,1)}, bf16[128,768]{1,0:T(8,128)(2,1)}, u32[]{:S(2)}, u32[]{:S(2)}) collective-permute-start(bf16[128,768]{1,0:T(8,128)(2,1)} %get-tuple-element.37), channel_id=1, source_target_pairs={{0,3},{1,2},{2,1},{3,0},{4,7},{5,6},{6,5},{7,4},{8,11},{9,10},{10,... | collective-permute-start | bytes 589832 | tf_op jit(solution)/shard_map/ppermute | solution.py:372
  256.4 32.5 %collective-permute-start.23 = (f32[8,768]{1,0:T(8,128)S(1)}, f32[8,768]{1,0:T(8,128)S(1)}, u32[]{:S(2)}, u32[]{:S(2)}) collective-permute-start(f32[8,768]{1,0:T(8,128)S(1)} %add.155), channel_id=1, source_target_pairs={{0,2},{1,3},{2,0},{3,1},{4,6},{5,7},{6,4},{7,5},{8,10},{9,11},{10,... | collective-permute-start | bytes 73736 | tf_op jit(solution)/shard_map/ppermute | solution.py:372
  259.9 35.4 %collective-permute-start.8 = (bf16[128,768]{1,0:T(8,128)(2,1)}, bf16[128,768]{1,0:T(8,128)(2,1)}, u32[]{:S(2)}, u32[]{:S(2)}) collective-permute-start(bf16[128,768]{1,0:T(8,128)(2,1)} %get-tuple-element.33), channel_id=1, source_target_pairs={{0,1},{1,0},{2,3},{3,2},{4,5},{5,4},{6,7},{7,6},{8,9},{9,8},{10,11... | collective-permute-start | bytes 589832 | tf_op jit(solution)/shard_map/ppermute | solution.py:372
  260.7 35.6 %collective-permute-start.10 = (bf16[128,768]{1,0:T(8,128)(2,1)S(1)}, bf16[128,768]{1,0:T(8,128)(2,1)}, u32[]{:S(2)}, u32[]{:S(2)}) collective-permute-start(bf16[128,768]{1,0:T(8,128)(2,1)S(1)} %get-tuple-element.34), channel_id=1, source_target_pairs={{0,2},{1,3},{2,0},{3,1},{4,6},{5,7},{6,4},{7,5},{8,10},{9,11},{10,... | collective-permute-start | bytes 589832 | tf_op jit(solution)/shard_map/ppermute | solution.py:372
  288.8 9.7 %collective-permute-start.9 = (bf16[128,768]{1,0:T(8,128)(2,1)S(1)}, bf16[128,768]{1,0:T(8,128)(2,1)}, u32[]{:S(2)}, u32[]{:S(2)}) collective-permute-start(bf16[128,768]{1,0:T(8,128)(2,1)S(1)} %get-tuple-element.35), channel_id=1, source_target_pairs={{0,3},{1,2},{2,1},{3,0},{4,7},{5,6},{6,5},{7,4},{8,11},{9,10},{10,... | collective-permute-start | bytes 589832 | tf_op jit(solution)/shard_map/ppermute | solution.py:372
  291.5 26.5 %collective-permute-start.18 = (bf16[624,768]{1,0:T(8,128)(2,1)S(1)}, bf16[624,768]{1,0:T(8,128)(2,1)S(1)}, u32[]{:S(2)}, u32[]{:S(2)}) collective-permute-start(bf16[624,768]{1,0:T(8,128)(2,1)S(1)} %add.151), channel_id=1, source_target_pairs={{0,1},{1,0},{2,3},{3,2},{4,5},{5,4},{6,7},{7,6},{8,9},{9,8},{10,11... | collective-permute-start | bytes 2875400 | tf_op jit(solution)/shard_map/ppermute | solution.py:372

commit v2 on v1

v2 whole, which is shorter than its diff:
```python
import functools

import jax
import jax.numpy as jnp
import numpy as np
from jax import lax
from jax.experimental import pallas as pl
from jax.experimental.pallas import tpu as pltpu
from jax.sharding import PartitionSpec as P

HEADS = 12
EPS = 1e-05
BF = jnp.bfloat16
F32 = jnp.float32
PAIRS = HEADS // 2
VMEM_LIMIT = 67043328
QUARTER = 192


def nn(a, b):
    return lax.dot_general(a, b, (((1,), (0,)), ((), ())), preferred_element_type=F32)


def nt(a, b):
    return lax.dot_general(a, b, (((1,), (1,)), ((), ())), preferred_element_type=F32)


def tn(a, b):
    return lax.dot_general(a, b, (((0,), (0,)), ((), ())), preferred_element_type=F32)


def trig_tables(quarter):
    freq = 10000.0 ** (-np.arange(quarter) / quarter)
    tables = []
    for step in (32.0, 1.0):
        angle = step * np.arange(32)[:, None] * freq[None, :]
        rest = np.concatenate([np.sin(angle), np.cos(angle)], axis=1).astype(np.float32)
        parts = []
        for _ in range(3):
            part = rest.astype(BF)
            parts.append(part)
            rest = rest - part.astype(np.float32)
        tables.append(np.concatenate(parts, axis=0))
    return tables


def features(slot, r):
    half = 2 * QUARTER
    iota = lax.broadcasted_iota(jnp.int32, (32, 128), 0)
    hi_tab, lo_tab = r.hi[...], r.lo[...]
    sines, cosines = [], []
    for axis in range(2):
        where = r.bx[slot, axis : axis + 1, :]
        pick_hi = (iota == lax.shift_right_logical(where, 5)).astype(F32).astype(BF)
        pick_lo = (iota == (where & 31)).astype(F32).astype(BF)
        hi = tn(jnp.concatenate([pick_hi] * 3, axis=0), hi_tab)
        lo = tn(jnp.concatenate([pick_lo] * 3, axis=0), lo_tab)
        sin_hi, cos_hi = hi[:, :QUARTER], hi[:, QUARTER:]
        sin_lo, cos_lo = lo[:, :QUARTER], lo[:, QUARTER:]
        sines.append(sin_hi * cos_lo + cos_hi * sin_lo)
        cosines.append(cos_hi * cos_lo - sin_hi * sin_lo)
    sine = jnp.concatenate(sines, axis=1)
    cosine = jnp.concatenate(cosines, axis=1)
    rows = pl.ds(128 * slot, 128)
    r.feat[rows, 0:half] = cosine.astype(BF)
    r.feat[rows, half : 2 * half] = sine.astype(BF)
    if slot < 2:
        r.sine[rows, :] = sine
        r.cosine[rows, :] = cosine


def head_stack(pair):
    first = lax.broadcasted_iota(jnp.int32, pair.shape, 1) < 64
    zero = jnp.zeros_like(pair)
    return jnp.concatenate([jnp.where(first, pair, zero), jnp.where(first, zero, pair)], axis=0)


def head_join(stack):
    half = stack.shape[0] // 2
    first = lax.broadcasted_iota(jnp.int32, (half, 128), 1) < 64
    return jnp.where(first, stack[:half], stack[half:])


def attend_pair(pair, live, r):
    cols = pl.ds(pl.multiple_of(128 * pair, 128), 128)
    stack = head_stack(r.q[:, cols].astype(F32) * 0.125).astype(BF)
    for head in range(2):
        rows = slice(256 * head, 256 * head + 256)
        left = nt(stack[rows], r.wr[0:384, cols])
        right = nt(stack[rows], r.wr[384:768, cols])
        sin, cos = r.sine[...], r.cosine[...]
        r.relq[rows, 0:384] = (left * sin + right * cos).astype(BF)
        r.relq[rows, 384:768] = (right * sin - left * cos).astype(BF)
    r.relq[:, 768:896] = stack
    r.feat[:, 768:896] = r.k[:, cols]
    r.score[...] = nt(r.relq[...], r.feat[...])
    for block in range(8):
        rows = pl.ds(64 * block, 64)
        score = jnp.where(live, r.score[rows, :], -1e30)
        top = jnp.max(score, axis=-1, keepdims=True)
        weight = jnp.exp(score - top)
        total = jnp.sum(weight, axis=-1, keepdims=True)
        r.probs[pair, rows, :] = (weight * (1.0 / total)).astype(BF)
    r.att[:, cols] = head_join(nn(r.probs[pair], r.v[:, cols])).astype(BF)


def attend_pair_back(pair, r):
    cols = pl.ds(pl.multiple_of(128 * pair, 128), 128)
    given = head_stack(r.att[:, cols].astype(F32)).astype(BF)
    stack = head_stack(r.q[:, cols].astype(F32)).astype(BF)
    r.score[...] = nt(given, r.v[:, cols])
    for block in range(8):
        rows = pl.ds(64 * block, 64)
        prob = r.probs[pair, rows, :].astype(F32)
        push = prob * r.score[rows, :]
        mean = jnp.sum(push, axis=-1, keepdims=True)
        r.dlog[rows, :] = ((push - prob * mean) * 0.125).astype(BF)
    r.feat[:, 768:896] = r.k[:, cols]
    r.v[:, cols] = tn(r.probs[pair], given).astype(BF)
    r.k[:, cols] = tn(r.dlog[...], stack).astype(BF)
    for head in range(2):
        rows = slice(256 * head, 256 * head + 256)
        first = nn(r.dlog[rows, :], r.feat[:, 0:384])
        second = nn(r.dlog[rows, :], r.feat[:, 384:768])
        sin, cos = r.sine[...], r.cosine[...]
        r.relq[rows, 0:384] = (first * sin - second * cos).astype(BF)
        r.relq[rows, 384:768] = (first * cos + second * sin).astype(BF)
    dq = nn(r.dlog[...], r.feat[:, 768:896]) + nn(r.relq[:, 0:768], r.wr[:, cols])
    r.q[:, cols] = head_join(dq).astype(BF)
    part = tn(r.relq[:, 0:768], stack).astype(BF)
    for piece, share in enumerate((0, 1, 4, 5, 2, 3, 6, 7)):
        c, y, x = share % 2, share // 4, share // 2 % 2
        r.pool[c, y, x, 96:192, cols] = part[96 * piece : 96 * piece + 96]


def norm_back(given, hat, scale, gain):
    push = given * gain
    mean = jnp.mean(push, axis=-1, keepdims=True)
    lean = jnp.mean(push * hat, axis=-1, keepdims=True)
    return scale * (push - mean - hat * lean)


def put_shares(ref, base, cols, part):
    for share in range(8):
        c, y, x = share % 2, share // 4, share // 2 % 2
        ref[c, y, x, pl.ds(base, 96), cols] = part[96 * share : 96 * share + 96].astype(BF)


class Refs:
    pass


CHUNKS = (("g", 384, 384, 384), ("g", 0, 384, 0), ("pool", 0, 192, 768), ("pool", 192, 288, 960))
STAGES = ("core", "xa", "xb", "ya", "yb", "z1", "z2", "z3")
SENDS = ("x1", "x2", "x3", "b1", "b2", "b3", "cot", "out", "d1", "d2", "d3")
SENDS += tuple("s%d" % i for i in range(5))
SENDS += tuple("%s%d" % (s, u) for u in range(4) for s in STAGES)
LOADS = ("x", "cot", "key", "value", "query", "out")
LOADS += tuple("rel%d" % i for i in range(4)) + tuple("up%d" % i for i in range(4))
LOADS += tuple("down%d" % i for i in range(4))
STORES = ("hid0", "hid1", "din", "share", "small")


class Net:
    def __init__(self, r):
        self.r = r
        self.sent = []

    def start(self, name, src, dst, peer):
        i = SENDS.index(name)
        copy = pltpu.make_async_remote_copy(
            src_ref=src,
            dst_ref=dst,
            send_sem=self.r.send_sem.at[i],
            recv_sem=self.r.recv_sem.at[i],
            device_id=peer,
            device_id_type=pl.DeviceIdType.MESH,
        )
        copy.start()
        self.sent.append((name, src, dst, peer))

    def _of(self, name):
        for key, src, dst, peer in self.sent:
            if key == name:
                i = SENDS.index(name)
                return pltpu.make_async_remote_copy(
                    src_ref=src,
                    dst_ref=dst,
                    send_sem=self.r.send_sem.at[i],
                    recv_sem=self.r.recv_sem.at[i],
                    device_id=peer,
                    device_id_type=pl.DeviceIdType.MESH,
                )
        raise KeyError(name)

    def got(self, name):
        self._of(name).wait_recv()

    def finish(self):
        for name, *_ in self.sent:
            self._of(name).wait_send()


def add_rows(count, body):
    def step(i, carry):
        body(pl.multiple_of(48 * i, 16))
        return carry

    lax.fori_loop(0, count // 48, step, 0)


class Reduction:
    def __init__(self, r, net, dp, z):
        self.r, self.net = r, net
        self.c, self.x, self.y = dp % 2, dp // 2 % 2, dp // 4
        self.low = z % 2
        self.pc = (dp + 1 - 2 * self.c, z)
        self.px = (dp + 2 - 4 * self.x, z)
        self.py = (dp + 4 - 8 * self.y, z)
        self.pz1 = (dp, z + 1 - 2 * self.low)
        self.pz2 = (dp, (z + 2) % 4)

    def parts(self, u):
        name, base, rows, out = CHUNKS[u]
        return getattr(self.r, name), base, rows // 2, out, self.r.r1[u], out // 2

    def core(self, u):
        g, base, half, _, r1, _ = self.parts(u)
        rows = pl.ds(base, 2 * half)
        self.net.start("core%d" % u, g.at[1 - self.c, :, :, rows], r1, self.pc)

    def first(self, u):
        g, base, half, _, r1, at = self.parts(u)
        c, x, y = self.c, self.x, self.y
        self.net.got("core%d" % u)

        def add(i):
            for k in range(2):
                rows, own = pl.ds(base + i, 48), pl.ds(i, 48)
                g[c, k, 1 - x, rows] = (
                    g[c, k, 1 - x, rows].astype(F32) + r1[k, 1 - x, own].astype(F32)
                ).astype(BF)
                rows, own = pl.ds(base + half + i, 48), pl.ds(half + i, 48)
                g[c, 1 - y, k, rows] = (
                    g[c, 1 - y, k, rows].astype(F32) + r1[1 - y, k, own].astype(F32)
                ).astype(BF)

        add_rows(half, add)
        rows = pl.ds(at, half)
        self.net.start(
            "xa%d" % u, g.at[c, :, 1 - x, pl.ds(base, half)], self.r.ra.at[:, rows], self.px
        )
        self.net.start(
            "yb%d" % u, g.at[c, 1 - y, :, pl.ds(base + half, half)], self.r.rb.at[:, rows], self.py
        )

    def second(self, u):
        g, base, half, _, r1, at = self.parts(u)
        c, x, y = self.c, self.x, self.y
        self.net.got("xa%d" % u)
        self.net.got("yb%d" % u)

        def add(i):
            rows, own, came = pl.ds(base + i, 48), pl.ds(i, 48), pl.ds(at + i, 48)
            g[c, 1 - y, x, rows] = (
                g[c, 1 - y, x, rows].astype(F32)
                + r1[1 - y, x, own].astype(F32)
                + self.r.ra[1 - y, came].astype(F32)
            ).astype(BF)
            rows, own = pl.ds(base + half + i, 48), pl.ds(half + i, 48)
            g[c, y, 1 - x, rows] = (
                g[c, y, 1 - x, rows].astype(F32)
                + r1[y, 1 - x, own].astype(F32)
                + self.r.rb[1 - x, came].astype(F32)
            ).astype(BF)

        add_rows(half, add)
        rows = pl.ds(at, half)
        self.net.start(
            "ya%d" % u, g.at[c, 1 - y, x, pl.ds(base, half)], self.r.ra2.at[rows], self.py
        )
        self.net.start(
            "xb%d" % u, g.at[c, y, 1 - x, pl.ds(base + half, half)], self.r.rb2.at[rows], self.px
        )

    def third(self, u):
        g, base, half, _, r1, at = self.parts(u)
        c, x, y = self.c, self.x, self.y
        self.net.got("ya%d" % u)
        self.net.got("xb%d" % u)

        def add(i):
            came = pl.ds(at + i, 48)
            rows, own = pl.ds(base + i, 48), pl.ds(i, 48)
            g[c, y, x, rows] = (
                g[c, y, x, rows].astype(F32)
                + r1[y, x, own].astype(F32)
                + self.r.ra[y, came].astype(F32)
                + self.r.ra2[came].astype(F32)
            ).astype(BF)
            rows, own = pl.ds(base + half + i, 48), pl.ds(half + i, 48)
            g[c, y, x, rows] = (
                g[c, y, x, rows].astype(F32)
                + r1[y, x, own].astype(F32)
                + self.r.rb[x, came].astype(F32)
                + self.r.rb2[came].astype(F32)
            ).astype(BF)

        add_rows(half, add)
        start = pl.multiple_of(base + half * (1 - self.low), 16)
        self.net.start(
            "z1%d" % u, g.at[c, y, x, pl.ds(start, half)], self.r.rz1.at[pl.ds(at, half)], self.pz1
        )

    def fourth(self, u):
        g, base, half, _, _, at = self.parts(u)
        c, x, y = self.c, self.x, self.y
        self.net.got("z1%d" % u)
        start = pl.multiple_of(base + half * self.low, 16)

        def add(i):
            rows = pl.ds(pl.multiple_of(start + i, 16), 48)
            g[c, y, x, rows] = (
                g[c, y, x, rows].astype(F32) + self.r.rz1[pl.ds(at + i, 48)].astype(F32)
            ).astype(BF)

        add_rows(half, add)
        self.net.start(
            "z2%d" % u, g.at[c, y, x, pl.ds(start, half)], self.r.rz2.at[pl.ds(at, half)], self.pz2
        )

    def fifth(self, u):
        g, base, half, out, _, at = self.parts(u)
        c, x, y = self.c, self.x, self.y
        self.net.got("z2%d" % u)
        start = pl.multiple_of(base + half * self.low, 16)
        dest = pl.multiple_of(out + half * self.low, 16)

        def add(i):
            rows = pl.ds(pl.multiple_of(start + i, 16), 48)
            self.r.sums[pl.ds(pl.multiple_of(dest + i, 16), 48)] = (
                g[c, y, x, rows].astype(F32) + self.r.rz2[pl.ds(at + i, 48)].astype(F32)
            ).astype(BF)

        add_rows(half, add)
        rows = pl.ds(dest, half)
        self.net.start("z3%d" % u, self.r.sums.at[rows], self.r.sums.at[rows], self.pz1)

    def small(self, i):
        if i:
            self.net.got("s%d" % (i - 1))
            self.r.sm[i] = self.r.sm[i - 1] + self.r.smr[i - 1]
        if i < 5:
            peer = (self.pc, self.px, self.py, self.pz1, self.pz2)[i]
            self.net.start("s%d" % i, self.r.sm.at[i], self.r.smr.at[i], peer)


def layer_kernel(names, reduce, *refs):
    r = Refs()
    for name, ref in zip(names, refs):
        setattr(r, name, ref)
    r.r1 = (r.r1_0, r.r1_1, r.r1_2, r.r1_3) if reduce else None
    dp, z = lax.axis_index("dp"), lax.axis_index("seq")
    micro = z // 2
    peers = {1: (dp, 3 - z), 2: (dp, z + 1 - 2 * (z % 2)), 3: (dp, (z + 2) % 4)}
    net = Net(r)
    red = Reduction(r, net, dp, z) if reduce else None

    loads = {}

    def load(name, src, dst):
        loads[name] = pltpu.make_async_copy(src, dst, r.load_sem.at[LOADS.index(name)])
        loads[name].start()

    load("x", r.hidden_in.at[micro], r.x.at[0:128])
    load("key", r.w_key, r.wk)
    load("value", r.w_value, r.wv)
    load("query", r.w_query, r.wq)

    greet = list(peers.values()) + ([red.pc, red.px, red.py] if reduce else [])
    barrier = pltpu.get_barrier_semaphore()
    for peer in greet:
        pl.semaphore_signal(barrier, 1, device_id=peer, device_id_type=pl.DeviceIdType.MESH)
    pl.semaphore_wait(barrier, len(greet))
    for slot in (1, 3, 2):
        far = peers[slot][1] // 2
        net.start("b%d" % slot, r.boxes.at[far], r.bx.at[slot], peers[slot])
    for slot in (1, 3, 2):
        far = peers[slot][1] // 2
        rows = pl.ds(128 * slot, 128)
        net.start("x%d" % slot, r.hidden_in.at[far], r.x.at[rows], peers[slot])
    net.start("cot", r.cotangent.at[1 - micro], r.cot.at[128:256], peers[1])

    for i, (dst, src) in enumerate(((0, 0), (192, 384), (384, 192), (576, 576))):
        load("rel%d" % i, r.w_rel.at[src : src + 192], r.wr.at[dst : dst + 192])
    load("out", r.w_out, r.wo)
    for j in range(4):
        load("up%d" % j, r.w_up.at[:, 768 * j : 768 * j + 768], r.pool.at[0, j // 2, j % 2])
    for j in range(4):
        load("down%d" % j, r.w_down.at[768 * j : 768 * j + 768], r.pool.at[1, j // 2, j % 2])
    load("cot", r.cotangent.at[micro], r.cot.at[0:128])

    def project(slot):
        rows = slice(128 * slot, 128 * slot + 128)
        for tile in range(3):
            cols = slice(256 * tile, 256 * tile + 256)
            r.k[rows, cols] = nn(r.x[rows, :], r.wk[:, cols]).astype(BF)
            r.v[rows, cols] = nn(r.x[rows, :], r.wv[:, cols]).astype(BF)
            if slot < 2:
                r.q[rows, cols] = nn(r.x[rows, :], r.wq[:, cols]).astype(BF)

    r.bx[0] = r.boxes[micro]
    features(0, r)
    loads["x"].wait()
    loads["key"].wait()
    loads["value"].wait()
    loads["query"].wait()
    project(0)
    for slot in (1, 2, 3):
        net.got("b%d" % slot)
        features(slot, r)
    for i in range(4):
        loads["rel%d" % i].wait()
    for slot in (2, 1, 3):
        net.got("x%d" % slot)
        project(slot)

    lane = lax.broadcasted_iota(jnp.int32, (1, 128), 1)
    length = r.lengths[micro, 0]
    blocks = (z, peers[1][1], peers[2][1], peers[3][1])
    live = jnp.concatenate([lane + 128 * block < length for block in blocks], axis=1)

    def attend(pair, carry):
        attend_pair(pair, live, r)
        return carry

    lax.fori_loop(0, PAIRS, attend, 0)

    loads["out"].wait()
    for tile in range(3):
        cols = slice(256 * tile, 256 * tile + 256)
        r.res[:, cols] = r.x[0:256, cols].astype(F32) + nn(r.att[...], r.wo[:, cols])

    gain1, bias1, gain2, bias2 = [r.vectors[4 + i : 5 + i, :] for i in range(4)]
    for block in range(4):
        rows = slice(64 * block, 64 * block + 64)
        res = r.res[rows, :]
        center = res - jnp.mean(res, axis=-1, keepdims=True)
        scale = lax.rsqrt(jnp.mean(center * center, axis=-1, keepdims=True) + EPS)
        hat = center * scale
        r.hat[rows, :] = hat
        r.scale[rows, :] = jnp.broadcast_to(scale, (64, 128))
        normed = hat * gain1 + bias1
        r.res[rows, :] = normed
        r.low[rows, :] = normed.astype(BF)

    for j in range(4):
        loads["up%d" % j].wait()
    for j in range(4):
        loads["down%d" % j].wait()

    def up_tile(tile):
        j = tile // 3
        return j // 2, j % 2, pl.ds(pl.multiple_of(256 * (tile % 3), 256), 256)

    def up(tile, carry):
        cols = pl.ds(pl.multiple_of(256 * tile, 256), 256)
        y, x, part = up_tile(tile)
        bias = r.vectors[pl.ds(tile // 3, 1), part]
        value = nn(r.low[...], r.pool[0, y, x, :, part]) + bias
        below = 0.5 * (1.0 + lax.erf(value * np.float32(np.sqrt(0.5))))
        dense = jnp.exp(value * value * -0.5) * np.float32(1.0 / np.sqrt(2.0 * np.pi))
        r.act[:, cols] = (value * below).astype(BF)
        r.slope[:, cols] = below + value * dense
        return carry

    lax.fori_loop(0, 12, up, 0)
    for tile in range(3):
        cols = slice(256 * tile, 256 * tile + 256)
        r.res[:, cols] = r.res[:, cols] + sum(
            nn(r.act[:, 768 * j : 768 * j + 768], r.pool[1, j // 2, j % 2, :, cols])
            for j in range(4)
        )

    loads["cot"].wait()
    net.got("cot")
    sums = [jnp.zeros((1, 768), F32) for _ in range(4)]
    for block in range(4):
        rows = slice(64 * block, 64 * block + 64)
        res = r.res[rows, :]
        center = res - jnp.mean(res, axis=-1, keepdims=True)
        scale = lax.rsqrt(jnp.mean(center * center, axis=-1, keepdims=True) + EPS)
        hat = center * scale
        r.out[rows, :] = (hat * gain2 + bias2).astype(BF)
        given = r.cot[rows, :].astype(F32)
        sums[2] = sums[2] + jnp.sum(given * hat, axis=0, keepdims=True)
        sums[3] = sums[3] + jnp.sum(given, axis=0, keepdims=True)
        dres = norm_back(given, hat, scale, gain2)
        r.res[rows, :] = dres
        r.dlow[rows, :] = dres.astype(BF)

    def grad_down(share, carry):
        cols = pl.ds(pl.multiple_of(384 * share, 128), 384)
        r.g[share % 2, share // 4, share // 2 % 2, 384:768, :] = tn(
            r.act[:, cols], r.dlow[...]
        ).astype(BF)
        return carry

    lax.fori_loop(0, 8, grad_down, 0)
    stores = {}

    def store(name, src, dst):
        stores[name] = pltpu.make_async_copy(src, dst, r.store_sem.at[STORES.index(name)])
        stores[name].start()

    net.start("out", r.out.at[128:256], r.outr, peers[1])
    if reduce:
        red.core(0)

    def up_back(tile, carry):
        cols = pl.ds(pl.multiple_of(256 * tile, 256), 256)
        y, x, part = up_tile(tile)
        push = nt(r.dlow[...], r.pool[1, y, x, part, :]) * r.slope[:, cols]
        low = push.astype(BF)
        r.act[:, cols] = low
        r.sm[0, pl.ds(tile // 3, 1), part] = jnp.sum(low.astype(F32), axis=0, keepdims=True)
        return carry

    lax.fori_loop(0, 12, up_back, 0)

    def grad_up(tile, carry):
        cols = pl.ds(pl.multiple_of(256 * tile, 256), 256)
        _, _, dest = up_tile(tile)
        put_shares(r.g, pl.multiple_of(96 * (tile // 3), 32), dest, tn(r.low[...], r.act[:, cols]))
        return carry

    lax.fori_loop(0, 12, grad_up, 0)
    if reduce:
        red.core(1)
        red.first(0)
    for tile in range(3):
        cols = slice(256 * tile, 256 * tile + 256)
        r.res[:, cols] = r.res[:, cols] + sum(
            nt(r.act[:, 768 * j : 768 * j + 768], r.pool[0, j // 2, j % 2, cols, :])
            for j in range(4)
        )
    for block in range(4):
        rows = slice(64 * block, 64 * block + 64)
        given, hat = r.res[rows, :], r.hat[rows, :]
        sums[0] = sums[0] + jnp.sum(given * hat, axis=0, keepdims=True)
        sums[1] = sums[1] + jnp.sum(given, axis=0, keepdims=True)
        dres = norm_back(given, hat, r.scale[rows, 0:1], gain1)
        r.res[rows, :] = dres
        r.dlow[rows, :] = dres.astype(BF)
    for row in range(4):
        r.sm[0, 4 + row : 5 + row, :] = sums[row]
    if reduce:
        red.first(1)
    for tile in range(3):
        cols = slice(256 * tile, 256 * tile + 256)
        put_shares(r.pool, 0, cols, tn(r.att[...], r.dlow[:, cols]))
    for tile in range(3):
        cols = slice(256 * tile, 256 * tile + 256)
        r.att[:, cols] = nt(r.dlow[...], r.wo[cols, :]).astype(BF)
    if reduce:
        red.small(0)

    def attend_back(pair, carry):
        attend_pair_back(pair, r)
        return carry

    lax.fori_loop(0, 4, attend_back, 0)
    if reduce:
        red.second(0)
        red.small(1)
    lax.fori_loop(4, PAIRS, attend_back, 0)
    if reduce:
        red.core(2)

    for tile in range(3):
        cols = slice(256 * tile, 256 * tile + 256)
        tail = nt(r.k[...], r.wk[cols, :]) + nt(r.v[...], r.wv[cols, :])
        r.relq[256:512, cols] = tail[256:512].astype(BF)
        r.relq[0:256, cols] = (
            tail[0:256] + r.res[:, cols] + nt(r.q[...], r.wq[cols, :])
        ).astype(BF)
    for slot in (1, 3, 2):
        rows = pl.ds(128 * slot, 128)
        net.start("d%d" % slot, r.relq.at[rows, 0:768], r.dxr.at[slot - 1], peers[slot])
    if reduce:
        red.first(2)
        red.second(1)
        red.small(2)
    for tile in range(3):
        cols = slice(256 * tile, 256 * tile + 256)
        put_shares(r.pool, 192, cols, tn(r.x[0:256, :], r.q[:, cols]))
        put_shares(r.pool, 288, cols, tn(r.x[...], r.k[:, cols]))
        put_shares(r.pool, 384, cols, tn(r.x[...], r.v[:, cols]))
    if reduce:
        red.core(3)
        red.third(0)
        red.small(3)
        red.first(3)
    store("hid0", r.out.at[0:128], r.hidden_out.at[micro])
    net.got("out")
    store("hid1", r.outr, r.hidden_out.at[1 - micro])
    if reduce:
        red.second(2)
        red.fourth(0)
        red.third(1)
        red.small(4)
        red.second(3)
        red.fifth(0)
        red.fourth(1)
        red.third(2)
    for slot in (1, 2, 3):
        net.got("d%d" % slot)
    r.din[micro] = (r.relq[0:128, 0:768].astype(F32) + r.dxr[1].astype(F32)).astype(BF)
    r.din[1 - micro] = (r.dxr[0].astype(F32) + r.dxr[2].astype(F32)).astype(BF)
    store("din", r.din, r.input_grad)
    if reduce:
        red.fifth(1)
        red.fourth(2)
        red.third(3)
        red.small(5)
        store("small", r.sm.at[5], r.small)
        red.fifth(2)
        red.fourth(3)
        red.fifth(3)
        for u in range(4):
            net.got("z3%d" % u)
        store("share", r.sums, r.share)
    else:
        store("small", r.sm.at[0], r.small)
        store("share", r.g, r.share.at[0])
        last = pltpu.make_async_copy(r.pool, r.share.at[1], r.load_sem.at[0])
        last.start()
        last.wait()
    for copy in stores.values():
        copy.wait()
    net.finish()


def scratch(reduce):
    shapes = [
        ("x", (512, 768), BF),
        ("bx", (4, 2, 128), jnp.int32),
        ("cot", (256, 768), BF),
        ("wq", (768, 768), BF),
        ("wk", (768, 768), BF),
        ("wv", (768, 768), BF),
        ("wo", (768, 768), BF),
        ("wr", (768, 768), BF),
        ("pool", (2, 2, 2, 768, 768), BF),
        ("g", (2, 2, 2, 768, 768), BF),
        ("sine", (256, 384), F32),
        ("cosine", (256, 384), F32),
        ("feat", (512, 896), BF),
        ("q", (256, 768), BF),
        ("k", (512, 768), BF),
        ("v", (512, 768), BF),
        ("att", (256, 768), BF),
        ("relq", (512, 896), BF),
        ("score", (512, 512), F32),
        ("dlog", (512, 512), BF),
        ("probs", (PAIRS, 512, 512), BF),
        ("res", (256, 768), F32),
        ("hat", (256, 768), F32),
        ("scale", (256, 128), F32),
        ("low", (256, 768), BF),
        ("act", (256, 3072), BF),
        ("slope", (256, 3072), F32),
        ("dlow", (256, 768), BF),
        ("out", (256, 768), BF),
        ("outr", (128, 768), BF),
        ("dxr", (3, 128, 768), BF),
        ("din", (2, 128, 768), BF),
        ("sm", (6, 8, 768), F32),
    ]
    if reduce:
        shapes += [("r1_%d" % u, (2, 2, c[2], 768), BF) for u, c in enumerate(CHUNKS)]
        shapes += [
            ("ra", (2, 624, 768), BF),
            ("rb", (2, 624, 768), BF),
            ("ra2", (624, 768), BF),
            ("rb2", (624, 768), BF),
            ("rz1", (624, 768), BF),
            ("rz2", (624, 768), BF),
            ("sums", (1248, 768), BF),
            ("smr", (5, 8, 768), F32),
        ]
    return shapes


def layer(lengths, hidden_in, boxes, cotangent, vectors, weights, reduce):
    hi, lo = trig_tables(QUARTER)
    any_space = pl.BlockSpec(memory_space=pl.ANY)
    vmem = pl.BlockSpec(memory_space=pltpu.VMEM)
    ins = (
        ("lengths", lengths, pl.BlockSpec(memory_space=pltpu.SMEM)),
        ("hidden_in", hidden_in, any_space),
        ("cotangent", cotangent, any_space),
        ("boxes", boxes, vmem),
        ("vectors", vectors, vmem),
        ("hi", jnp.asarray(hi), vmem),
        ("lo", jnp.asarray(lo), vmem),
    ) + tuple((name, w, any_space) for name, w in weights)
    outs = (
        ("hidden_out", (2, 128, 768), BF),
        ("input_grad", (2, 128, 768), BF),
        ("share", (1248, 768) if reduce else (2, 2, 2, 2, 768, 768), BF),
        ("small", (8, 768), F32),
    )
    shapes = scratch(reduce)
    sems = ("send_sem", "recv_sem", "load_sem", "store_sem")
    names = tuple(i[0] for i in ins) + tuple(o[0] for o in outs)
    names += tuple(s[0] for s in shapes) + sems
    dma = pltpu.SemaphoreType.DMA
    return pl.pallas_call(
        functools.partial(layer_kernel, names, reduce),
        out_shape=[jax.ShapeDtypeStruct(o[1], o[2]) for o in outs],
        in_specs=[i[2] for i in ins],
        out_specs=[any_space] * len(outs),
        scratch_shapes=[pltpu.VMEM(s[1], s[2]) for s in shapes]
        + [dma((len(SENDS),)), dma((len(SENDS),)), dma((len(LOADS),)), dma((len(STORES),))],
        compiler_params=pltpu.CompilerParams(
            vmem_limit_bytes=VMEM_LIMIT, collective_id=0, has_side_effects=True
        ),
        name="layer",
    )(*[i[1] for i in ins])


def finish_kernel(share, small, dq, dk, dv, dout, drel, dup, dbup, ddown, *vectors):
    for j in range(4):
        dup[:, 768 * j : 768 * j + 768] = share[96 * j : 96 * j + 96, :].astype(F32)
    ddown[...] = share[384:768, :].astype(F32)
    for i, ref in enumerate((dout, drel, dq, dk, dv)):
        ref[...] = share[768 + 96 * i : 864 + 96 * i, :].astype(F32)
    dp = lax.axis_index("dp")
    row = small[pl.ds(dp // 2, 1), :]
    dbup[...] = jnp.where(dp % 2 == 0, row[:, 0:384], row[:, 384:768])
    turned = pltpu.roll(small[...], lax.rem(768 - 96 * dp, 768), 1)
    for i, ref in enumerate(vectors):
        ref[...] = turned[4 + i : 5 + i, 0:96]


def finish(share, small):
    shapes = [(96, 768)] * 5 + [(96, 3072), (1, 384), (384, 768)] + [(1, 96)] * 4
    outs = pl.pallas_call(
        finish_kernel,
        out_shape=[jax.ShapeDtypeStruct(s, F32) for s in shapes],
        name="finish",
    )(share, small)
    return [o.reshape(-1) if o.shape[0] == 1 else o for o in outs]


def finish_any(g, small):
    order = g.transpose(0, 2, 3, 1, 4, 5).reshape(2, 8, 768, 768)

    def weight(which, base):
        return order[which, :, base : base + 96].reshape(768, 768)

    up = jnp.concatenate([weight(0, 96 * j) for j in range(4)], axis=1)
    down = order[0, :, 384:768].reshape(3072, 768)
    full = [weight(1, base) for base in (192, 288, 384, 0, 96)] + [up, down]
    grads = [
        lax.psum(lax.psum_scatter(w, "dp", scatter_dimension=0, tiled=True), "seq").astype(F32)
        for w in full
    ]
    small = lax.psum(small, ("dp", "seq"))
    dp, count = lax.axis_index("dp"), lax.axis_size("dp")

    def own_part(vector):
        size = vector.shape[0] // count
        return lax.dynamic_slice_in_dim(vector, dp * size, size)

    parts = [own_part(small[4 + i]) for i in range(4)]
    return grads[:6] + [own_part(small[0:4].reshape(-1)), grads[6]] + parts


def shards(
    hidden_in,
    boxes,
    lengths,
    w_query,
    w_key,
    w_value,
    w_out,
    w_rel,
    w_up,
    b_up,
    w_down,
    gain_attn,
    bias_attn,
    gain_ffn,
    bias_ffn,
    cotangent,
):
    vectors = jnp.concatenate([b_up, gain_attn, bias_attn, gain_ffn, bias_ffn])
    weights = (
        ("w_query", w_query),
        ("w_key", w_key),
        ("w_value", w_value),
        ("w_out", w_out),
        ("w_rel", w_rel),
        ("w_up", w_up),
        ("w_down", w_down),
    )
    reduce = lax.axis_size("dp") == 8
    hidden, dinput, share, small = layer(
        lengths,
        hidden_in[:, 0],
        boxes[:, :, 0].transpose(1, 0, 2),
        cotangent[:, 0],
        vectors.astype(F32).reshape(8, 768),
        weights,
        reduce,
    )
    rest = finish(share, small) if reduce else finish_any(share, small)
    return (hidden[:, None], dinput[:, None], *rest)


def solution(mesh):
    rows = P(None, "dp", "seq", None)
    placed = (rows, P(None, None, "dp", "seq"), P(None, "dp")) + (P(),) * 12 + (rows,)
    matrix, vector = P("dp", None), P("dp")
    return jax.shard_map(
        shards,
        mesh=mesh,
        in_specs=placed,
        out_specs=(rows, rows) + (matrix,) * 6 + (vector, matrix) + (vector,) * 4,
        check_vma=False,
    )
```

time: 322 us -> 181 us (0.56)
  waiting for transfers between devices: 166 us -> 0 us
  Pallas kernels: 60.8 us -> 169 us
  starting transfers between devices: 34.7 us -> 0 us
  other arithmetic: 26.6 us -> 1.28 us
  local copies, waits for them, and re-layouts: 33 us -> 8.78 us
    ppermute x24 -> x0, waiting for transfers between devices: 166 us -> none  [swap(): return lax.ppermute(value, axis, [(i, i ^ bit) for i in range(count)])]
    pallas_call x1 -> x2, Pallas kernels: 60.8 us -> 169 us  [the longest x1 166 us: layer(): pl.pallas_call(functools.partial(layer_kernel, names, reduce), out_shape=...]
    ppermute x24 -> x0, starting transfers between devices: 34.7 us -> none  [swap(): return lax.ppermute(value, axis, [(i, i ^ bit) for i in range(count)])]
    add x12 -> x0, other arithmetic: 16.5 us -> none  [the longest x1 9.25 us: reduce_grads(): mine = (pick(g, core) + got).reshape(2, 2, G_ROWS, 768)]
    squeeze x8 -> x0, local copies, waits for them, and re-layouts: 14.3 us -> none  [pick(): return lax.dynamic_index_in_dim(stacked, index, 0, keepdims=False)]
    slice x6 -> x0, local copies, waits for them, and re-layouts: 8.81 us -> none  [the longest x1 4.76 us: reduce_grads(): a, b = (mine[:, :, :cut], mine[:, :, cut:])]
    unnamed x24 -> x12, local copies, waits for them, and re-layouts: 3.07 us -> 7.3 us
    another operation x4 -> x0, other arithmetic: 3.96 us -> none  [the longest x2 2.14 us: by_micro(): jnp.stack([own, other])]
  transfers between devices with their start and end apart: 24 -> 0, of which waited for: 13 -> 0; matrix products, arithmetic and copies ran while one was open for 8% -> 0% of each run, Pallas kernels for 0% -> 0%
where the time goes in v2:
time: 181 us; the launch traced here: 180 us
  Pallas kernels  169 us (93%)
  local copies, waits for them, and re-layouts  8.78 us (5%)
    pallas_call x1, Pallas kernels, layer(): pl.pallas_call(functools.partial(layer_kernel, names, reduce), out_shape=...  166 us
    unnamed x12, local copies, waits for them, and re-layouts  7.3 us

profile of v2, /device:TPU:0, one launch (start us, length us, event | category | flops | bytes accessed | tf_op | source)
XLA Modules:
  0.0 180.2 jit_solution(363785363341915544)
XLA Ops:
  0.6 1.3 copy.33.refs_0_
  1.9 1.3 copy.37
  3.2 0.7 constant_dynamic-update-slice_fusion
  3.9 0.8 dynamic-update-slice.1
  4.7 0.8 dynamic-update-slice.2
  5.6 0.9 dynamic-update-slice.3
  6.4 0.8 dynamic-update-slice.4
  7.3 0.6 reshape.52.refs_4_
  7.9 165.9 %layer.1 = (bf16[2,128,768]{2,1,0:T(8,128)(2,1)}, bf16[2,128,768]{2,1,0:T(8,128)(2,1)}, bf16[1248,768]{1,0:T(8,128)(2,1)}, f32[8,768]{1,0:T(8,128)}) custom-call(s32[2,1]{1,0:T(2,128)} %copy.33.refs_0_, bf16[2,128,768]{2,1,0:T(8,128)(2,1)} %bitcast.19, bf16[2,128,768]{2,1,0:T(8,128)(2,1)} %bitcast.20, s32[2,2,128]{2,1,0:T(2,128)} %bitcast.21, ...), custom_call_target="tpu_custom_call" | custom-call | tf_op jit(solution)/shard_map/layer/pallas_call | solution.py:719
  173.9 0.0 copy-start.1
  173.9 0.0 copy-start
  173.9 3.5 %finish.1 = (f32[96,768]{1,0:T(8,128)}, f32[96,768]{1,0:T(8,128)}, f32[96,768]{1,0:T(8,128)}, f32[96,768]{1,0:T(8,128)}, f32[96,768]{1,0:T(8,128)}, /*index=5*/f...) custom-call(bf16[1248,768]{1,0:T(8,128)(2,1)} %get-tuple-element.32., ...), custom_call_target="tpu_custom_call" | custom-call | tf_op jit(solution)/shard_map/finish/pallas_call | solution.py:749
  177.4 1.3 reduce
  178.7 0.0 copy-done.1
  178.7 0.7 copy.44
  179.4 0.0 copy-done
  179.4 0.7 copy.45
Async XLA Ops:
  173.9 4.8 %copy-start.1 = (bf16[2,128,768]{2,1,0:T(8,128)(2,1)S(1)}, bf16[2,128,768]{2,1,0:T(8,128)(2,1)}, u32[]{:S(2)}) copy-start(bf16[2,128,768]{2,1,0:T(8,128)(2,1)} %get-tuple-element.30) | copy-start | bytes 1179652
  173.9 5.6 %copy-start = (bf16[2,128,768]{2,1,0:T(8,128)(2,1)S(1)}, bf16[2,128,768]{2,1,0:T(8,128)(2,1)}, u32[]{:S(2)}) copy-start(bf16[2,128,768]{2,1,0:T(8,128)(2,1)} %get-tuple-element.31) | copy-start | bytes 1179652

commit v3 on v2

--- a/solution.py
+++ b/solution.py
@@ -150,11 +150,20 @@
     pass
 
 
-CHUNKS = (("g", 384, 384, 384), ("g", 0, 384, 0), ("pool", 0, 192, 768), ("pool", 192, 288, 960))
+CHUNKS = (
+    ("g", 384, 128, 384),
+    ("g", 512, 256, 512),
+    ("g", 0, 192, 0),
+    ("g", 192, 192, 192),
+    ("pool", 0, 192, 768),
+    ("pool", 192, 96, 960),
+    ("pool", 288, 96, 1056),
+    ("pool", 384, 96, 1152),
+)
 STAGES = ("core", "xa", "xb", "ya", "yb", "z1", "z2", "z3")
-SENDS = ("x1", "x2", "x3", "b1", "b2", "b3", "cot", "out", "d1", "d2", "d3")
+SENDS = tuple("t%d" % i for i in range(1, 8)) + ("b1", "b2", "b3", "cot", "out", "d1", "d2", "d3")
 SENDS += tuple("s%d" % i for i in range(5))
-SENDS += tuple("%s%d" % (s, u) for u in range(4) for s in STAGES)
+SENDS += tuple("%s%d" % (s, u) for u in range(len(CHUNKS)) for s in STAGES)
 LOADS = ("x", "cot", "key", "value", "query", "out")
 LOADS += tuple("rel%d" % i for i in range(4)) + tuple("up%d" % i for i in range(4))
 LOADS += tuple("down%d" % i for i in range(4))
@@ -164,11 +173,13 @@
 class Net:
     def __init__(self, r):
         self.r = r
-        self.sent = []
-
-    def start(self, name, src, dst, peer):
+        self.made = {}
+        self.order = {"all": [], "end": [], "mid": []}
+
+    def _of(self, name):
         i = SENDS.index(name)
-        copy = pltpu.make_async_remote_copy(
+        src, dst, peer = self.made[name]()
+        return pltpu.make_async_remote_copy(
             src_ref=src,
             dst_ref=dst,
             send_sem=self.r.send_sem.at[i],
@@ -176,49 +187,47 @@
             device_id=peer,
             device_id_type=pl.DeviceIdType.MESH,
         )
-        copy.start()
-        self.sent.append((name, src, dst, peer))
-
-    def _of(self, name):
-        for key, src, dst, peer in self.sent:
-            if key == name:
-                i = SENDS.index(name)
-                return pltpu.make_async_remote_copy(
-                    src_ref=src,
-                    dst_ref=dst,
-                    send_sem=self.r.send_sem.at[i],
-                    recv_sem=self.r.recv_sem.at[i],
-                    device_id=peer,
-                    device_id_type=pl.DeviceIdType.MESH,
-                )
-        raise KeyError(name)
+
+    def start(self, name, make, role="all"):
+        self.made[name] = make
+        self._of(name).start()
+        self.order[role].append(name)
 
     def got(self, name):
         self._of(name).wait_recv()
 
-    def finish(self):
-        for name, *_ in self.sent:
+    def finish(self, role):
+        for name in self.order[role]:
             self._of(name).wait_send()
 
 
 def add_rows(count, body):
+    size = 48 if count % 48 == 0 else 32
+
     def step(i, carry):
-        body(pl.multiple_of(48 * i, 16))
+        body(pl.multiple_of(size * i, 16), size)
         return carry
 
-    lax.fori_loop(0, count // 48, step, 0)
+    lax.fori_loop(0, count // size, step, 0)
+
+
+def total(*terms):
+    out = terms[0].astype(F32)
+    for term in terms[1:]:
+        out = out + term.astype(F32)
+    return out.astype(BF)
 
 
 class Reduction:
     def __init__(self, r, net, dp, z):
         self.r, self.net = r, net
         self.c, self.x, self.y = dp % 2, dp // 2 % 2, dp // 4
-        self.low = z % 2
         self.pc = (dp + 1 - 2 * self.c, z)
         self.px = (dp + 2 - 4 * self.x, z)
         self.py = (dp + 4 - 8 * self.y, z)
-        self.pz1 = (dp, z + 1 - 2 * self.low)
+        self.pz1 = (dp, z + 1 - 2 * (z % 2))
         self.pz2 = (dp, (z + 2) % 4)
+        self.across = (dp, 3 - z)
 
     def parts(self, u):
         name, base, rows, out = CHUNKS[u]
@@ -226,125 +235,89 @@
 
     def core(self, u):
         g, base, half, _, r1, _ = self.parts(u)
-        rows = pl.ds(base, 2 * half)
-        self.net.start("core%d" % u, g.at[1 - self.c, :, :, rows], r1, self.pc)
+        self.net.start(
+            "core%d" % u, lambda: (g.at[1 - self.c, :, :, pl.ds(base, 2 * half)], r1, self.pc)
+        )
 
     def first(self, u):
         g, base, half, _, r1, at = self.parts(u)
         c, x, y = self.c, self.x, self.y
         self.net.got("core%d" % u)
 
-        def add(i):
+        def add(i, size):
             for k in range(2):
-                rows, own = pl.ds(base + i, 48), pl.ds(i, 48)
-                g[c, k, 1 - x, rows] = (
-                    g[c, k, 1 - x, rows].astype(F32) + r1[k, 1 - x, own].astype(F32)
-                ).astype(BF)
-                rows, own = pl.ds(base + half + i, 48), pl.ds(half + i, 48)
-                g[c, 1 - y, k, rows] = (
-                    g[c, 1 - y, k, rows].astype(F32) + r1[1 - y, k, own].astype(F32)
-                ).astype(BF)
+                rows, own = pl.ds(base + i, size), pl.ds(i, size)
+                g[c, k, 1 - x, rows] = total(g[c, k, 1 - x, rows], r1[k, 1 - x, own])
+                rows, own = pl.ds(base + half + i, size), pl.ds(half + i, size)
+                g[c, 1 - y, k, rows] = total(g[c, 1 - y, k, rows], r1[1 - y, k, own])
 
         add_rows(half, add)
-        rows = pl.ds(at, half)
-        self.net.start(
-            "xa%d" % u, g.at[c, :, 1 - x, pl.ds(base, half)], self.r.ra.at[:, rows], self.px
-        )
-        self.net.start(
-            "yb%d" % u, g.at[c, 1 - y, :, pl.ds(base + half, half)], self.r.rb.at[:, rows], self.py
-        )
+        a, b, to = pl.ds(base, half), pl.ds(base + half, half), pl.ds(at, half)
+        self.net.start("xa%d" % u, lambda: (g.at[c, :, 1 - x, a], self.r.ra.at[:, to], self.px))
+        self.net.start("yb%d" % u, lambda: (g.at[c, 1 - y, :, b], self.r.rb.at[:, to], self.py))
 
     def second(self, u):
         g, base, half, _, r1, at = self.parts(u)
         c, x, y = self.c, self.x, self.y
+        ra, rb = self.r.ra, self.r.rb
         self.net.got("xa%d" % u)
         self.net.got("yb%d" % u)
 
-        def add(i):
-            rows, own, came = pl.ds(base + i, 48), pl.ds(i, 48), pl.ds(at + i, 48)
-            g[c, 1 - y, x, rows] = (
-                g[c, 1 - y, x, rows].astype(F32)
-                + r1[1 - y, x, own].astype(F32)
-                + self.r.ra[1 - y, came].astype(F32)
-            ).astype(BF)
-            rows, own = pl.ds(base + half + i, 48), pl.ds(half + i, 48)
-            g[c, y, 1 - x, rows] = (
-                g[c, y, 1 - x, rows].astype(F32)
-                + r1[y, 1 - x, own].astype(F32)
-                + self.r.rb[1 - x, came].astype(F32)
-            ).astype(BF)
+        def add(i, size):
+            came = pl.ds(at + i, size)
+            rows, own = pl.ds(base + i, size), pl.ds(i, size)
+            g[c, 1 - y, x, rows] = total(g[c, 1 - y, x, rows], r1[1 - y, x, own], ra[1 - y, came])
+            rows, own = pl.ds(base + half + i, size), pl.ds(half + i, size)
+            g[c, y, 1 - x, rows] = total(g[c, y, 1 - x, rows], r1[y, 1 - x, own], rb[1 - x, came])
 
         add_rows(half, add)
-        rows = pl.ds(at, half)
-        self.net.start(
-            "ya%d" % u, g.at[c, 1 - y, x, pl.ds(base, half)], self.r.ra2.at[rows], self.py
-        )
-        self.net.start(
-            "xb%d" % u, g.at[c, y, 1 - x, pl.ds(base + half, half)], self.r.rb2.at[rows], self.px
-        )
-
-    def third(self, u):
-        g, base, half, _, r1, at = self.parts(u)
+        a, b, to = pl.ds(base, half), pl.ds(base + half, half), pl.ds(at, half)
+        self.net.start("ya%d" % u, lambda: (g.at[c, 1 - y, x, a], self.r.ra2.at[to], self.py))
+        self.net.start("xb%d" % u, lambda: (g.at[c, y, 1 - x, b], self.r.rb2.at[to], self.px))
+
+    def third(self, u, mid):
+        g, base, half, out, r1, at = self.parts(u)
         c, x, y = self.c, self.x, self.y
+        ra, rb, ra2, rb2, zr = self.r.ra, self.r.rb, self.r.ra2, self.r.rb2, self.r.zr
         self.net.got("ya%d" % u)
         self.net.got("xb%d" % u)
-
-        def add(i):
-            came = pl.ds(at + i, 48)
-            rows, own = pl.ds(base + i, 48), pl.ds(i, 48)
-            g[c, y, x, rows] = (
-                g[c, y, x, rows].astype(F32)
-                + r1[y, x, own].astype(F32)
-                + self.r.ra[y, came].astype(F32)
-                + self.r.ra2[came].astype(F32)
-            ).astype(BF)
-            rows, own = pl.ds(base + half + i, 48), pl.ds(half + i, 48)
-            g[c, y, x, rows] = (
-                g[c, y, x, rows].astype(F32)
-                + r1[y, x, own].astype(F32)
-                + self.r.rb[x, came].astype(F32)
-                + self.r.rb2[came].astype(F32)
-            ).astype(BF)
+        if mid:
+            self.net.got("z1%d" % u)
+
+        def add(i, size):
+            came = pl.ds(at + i, size)
+            rows, own = pl.ds(base + i, size), pl.ds(i, size)
+            more = (zr[pl.ds(out + i, size)],) if mid else ()
+            g[c, y, x, rows] = total(
+                g[c, y, x, rows], r1[y, x, own], ra[y, came], ra2[came], *more
+            )
+            rows, own = pl.ds(base + half + i, size), pl.ds(half + i, size)
+            more = (zr[pl.ds(out + half + i, size)],) if mid else ()
+            g[c, y, x, rows] = total(
+                g[c, y, x, rows], r1[y, x, own], rb[x, came], rb2[came], *more
+            )
 
         add_rows(half, add)
-        start = pl.multiple_of(base + half * (1 - self.low), 16)
-        self.net.start(
-            "z1%d" % u, g.at[c, y, x, pl.ds(start, half)], self.r.rz1.at[pl.ds(at, half)], self.pz1
-        )
+        rows, to = pl.ds(base, 2 * half), pl.ds(out, 2 * half)
+        if mid:
+            make = lambda: (g.at[c, y, x, rows], self.r.za.at[to], self.across)
+            self.net.start("z2%d" % u, make, "mid")
+        else:
+            make = lambda: (g.at[c, y, x, rows], self.r.zr.at[to], self.pz1)
+            self.net.start("z1%d" % u, make, "end")
 
     def fourth(self, u):
-        g, base, half, _, _, at = self.parts(u)
-        c, x, y = self.c, self.x, self.y
-        self.net.got("z1%d" % u)
-        start = pl.multiple_of(base + half * self.low, 16)
-
-        def add(i):
-            rows = pl.ds(pl.multiple_of(start + i, 16), 48)
-            g[c, y, x, rows] = (
-                g[c, y, x, rows].astype(F32) + self.r.rz1[pl.ds(at + i, 48)].astype(F32)
-            ).astype(BF)
-
-        add_rows(half, add)
-        self.net.start(
-            "z2%d" % u, g.at[c, y, x, pl.ds(start, half)], self.r.rz2.at[pl.ds(at, half)], self.pz2
-        )
-
-    def fifth(self, u):
-        g, base, half, out, _, at = self.parts(u)
+        g, base, half, out, _, _ = self.parts(u)
         c, x, y = self.c, self.x, self.y
         self.net.got("z2%d" % u)
-        start = pl.multiple_of(base + half * self.low, 16)
-        dest = pl.multiple_of(out + half * self.low, 16)
-
-        def add(i):
-            rows = pl.ds(pl.multiple_of(start + i, 16), 48)
-            self.r.sums[pl.ds(pl.multiple_of(dest + i, 16), 48)] = (
-                g[c, y, x, rows].astype(F32) + self.r.rz2[pl.ds(at + i, 48)].astype(F32)
-            ).astype(BF)
-
-        add_rows(half, add)
-        rows = pl.ds(dest, half)
-        self.net.start("z3%d" % u, self.r.sums.at[rows], self.r.sums.at[rows], self.pz1)
+
+        def add(i, size):
+            rows, to = pl.ds(base + i, size), pl.ds(out + i, size)
+            self.r.sums[to] = total(g[c, y, x, rows], self.r.za[to])
+
+        add_rows(2 * half, add)
+        to = pl.ds(out, 2 * half)
+        self.net.start("z3%d" % u, lambda: (self.r.sums.at[to], self.r.sums.at[to], self.pz1), "mid")
 
     def small(self, i):
         if i:
@@ -352,19 +325,47 @@
             self.r.sm[i] = self.r.sm[i - 1] + self.r.smr[i - 1]
         if i < 5:
             peer = (self.pc, self.px, self.py, self.pz1, self.pz2)[i]
-            self.net.start("s%d" % i, self.r.sm.at[i], self.r.smr.at[i], peer)
+            self.net.start("s%d" % i, lambda: (self.r.sm.at[i], self.r.smr.at[i], peer))
 
 
 def layer_kernel(names, reduce, *refs):
     r = Refs()
     for name, ref in zip(names, refs):
         setattr(r, name, ref)
-    r.r1 = (r.r1_0, r.r1_1, r.r1_2, r.r1_3) if reduce else None
     dp, z = lax.axis_index("dp"), lax.axis_index("seq")
     micro = z // 2
+    is_mid = lax.rem(z, 3) > 0
+    is_end = lax.rem(z, 3) == 0
     peers = {1: (dp, 3 - z), 2: (dp, z + 1 - 2 * (z % 2)), 3: (dp, (z + 2) % 4)}
     net = Net(r)
-    red = Reduction(r, net, dp, z) if reduce else None
+    red = None
+    if reduce:
+        r.r1 = tuple(getattr(r, "r1_%d" % u) for u in range(len(CHUNKS)))
+        red = Reduction(r, net, dp, z)
+
+    def run(*steps):
+        if not reduce:
+            return
+        for step in steps:
+            kind, u = step[0], int(step[1:])
+            if kind == "C":
+                red.core(u)
+            elif kind == "F":
+                red.first(u)
+            elif kind == "S":
+                red.second(u)
+            elif kind == "T":
+                pl.when(is_end)(lambda: red.third(u, False))
+            elif kind == "M":
+                pl.when(is_mid)(lambda: red.third(u, True))
+            elif kind == "N":
+                pl.when(is_mid)(lambda: red.fourth(u))
+            elif kind == "s":
+                red.small(u)
+
+    def run_at(index, plan):
+        for at, steps in plan.items():
+            pl.when(index == at)(functools.partial(run, *steps))
 
     loads = {}
 
@@ -382,15 +383,26 @@
     for peer in greet:
         pl.semaphore_signal(barrier, 1, device_id=peer, device_id_type=pl.DeviceIdType.MESH)
     pl.semaphore_wait(barrier, len(greet))
+
+    def slot_rows(slot):
+        return r.x.at[128 * slot : 128 * slot + 128]
+
+    @pl.when(is_end)
+    def _():
+        net.start("t1", lambda: (r.hidden_in.at[1 - micro], r.relay, peers[2]), "end")
+        net.start("t2", lambda: (r.hidden_in.at[micro], slot_rows(2), peers[2]), "end")
+
+    @pl.when(is_mid)
+    def _():
+        net.start("t4", lambda: (r.hidden_in.at[1 - micro], slot_rows(1), peers[1]), "mid")
+        net.start("t3", lambda: (r.hidden_in.at[micro], slot_rows(2), peers[2]), "mid")
+
     for slot in (1, 3, 2):
         far = peers[slot][1] // 2
-        net.start("b%d" % slot, r.boxes.at[far], r.bx.at[slot], peers[slot])
-    for slot in (1, 3, 2):
-        far = peers[slot][1] // 2
-        rows = pl.ds(128 * slot, 128)
-        net.start("x%d" % slot, r.hidden_in.at[far], r.x.at[rows], peers[slot])
-    net.start("cot", r.cotangent.at[1 - micro], r.cot.at[128:256], peers[1])
-
+        net.start(
+            "b%d" % slot,
+            lambda slot=slot, far=far: (r.boxes.at[:, far], r.bx.at[slot], peers[slot]),
+        )
     for i, (dst, src) in enumerate(((0, 0), (192, 384), (384, 192), (576, 576))):
         load("rel%d" % i, r.w_rel.at[src : src + 192], r.wr.at[dst : dst + 192])
     load("out", r.w_out, r.wo)
@@ -409,24 +421,50 @@
             if slot < 2:
                 r.q[rows, cols] = nn(r.x[rows, :], r.wq[:, cols]).astype(BF)
 
-    r.bx[0] = r.boxes[micro]
+    for j in range(4):
+        r.vectors[j : j + 1, :] = r.vector0[768 * j : 768 * j + 768].astype(F32).reshape(1, 768)
+        row = getattr(r, "vector%d" % (j + 1))[...]
+        r.vectors[4 + j : 5 + j, :] = row.astype(F32).reshape(1, 768)
+    for axis in range(2):
+        r.bx[0, axis : axis + 1, :] = r.boxes[axis, pl.ds(micro, 1), :]
     features(0, r)
     loads["x"].wait()
     loads["key"].wait()
     loads["value"].wait()
     loads["query"].wait()
     project(0)
+
+    @pl.when(is_mid)
+    def _():
+        net.made["t1"] = lambda: (r.hidden_in.at[1 - micro], r.relay, peers[2])
+        net.got("t1")
+        net.start("t5", lambda: (r.relay, slot_rows(3), peers[1]), "mid")
+        net.got("t4")
+        net.start("t6", lambda: (slot_rows(1), slot_rows(3), peers[2]), "mid")
+
     for slot in (1, 2, 3):
         net.got("b%d" % slot)
         features(slot, r)
     for i in range(4):
         loads["rel%d" % i].wait()
-    for slot in (2, 1, 3):
-        net.got("x%d" % slot)
-        project(slot)
+
+    pl.when(is_mid)(lambda: net.got("t2"))
+    pl.when(is_end)(lambda: net.got("t3"))
+    project(2)
+
+    @pl.when(is_mid)
+    def _():
+        net.got("t5")
+        net.start("t7", lambda: (slot_rows(3), slot_rows(1), peers[2]), "mid")
+
+    pl.when(is_end)(lambda: net.got("t6"))
+    project(3)
+    pl.when(is_end)(lambda: net.got("t7"))
+    net.start("cot", lambda: (r.cotangent.at[1 - micro], r.cot.at[128:256], peers[1]))
+    project(1)
 
     lane = lax.broadcasted_iota(jnp.int32, (1, 128), 1)
-    length = r.lengths[micro, 0]
+    length = r.lengths[micro]
     blocks = (z, peers[1][1], peers[2][1], peers[3][1])
     live = jnp.concatenate([lane + 128 * block < length for block in blocks], axis=1)
 
@@ -471,7 +509,10 @@
         below = 0.5 * (1.0 + lax.erf(value * np.float32(np.sqrt(0.5))))
         dense = jnp.exp(value * value * -0.5) * np.float32(1.0 / np.sqrt(2.0 * np.pi))
         r.act[:, cols] = (value * below).astype(BF)
-        r.slope[:, cols] = below + value * dense
+        slope = below + value * dense
+        top = slope.astype(BF)
+        r.g[0, y, x, 0:256, part] = top
+        r.g[1, y, x, 0:256, part] = (slope - top.astype(F32)).astype(BF)
         return carry
 
     lax.fori_loop(0, 12, up, 0)
@@ -499,31 +540,34 @@
         r.res[rows, :] = dres
         r.dlow[rows, :] = dres.astype(BF)
 
-    def grad_down(share, carry):
-        cols = pl.ds(pl.multiple_of(384 * share, 128), 384)
-        r.g[share % 2, share // 4, share // 2 % 2, 384:768, :] = tn(
+    def grad_down(offset, size, share, carry):
+        cols = pl.ds(pl.multiple_of(384 * share + offset, 128), size)
+        r.g[share % 2, share // 4, share // 2 % 2, 384 + offset : 384 + offset + size, :] = tn(
             r.act[:, cols], r.dlow[...]
         ).astype(BF)
         return carry
 
-    lax.fori_loop(0, 8, grad_down, 0)
+    lax.fori_loop(0, 8, functools.partial(grad_down, 0, 128), 0)
+    run("C0")
+    lax.fori_loop(0, 8, functools.partial(grad_down, 128, 256), 0)
+    run("C1")
     stores = {}
 
     def store(name, src, dst):
         stores[name] = pltpu.make_async_copy(src, dst, r.store_sem.at[STORES.index(name)])
         stores[name].start()
 
-    net.start("out", r.out.at[128:256], r.outr, peers[1])
-    if reduce:
-        red.core(0)
+    net.start("out", lambda: (r.out.at[128:256], r.outr, peers[1]))
 
     def up_back(tile, carry):
         cols = pl.ds(pl.multiple_of(256 * tile, 256), 256)
         y, x, part = up_tile(tile)
-        push = nt(r.dlow[...], r.pool[1, y, x, part, :]) * r.slope[:, cols]
+        slope = r.g[0, y, x, 0:256, part].astype(F32) + r.g[1, y, x, 0:256, part].astype(F32)
+        push = nt(r.dlow[...], r.pool[1, y, x, part, :]) * slope
         low = push.astype(BF)
         r.act[:, cols] = low
         r.sm[0, pl.ds(tile // 3, 1), part] = jnp.sum(low.astype(F32), axis=0, keepdims=True)
+        run_at(tile, PLAN["up_back"])
         return carry
 
     lax.fori_loop(0, 12, up_back, 0)
@@ -532,12 +576,10 @@
         cols = pl.ds(pl.multiple_of(256 * tile, 256), 256)
         _, _, dest = up_tile(tile)
         put_shares(r.g, pl.multiple_of(96 * (tile // 3), 32), dest, tn(r.low[...], r.act[:, cols]))
+        run_at(tile, PLAN["grad_up"])
         return carry
 
     lax.fori_loop(0, 12, grad_up, 0)
-    if reduce:
-        red.core(1)
-        red.first(0)
     for tile in range(3):
         cols = slice(256 * tile, 256 * tile + 256)
         r.res[:, cols] = r.res[:, cols] + sum(
@@ -554,28 +596,33 @@
         r.dlow[rows, :] = dres.astype(BF)
     for row in range(4):
         r.sm[0, 4 + row : 5 + row, :] = sums[row]
-    if reduce:
-        red.first(1)
+    run(*PLAN["norm"])
     for tile in range(3):
         cols = slice(256 * tile, 256 * tile + 256)
         put_shares(r.pool, 0, cols, tn(r.att[...], r.dlow[:, cols]))
     for tile in range(3):
         cols = slice(256 * tile, 256 * tile + 256)
         r.att[:, cols] = nt(r.dlow[...], r.wo[cols, :]).astype(BF)
-    if reduce:
-        red.small(0)
 
     def attend_back(pair, carry):
         attend_pair_back(pair, r)
+        run_at(pair, PLAN["pairs"])
         return carry
 
-    lax.fori_loop(0, 4, attend_back, 0)
-    if reduce:
-        red.second(0)
-        red.small(1)
-    lax.fori_loop(4, PAIRS, attend_back, 0)
-    if reduce:
-        red.core(2)
+    lax.fori_loop(0, PAIRS, attend_back, 0)
+    run("C4")
+    for tile in range(3):
+        cols = slice(256 * tile, 256 * tile + 256)
+        put_shares(r.pool, 192, cols, tn(r.x[0:256, :], r.q[:, cols]))
+    run("C5", *PLAN["query"])
+    for tile in range(3):
+        cols = slice(256 * tile, 256 * tile + 256)
+        put_shares(r.pool, 288, cols, tn(r.x[...], r.k[:, cols]))
+    run("C6", *PLAN["key"])
+    for tile in range(3):
+        cols = slice(256 * tile, 256 * tile + 256)
+        put_shares(r.pool, 384, cols, tn(r.x[...], r.v[:, cols]))
+    run("C7", *PLAN["value"])
 
     for tile in range(3):
         cols = slice(256 * tile, 256 * tile + 256)
@@ -585,50 +632,34 @@
             tail[0:256] + r.res[:, cols] + nt(r.q[...], r.wq[cols, :])
         ).astype(BF)
     for slot in (1, 3, 2):
-        rows = pl.ds(128 * slot, 128)
-        net.start("d%d" % slot, r.relq.at[rows, 0:768], r.dxr.at[slot - 1], peers[slot])
-    if reduce:
-        red.first(2)
-        red.second(1)
-        red.small(2)
-    for tile in range(3):
-        cols = slice(256 * tile, 256 * tile + 256)
-        put_shares(r.pool, 192, cols, tn(r.x[0:256, :], r.q[:, cols]))
-        put_shares(r.pool, 288, cols, tn(r.x[...], r.k[:, cols]))
-        put_shares(r.pool, 384, cols, tn(r.x[...], r.v[:, cols]))
-    if reduce:
-        red.core(3)
-        red.third(0)
-        red.small(3)
-        red.first(3)
+        rows = slice(128 * slot, 128 * slot + 128)
+        net.start(
+            "d%d" % slot,
+            lambda slot=slot, rows=rows: (
+                r.relq.at[rows, 0:768],
+                r.dxr.at[slot - 1],
+                peers[slot],
+            ),
+        )
+    run(*PLAN["input"])
     store("hid0", r.out.at[0:128], r.hidden_out.at[micro])
     net.got("out")
     store("hid1", r.outr, r.hidden_out.at[1 - micro])
-    if reduce:
-        red.second(2)
-        red.fourth(0)
-        red.third(1)
-        red.small(4)
-        red.second(3)
-        red.fifth(0)
-        red.fourth(1)
-        red.third(2)
+    run(*PLAN["tail"])
     for slot in (1, 2, 3):
         net.got("d%d" % slot)
     r.din[micro] = (r.relq[0:128, 0:768].astype(F32) + r.dxr[1].astype(F32)).astype(BF)
     r.din[1 - micro] = (r.dxr[0].astype(F32) + r.dxr[2].astype(F32)).astype(BF)
     store("din", r.din, r.input_grad)
+    run(*PLAN["last"])
     if reduce:
-        red.fifth(1)
-        red.fourth(2)
-        red.third(3)
-        red.small(5)
         store("small", r.sm.at[5], r.small)
-        red.fifth(2)
-        red.fourth(3)
-        red.fifth(3)
-        for u in range(4):
-            net.got("z3%d" % u)
+
+        @pl.when(is_end)
+        def _():
+            for u in range(len(CHUNKS)):
+                net.got("z3%d" % u)
+
         store("share", r.sums, r.share)
     else:
         store("small", r.sm.at[0], r.small)
@@ -638,14 +669,33 @@
         last.wait()
     for copy in stores.values():
         copy.wait()
-    net.finish()
+    net.finish("all")
+    pl.when(is_end)(lambda: net.finish("end"))
+    pl.when(is_mid)(lambda: net.finish("mid"))
+
+
+PLAN = {
+    "up_back": {4: ("F0",), 9: ("F1",)},
+    "grad_up": {5: ("C2",), 11: ("C3",)},
+    "norm": ("S0", "F2", "s0"),
+    "pairs": {2: ("S1", "F3", "s1"), 3: ("T0",), 5: ("s2",)},
+    "query": ("S2", "F4"),
+    "key": ("M0", "T1"),
+    "value": ("F5",),
+    "input": ("s3",),
+    "tail": ("M1", "T2", "S3", "N0", "F6", "M2", "N1", "S4", "F7", "s4", "T3", "N2", "S5", "M3"),
+    "last": ("T4", "S6", "N3", "M4", "T5", "s5", "S7", "N4", "M5", "T6", "N5", "M6", "T7")
+    + ("N6", "M7", "N7"),
+}
 
 
 def scratch(reduce):
     shapes = [
         ("x", (512, 768), BF),
+        ("relay", (128, 768), BF),
         ("bx", (4, 2, 128), jnp.int32),
         ("cot", (256, 768), BF),
+        ("vectors", (8, 768), F32),
         ("wq", (768, 768), BF),
         ("wk", (768, 768), BF),
         ("wv", (768, 768), BF),
@@ -669,7 +719,6 @@
         ("scale", (256, 128), F32),
         ("low", (256, 768), BF),
         ("act", (256, 3072), BF),
-        ("slope", (256, 3072), F32),
         ("dlow", (256, 768), BF),
         ("out", (256, 768), BF),
         ("outr", (128, 768), BF),
@@ -684,8 +733,8 @@
             ("rb", (2, 624, 768), BF),
             ("ra2", (624, 768), BF),
             ("rb2", (624, 768), BF),
-            ("rz1", (624, 768), BF),
-            ("rz2", (624, 768), BF),
+            ("zr", (1248, 768), BF),
+            ("za", (1248, 768), BF),
             ("sums", (1248, 768), BF),
             ("smr", (5, 8, 768), F32),
         ]
@@ -697,14 +746,15 @@
     any_space = pl.BlockSpec(memory_space=pl.ANY)
     vmem = pl.BlockSpec(memory_space=pltpu.VMEM)
     ins = (
-        ("lengths", lengths, pl.BlockSpec(memory_space=pltpu.SMEM)),
+        ("lengths", lengths.reshape(-1), pl.BlockSpec(memory_space=pltpu.SMEM)),
         ("hidden_in", hidden_in, any_space),
         ("cotangent", cotangent, any_space),
         ("boxes", boxes, vmem),
-        ("vectors", vectors, vmem),
         ("hi", jnp.asarray(hi), vmem),
         ("lo", jnp.asarray(lo), vmem),
-    ) + tuple((name, w, any_space) for name, w in weights)
+    )
+    ins += tuple(("vector%d" % i, v, vmem) for i, v in enumerate(vectors))
+    ins += tuple((name, w, any_space) for name, w in weights)
     outs = (
         ("hidden_out", (2, 128, 768), BF),
         ("input_grad", (2, 128, 768), BF),
@@ -730,7 +780,10 @@
     )(*[i[1] for i in ins])
 
 
-def finish_kernel(share, small, dq, dk, dv, dout, drel, dup, dbup, ddown, *vectors):
+def finish_kernel(share, small, hid, din, hidden, dinput, dq, dk, dv, dout, drel, dup, *rest):
+    dbup, ddown, vectors = rest[0], rest[1], rest[2:]
+    hidden[...] = hid[...]
+    dinput[...] = din[...]
     for j in range(4):
         dup[:, 768 * j : 768 * j + 768] = share[96 * j : 96 * j + 96, :].astype(F32)
     ddown[...] = share[384:768, :].astype(F32)
@@ -738,20 +791,20 @@
         ref[...] = share[768 + 96 * i : 864 + 96 * i, :].astype(F32)
     dp = lax.axis_index("dp")
     row = small[pl.ds(dp // 2, 1), :]
-    dbup[...] = jnp.where(dp % 2 == 0, row[:, 0:384], row[:, 384:768])
+    dbup[...] = jnp.where(dp % 2 == 0, row[:, 0:384], row[:, 384:768]).reshape(384)
     turned = pltpu.roll(small[...], lax.rem(768 - 96 * dp, 768), 1)
     for i, ref in enumerate(vectors):
-        ref[...] = turned[4 + i : 5 + i, 0:96]
-
-
-def finish(share, small):
-    shapes = [(96, 768)] * 5 + [(96, 3072), (1, 384), (384, 768)] + [(1, 96)] * 4
-    outs = pl.pallas_call(
+        ref[...] = turned[4 + i : 5 + i, 0:96].reshape(96)
+
+
+def finish(share, small, hidden, dinput):
+    shapes = [(96, 768)] * 5 + [(96, 3072), (384,), (384, 768)] + [(96,)] * 4
+    low = jax.ShapeDtypeStruct(hidden.shape, BF)
+    return pl.pallas_call(
         finish_kernel,
-        out_shape=[jax.ShapeDtypeStruct(s, F32) for s in shapes],
+        out_shape=[low, low] + [jax.ShapeDtypeStruct(s, F32) for s in shapes],
         name="finish",
-    )(share, small)
-    return [o.reshape(-1) if o.shape[0] == 1 else o for o in outs]
+    )(share, small, hidden, dinput)
 
 
 def finish_any(g, small):
@@ -796,7 +849,7 @@
     bias_ffn,
     cotangent,
 ):
-    vectors = jnp.concatenate([b_up, gain_attn, bias_attn, gain_ffn, bias_ffn])
+    vectors = (b_up, gain_attn, bias_attn, gain_ffn, bias_ffn)
     weights = (
         ("w_query", w_query),
         ("w_key", w_key),
@@ -810,13 +863,16 @@
     hidden, dinput, share, small = layer(
         lengths,
         hidden_in[:, 0],
-        boxes[:, :, 0].transpose(1, 0, 2),
+        boxes[:, :, 0],
         cotangent[:, 0],
-        vectors.astype(F32).reshape(8, 768),
+        vectors,
         weights,
         reduce,
     )
-    rest = finish(share, small) if reduce else finish_any(share, small)
+    if reduce:
+        hidden, dinput, *rest = finish(share, small, hidden, dinput)
+    else:
+        rest = finish_any(share, small)
     return (hidden[:, None], dinput[:, None], *rest)
 
 

time: 181 us -> 166 us (0.917)
  local copies, waits for them, and re-layouts: 8.78 us -> 0 us
  Pallas kernels: 169 us -> 165 us
    unnamed x12 -> x0, local copies, waits for them, and re-layouts: 7.3 us -> none
    pallas_call x1, Pallas kernels: 166 us -> 161 us  [layer(): pl.pallas_call(functools.partial(layer_kernel, names, reduce), out_shape=...]
where the time goes in v3:
time: 166 us; the launch traced here: 165 us
  Pallas kernels  165 us (99%)
    pallas_call x1, Pallas kernels, layer(): pl.pallas_call(functools.partial(layer_kernel, names, reduce), out_shape=...  161 us
    pallas_call x1, Pallas kernels, finish(): pl.pallas_call(finish_kernel, out_shape=[low, low] + [jax.ShapeDtypeStruc...  3.9 us

profile of v3, /device:TPU:0, one launch (start us, length us, event | category | flops | bytes accessed | tf_op | source)
XLA Modules:
  0.0 165.5 jit_solution(9860970513157171377)
XLA Ops:
  0.7 160.7 %layer.1 = (bf16[2,128,768]{2,1,0:T(8,128)(2,1)}, bf16[2,128,768]{2,1,0:T(8,128)(2,1)}, bf16[1248,768]{1,0:T(8,128)(2,1)}, f32[8,768]{1,0:T(8,128)}) custom-call(s32[2]{0:T(128)} %bitcast.13, bf16[2,128,768]{2,1,0:T(8,128)(2,1)} %bitcast.10, bf16[2,128,768]{2,1,0:T(8,128)(2,1)} %bitcast.11, s32[2,2,128]{2,1,0:T(2,128)} %bitcast.12, ...), custom_call_target="tpu_custom_call" | custom-call | tf_op jit(solution)/shard_map/layer/pallas_call | solution.py:769
  161.4 3.9 %finish.1 = (bf16[2,128,768]{2,1,0:T(8,128)(2,1)}, bf16[2,128,768]{2,1,0:T(8,128)(2,1)}, f32[96,768]{1,0:T(8,128)}, f32[96,768]{1,0:T(8,128)}, f32[96,768]{1,0:T...) custom-call(bf16[1248,768]{1,0:T(8,128)(2,1)} %get-tuple-element.32., ...), custom_call_target="tpu_custom_call" | custom-call | tf_op jit(solution)/shard_map/finish/pallas_call | solution.py:803

commit v4 on v3

--- a/solution.py
+++ b/solution.py
@@ -44,13 +44,14 @@
     return tables
 
 
-def features(slot, r):
+def features(slot, c, micro, r):
     half = 2 * QUARTER
     iota = lax.broadcasted_iota(jnp.int32, (32, 128), 0)
     hi_tab, lo_tab = r.hi[...], r.lo[...]
+    block = pltpu.roll(r.meta[slot], 64 * c, 1)
     sines, cosines = [], []
     for axis in range(2):
-        where = r.bx[slot, axis : axis + 1, :]
+        where = jnp.where(micro == 0, block[axis : axis + 1], block[2 + axis : 3 + axis])
         pick_hi = (iota == lax.shift_right_logical(where, 5)).astype(F32).astype(BF)
         pick_lo = (iota == (where & 31)).astype(F32).astype(BF)
         hi = tn(jnp.concatenate([pick_hi] * 3, axis=0), hi_tab)
@@ -61,12 +62,14 @@
         cosines.append(cos_hi * cos_lo - sin_hi * sin_lo)
     sine = jnp.concatenate(sines, axis=1)
     cosine = jnp.concatenate(cosines, axis=1)
-    rows = pl.ds(128 * slot, 128)
-    r.feat[rows, 0:half] = cosine.astype(BF)
-    r.feat[rows, half : 2 * half] = sine.astype(BF)
-    if slot < 2:
-        r.sine[rows, :] = sine
-        r.cosine[rows, :] = cosine
+    for part in range(2):
+        mine = slice(64 * part, 64 * part + 64)
+        rows = pl.ds(256 * part + 64 * slot, 64)
+        r.feat[rows, 0:half] = cosine[mine].astype(BF)
+        r.feat[rows, half : 2 * half] = sine[mine].astype(BF)
+    rows = pl.ds(64 * slot, 64)
+    r.sine[rows, :] = sine[0:64]
+    r.cosine[rows, :] = cosine[0:64]
 
 
 def head_stack(pair):
@@ -161,13 +164,16 @@
     ("pool", 384, 96, 1152),
 )
 STAGES = ("core", "xa", "xb", "ya", "yb", "z1", "z2", "z3")
-SENDS = tuple("t%d" % i for i in range(1, 8)) + ("b1", "b2", "b3", "cot", "out", "d1", "d2", "d3")
+BLOCKS = ("x", "m", "c", "f", "o", "d")
+SENDS = tuple(k + str(i) for k in BLOCKS for i in range(4)) + ("dx0",)
 SENDS += tuple("s%d" % i for i in range(5))
 SENDS += tuple("%s%d" % (s, u) for u in range(len(CHUNKS)) for s in STAGES)
-LOADS = ("x", "cot", "key", "value", "query", "out")
+LOADS = ("x", "x2", "cot", "key", "value", "query", "out")
 LOADS += tuple("rel%d" % i for i in range(4)) + tuple("up%d" % i for i in range(4))
 LOADS += tuple("down%d" % i for i in range(4))
-STORES = ("hid0", "hid1", "din", "share", "small")
+STORES = ("hid", "din", "share", "small")
+POSTS = tuple(k + i for k in "xmc" for i in ("a0", "a1", "b0", "b1", "p"))
+POSTS += tuple(k + str(i) for k in "fod" for i in range(4)) + ("dx",)
 
 
 class Net:
@@ -175,6 +181,7 @@
         self.r = r
         self.made = {}
         self.order = {"all": [], "end": [], "mid": []}
+        self.posts = {"all": [], "own": [], "far": []}
 
     def _of(self, name):
         i = SENDS.index(name)
@@ -196,9 +203,33 @@
     def got(self, name):
         self._of(name).wait_recv()
 
+    def _post(self, name, src, dst, at, peer):
+        return pltpu.make_async_remote_copy(
+            src_ref=src,
+            dst_ref=dst,
+            send_sem=self.r.post_sem.at[POSTS.index(name)],
+            recv_sem=self.r.recv_sem.at[at],
+            device_id=peer,
+            device_id_type=pl.DeviceIdType.MESH,
+        )
+
+    def post(self, name, kind, index, make, role="all"):
+        src, dst, peer = make()
+        self._post(name, src, dst, SENDS.index(kind + "0") + index, peer).start()
+        self.posts[role].append((name, kind, index, make))
+
+    def came(self, kind, index, make):
+        src, dst, peer = make()
+        self._post(POSTS[0], src, dst, SENDS.index(kind + "0") + index, peer).wait_recv()
+
     def finish(self, role):
         for name in self.order[role]:
             self._of(name).wait_send()
+
+    def posted(self, role):
+        for name, kind, index, make in self.posts[role]:
+            src, dst, peer = make()
+            self._post(name, src, dst, SENDS.index(kind + "0") + index, peer).wait_send()
 
 
 def add_rows(count, body):
@@ -333,10 +364,17 @@
     for name, ref in zip(names, refs):
         setattr(r, name, ref)
     dp, z = lax.axis_index("dp"), lax.axis_index("seq")
-    micro = z // 2
+    micro, c = z // 2, dp % 2
     is_mid = lax.rem(z, 3) > 0
     is_end = lax.rem(z, 3) == 0
-    peers = {1: (dp, 3 - z), 2: (dp, z + 1 - 2 * (z % 2)), 3: (dp, (z + 2) % 4)}
+    own = c == z % 2
+    far = c != z % 2
+    base = jnp.where(own, 0, 1)
+    column = dp - c
+    source = column + z % 2
+    pair = (dp + 1 - 2 * c, z)
+    half = pl.ds(pl.multiple_of(64 * c, 64), 64)
+    other = pl.ds(pl.multiple_of(64 - 64 * c, 64), 64)
     net = Net(r)
     red = None
     if reduce:
@@ -370,103 +408,132 @@
     loads = {}
 
     def load(name, src, dst):
-        loads[name] = pltpu.make_async_copy(src, dst, r.load_sem.at[LOADS.index(name)])
-        loads[name].start()
-
-    load("x", r.hidden_in.at[micro], r.x.at[0:128])
-    load("key", r.w_key, r.wk)
-    load("value", r.w_value, r.wv)
-    load("query", r.w_query, r.wq)
-
-    greet = list(peers.values()) + ([red.pc, red.px, red.py] if reduce else [])
+        loads[name] = lambda: (src(), dst(), r.load_sem.at[LOADS.index(name)])
+        pltpu.make_async_copy(*loads[name]()).start()
+
+    def loaded(name):
+        pltpu.make_async_copy(*loads[name]()).wait()
+
+    load("key", lambda: r.w_key, lambda: r.wk)
+    load("value", lambda: r.w_value, lambda: r.wv)
+    load("query", lambda: r.w_query, lambda: r.wq)
+
+    greet = [pair] + [(column + h, (z + i) % 4) for i in range(1, 4) for h in range(2)]
+    greet += [red.px, red.py] if reduce else []
+    line = lax.broadcasted_iota(jnp.int32, (8, 128), 0)
+    wide = [r.boxes[axis, m : m + 1, :] for m in range(2) for axis in range(2)]
+    wide = jnp.concatenate(wide * 2, axis=0)
+    wide = jnp.where(line == 4, r.lengths[0], jnp.where(line == 5, r.lengths[1], wide))
+    r.facts[...] = wide
     barrier = pltpu.get_barrier_semaphore()
     for peer in greet:
         pl.semaphore_signal(barrier, 1, device_id=peer, device_id_type=pl.DeviceIdType.MESH)
     pl.semaphore_wait(barrier, len(greet))
 
-    def slot_rows(slot):
-        return r.x.at[128 * slot : 128 * slot + 128]
-
-    @pl.when(is_end)
+    def spread(kind, src, dst):
+        for first in (False, True):
+            step = base if first else base + 2
+            to = (z + 4 - step) % 4
+            rows = pl.ds(pl.multiple_of(64 * step, 64), 64)
+            for h in range(2):
+                def make(h=h, to=to, rows=rows, step=step):
+                    return src(to // 2, pl.ds(64 * h, 64)), dst(step, rows), (column + h, to)
+
+                name = kind + ("a" if first else "b") + str(h)
+                if first:
+                    pl.when(far)(functools.partial(net.post, name, kind, step, make, "far"))
+                else:
+                    net.post(name, kind, step, make)
+
+    def here(kind, src, dst):
+        make = lambda: (src(micro, other), dst(0, pl.ds(0, 64)), pair)
+        net.post(kind + "p", kind, 0, make, "own")
+
+    hidden = lambda m, rows: r.hidden_in.at[m, rows]
+    grads = lambda m, rows: r.cotangent.at[m, rows]
+
+    x_to = lambda step, rows: r.x.at[rows]
+    m_to = lambda step, rows: r.meta.at[step]
+    c_to = lambda step, rows: r.cot.at[rows]
+    spread("m", lambda m, rows: r.facts, m_to)
+    spread("x", hidden, x_to)
+
+    @pl.when(own)
     def _():
-        net.start("t1", lambda: (r.hidden_in.at[1 - micro], r.relay, peers[2]), "end")
-        net.start("t2", lambda: (r.hidden_in.at[micro], slot_rows(2), peers[2]), "end")
-
-    @pl.when(is_mid)
-    def _():
-        net.start("t4", lambda: (r.hidden_in.at[1 - micro], slot_rows(1), peers[1]), "mid")
-        net.start("t3", lambda: (r.hidden_in.at[micro], slot_rows(2), peers[2]), "mid")
-
-    for slot in (1, 3, 2):
-        far = peers[slot][1] // 2
-        net.start(
-            "b%d" % slot,
-            lambda slot=slot, far=far: (r.boxes.at[:, far], r.bx.at[slot], peers[slot]),
-        )
+        here("m", lambda m, rows: r.facts, m_to)
+        here("x", hidden, x_to)
+        make = lambda: (hidden(micro, half), r.x.at[256:320], pair)
+        net.post("f0", "f", 0, make, "own")
+        load("x", lambda: hidden(micro, half), lambda: r.x.at[0:64])
+        load("x2", lambda: hidden(micro, other), lambda: r.x.at[256:320])
+        r.meta[0] = r.facts[...]
+
     for i, (dst, src) in enumerate(((0, 0), (192, 384), (384, 192), (576, 576))):
-        load("rel%d" % i, r.w_rel.at[src : src + 192], r.wr.at[dst : dst + 192])
-    load("out", r.w_out, r.wo)
+        load("rel%d" % i, lambda src=src, dst=dst: r.w_rel.at[src : src + 192], lambda src=src, dst=dst: r.wr.at[dst : dst + 192])
+    load("out", lambda: r.w_out, lambda: r.wo)
     for j in range(4):
-        load("up%d" % j, r.w_up.at[:, 768 * j : 768 * j + 768], r.pool.at[0, j // 2, j % 2])
+        load("up%d" % j, lambda j=j: r.w_up.at[:, 768 * j : 768 * j + 768], lambda j=j: r.pool.at[0, j // 2, j % 2])
     for j in range(4):
-        load("down%d" % j, r.w_down.at[768 * j : 768 * j + 768], r.pool.at[1, j // 2, j % 2])
-    load("cot", r.cotangent.at[micro], r.cot.at[0:128])
-
-    def project(slot):
-        rows = slice(128 * slot, 128 * slot + 128)
+        load("down%d" % j, lambda j=j: r.w_down.at[768 * j : 768 * j + 768], lambda j=j: r.pool.at[1, j // 2, j % 2])
+    pl.when(own)(lambda: load("cot", lambda: grads(micro, half), lambda: r.cot.at[0:64]))
+
+    def project(start, stop):
+        rows = slice(start, stop)
         for tile in range(3):
             cols = slice(256 * tile, 256 * tile + 256)
             r.k[rows, cols] = nn(r.x[rows, :], r.wk[:, cols]).astype(BF)
             r.v[rows, cols] = nn(r.x[rows, :], r.wv[:, cols]).astype(BF)
-            if slot < 2:
+            if stop <= 256:
                 r.q[rows, cols] = nn(r.x[rows, :], r.wq[:, cols]).astype(BF)
 
     for j in range(4):
         r.vectors[j : j + 1, :] = r.vector0[768 * j : 768 * j + 768].astype(F32).reshape(1, 768)
         row = getattr(r, "vector%d" % (j + 1))[...]
         r.vectors[4 + j : 5 + j, :] = row.astype(F32).reshape(1, 768)
-    for axis in range(2):
-        r.bx[0, axis : axis + 1, :] = r.boxes[axis, pl.ds(micro, 1), :]
-    features(0, r)
-    loads["x"].wait()
-    loads["key"].wait()
-    loads["value"].wait()
-    loads["query"].wait()
-    project(0)
-
-    @pl.when(is_mid)
+    x_size = lambda: (hidden(0, pl.ds(0, 64)), r.x.at[0:64], pair)
+    m_size = lambda: (r.facts, r.meta.at[0], pair)
+    pl.when(far)(lambda: net.came("m", 0, m_size))
+    features(0, c, micro, r)
+    for slot in (1, 3, 2):
+        net.came("m", slot, m_size)
+        features(slot, c, micro, r)
+    loaded("key")
+    loaded("value")
+    loaded("query")
+
+    @pl.when(own)
     def _():
-        net.made["t1"] = lambda: (r.hidden_in.at[1 - micro], r.relay, peers[2])
-        net.got("t1")
-        net.start("t5", lambda: (r.relay, slot_rows(3), peers[1]), "mid")
-        net.got("t4")
-        net.start("t6", lambda: (slot_rows(1), slot_rows(3), peers[2]), "mid")
-
-    for slot in (1, 2, 3):
-        net.got("b%d" % slot)
-        features(slot, r)
+        loaded("x")
+        loaded("x2")
+
+    @pl.when(far)
+    def _():
+        net.came("x", 0, x_size)
+        net.came("f", 0, x_size)
+
+    project(0, 64)
+    project(256, 320)
     for i in range(4):
-        loads["rel%d" % i].wait()
-
-    pl.when(is_mid)(lambda: net.got("t2"))
-    pl.when(is_end)(lambda: net.got("t3"))
-    project(2)
-
-    @pl.when(is_mid)
-    def _():
-        net.got("t5")
-        net.start("t7", lambda: (slot_rows(3), slot_rows(1), peers[2]), "mid")
-
-    pl.when(is_end)(lambda: net.got("t6"))
-    project(3)
-    pl.when(is_end)(lambda: net.got("t7"))
-    net.start("cot", lambda: (r.cotangent.at[1 - micro], r.cot.at[128:256], peers[1]))
-    project(1)
-
-    lane = lax.broadcasted_iota(jnp.int32, (1, 128), 1)
-    length = r.lengths[micro]
-    blocks = (z, peers[1][1], peers[2][1], peers[3][1])
-    live = jnp.concatenate([lane + 128 * block < length for block in blocks], axis=1)
+        loaded("rel%d" % i)
+    for slot in (1, 3, 2):
+        net.came("x", slot, x_size)
+        mine, theirs = slice(64 * slot, 64 * slot + 64), slice(256 + 64 * slot, 320 + 64 * slot)
+        make = lambda mine=mine, theirs=theirs: (r.x.at[mine], r.x.at[theirs], pair)
+        net.post("f%d" % slot, "f", slot, make)
+    spread("c", grads, c_to)
+    pl.when(own)(lambda: here("c", grads, c_to))
+    project(64, 256)
+    for slot in (1, 3, 2):
+        net.came("f", slot, x_size)
+    project(320, 512)
+
+    place = lax.broadcasted_iota(jnp.int32, (1, 512), 1)
+    turn = lax.shift_right_logical(place, 8)
+    token = 128 * ((z + (lax.shift_right_logical(place, 6) & 3)) & 3) + (place & 63)
+    token = token + 64 * ((c + turn) & 1)
+    known = r.meta[1]
+    length = jnp.where(micro == 0, known[4:5], known[5:6])
+    live = token < jnp.concatenate([length] * 4, axis=1)
 
     def attend(pair, carry):
         attend_pair(pair, live, r)
@@ -474,7 +541,7 @@
 
     lax.fori_loop(0, PAIRS, attend, 0)
 
-    loads["out"].wait()
+    loaded("out")
     for tile in range(3):
         cols = slice(256 * tile, 256 * tile + 256)
         r.res[:, cols] = r.x[0:256, cols].astype(F32) + nn(r.att[...], r.wo[:, cols])
@@ -493,9 +560,9 @@
         r.low[rows, :] = normed.astype(BF)
 
     for j in range(4):
-        loads["up%d" % j].wait()
+        loaded("up%d" % j)
     for j in range(4):
-        loads["down%d" % j].wait()
+        loaded("down%d" % j)
 
     def up_tile(tile):
         j = tile // 3
@@ -523,8 +590,11 @@
             for j in range(4)
         )
 
-    loads["cot"].wait()
-    net.got("cot")
+    c_size = lambda: (grads(0, pl.ds(0, 64)), r.cot.at[0:64], pair)
+    pl.when(own)(lambda: loaded("cot"))
+    pl.when(far)(lambda: net.came("c", 0, c_size))
+    for slot in (1, 2, 3):
+        net.came("c", slot, c_size)
     sums = [jnp.zeros((1, 768), F32) for _ in range(4)]
     for block in range(4):
         rows = slice(64 * block, 64 * block + 64)
@@ -554,10 +624,33 @@
     stores = {}
 
     def store(name, src, dst):
-        stores[name] = pltpu.make_async_copy(src, dst, r.store_sem.at[STORES.index(name)])
-        stores[name].start()
-
-    net.start("out", lambda: (r.out.at[128:256], r.outr, peers[1]))
+        stores[name] = lambda: (src(), dst(), r.store_sem.at[STORES.index(name)])
+        pltpu.make_async_copy(*stores[name]()).start()
+
+    def stored(name):
+        pltpu.make_async_copy(*stores[name]()).wait()
+
+    def give_back(kind, src, dst):
+        for slot in (3, 1, 2, 0):
+            rows = slice(64 * slot, 64 * slot + 64)
+            to = (source, (z + slot) % 4)
+            make = lambda rows=rows, to=to: (src.at[rows], dst.at[micro, half], to)
+            role = "all" if slot else "far"
+            post = functools.partial(net.post, kind + str(slot), kind, 2 * micro + c, make, role)
+            if slot:
+                post()
+            else:
+                pl.when(far)(post)
+
+    def given_back(kind, dst):
+        size = lambda: (r.out.at[0:64], dst.at[0, 0:64], pair)
+        for m in range(2):
+            for h in range(2):
+                local = own & (micro == m) & (c == h)
+                pl.when(jnp.logical_not(local))(functools.partial(net.came, kind, 2 * m + h, size))
+
+    give_back("o", r.out, r.hidden_out)
+    pl.when(own)(lambda: store("hid", lambda: r.out.at[0:64], lambda: r.hidden_out.at[micro, half]))
 
     def up_back(tile, carry):
         cols = pl.ds(pl.multiple_of(256 * tile, 256), 256)
@@ -631,44 +724,42 @@
         r.relq[0:256, cols] = (
             tail[0:256] + r.res[:, cols] + nt(r.q[...], r.wq[cols, :])
         ).astype(BF)
-    for slot in (1, 3, 2):
-        rows = slice(128 * slot, 128 * slot + 128)
-        net.start(
-            "d%d" % slot,
-            lambda slot=slot, rows=rows: (
-                r.relq.at[rows, 0:768],
-                r.dxr.at[slot - 1],
-                peers[slot],
-            ),
-        )
+    net.post("dx", "dx", 0, lambda: (r.relq.at[256:512, 0:768], r.dxr, pair))
     run(*PLAN["input"])
-    store("hid0", r.out.at[0:128], r.hidden_out.at[micro])
-    net.got("out")
-    store("hid1", r.outr, r.hidden_out.at[1 - micro])
+    net.came("dx", 0, lambda: (r.relq.at[256:512, 0:768], r.dxr, pair))
+    r.din[...] = (r.relq[0:256, 0:768].astype(F32) + r.dxr[...].astype(F32)).astype(BF)
+    give_back("d", r.din, r.input_grad)
+    pl.when(own)(lambda: store("din", lambda: r.din.at[0:64], lambda: r.input_grad.at[micro, half]))
     run(*PLAN["tail"])
-    for slot in (1, 2, 3):
-        net.got("d%d" % slot)
-    r.din[micro] = (r.relq[0:128, 0:768].astype(F32) + r.dxr[1].astype(F32)).astype(BF)
-    r.din[1 - micro] = (r.dxr[0].astype(F32) + r.dxr[2].astype(F32)).astype(BF)
-    store("din", r.din, r.input_grad)
     run(*PLAN["last"])
     if reduce:
-        store("small", r.sm.at[5], r.small)
+        store("small", lambda: r.sm.at[5], lambda: r.small)
 
         @pl.when(is_end)
         def _():
             for u in range(len(CHUNKS)):
                 net.got("z3%d" % u)
 
-        store("share", r.sums, r.share)
+        store("share", lambda: r.sums, lambda: r.share)
     else:
-        store("small", r.sm.at[0], r.small)
-        store("share", r.g, r.share.at[0])
+        store("small", lambda: r.sm.at[0], lambda: r.small)
+        store("share", lambda: r.g, lambda: r.share.at[0])
         last = pltpu.make_async_copy(r.pool, r.share.at[1], r.load_sem.at[0])
         last.start()
         last.wait()
-    for copy in stores.values():
-        copy.wait()
+    given_back("o", r.hidden_out)
+    given_back("d", r.input_grad)
+    stored("small")
+    stored("share")
+
+    @pl.when(own)
+    def _():
+        stored("hid")
+        stored("din")
+        net.posted("own")
+
+    pl.when(far)(lambda: net.posted("far"))
+    net.posted("all")
     net.finish("all")
     pl.when(is_end)(lambda: net.finish("end"))
     pl.when(is_mid)(lambda: net.finish("mid"))
@@ -692,8 +783,8 @@
 def scratch(reduce):
     shapes = [
         ("x", (512, 768), BF),
-        ("relay", (128, 768), BF),
-        ("bx", (4, 2, 128), jnp.int32),
+        ("facts", (8, 128), jnp.int32),
+        ("meta", (4, 8, 128), jnp.int32),
         ("cot", (256, 768), BF),
         ("vectors", (8, 768), F32),
         ("wq", (768, 768), BF),
@@ -721,9 +812,8 @@
         ("act", (256, 3072), BF),
         ("dlow", (256, 768), BF),
         ("out", (256, 768), BF),
-        ("outr", (128, 768), BF),
-        ("dxr", (3, 128, 768), BF),
-        ("din", (2, 128, 768), BF),
+        ("dxr", (256, 768), BF),
+        ("din", (256, 768), BF),
         ("sm", (6, 8, 768), F32),
     ]
     if reduce:
@@ -762,7 +852,7 @@
         ("small", (8, 768), F32),
     )
     shapes = scratch(reduce)
-    sems = ("send_sem", "recv_sem", "load_sem", "store_sem")
+    sems = ("send_sem", "recv_sem", "post_sem", "load_sem", "store_sem")
     names = tuple(i[0] for i in ins) + tuple(o[0] for o in outs)
     names += tuple(s[0] for s in shapes) + sems
     dma = pltpu.SemaphoreType.DMA
@@ -772,7 +862,7 @@
         in_specs=[i[2] for i in ins],
         out_specs=[any_space] * len(outs),
         scratch_shapes=[pltpu.VMEM(s[1], s[2]) for s in shapes]
-        + [dma((len(SENDS),)), dma((len(SENDS),)), dma((len(LOADS),)), dma((len(STORES),))],
+        + [dma((len(i),)) for i in (SENDS, SENDS, POSTS, LOADS, STORES)],
         compiler_params=pltpu.CompilerParams(
             vmem_limit_bytes=VMEM_LIMIT, collective_id=0, has_side_effects=True
         ),

time: 166 us -> 157 us (0.946)
  Pallas kernels: 165 us -> 156 us
    pallas_call x1, Pallas kernels: 161 us -> 152 us  [layer(): pl.pallas_call(functools.partial(layer_kernel, names, reduce), out_shape=...]
where the time goes in v4:
time: 157 us
  Pallas kernels  156 us (99%)
    pallas_call x1, Pallas kernels, layer(): pl.pallas_call(functools.partial(layer_kernel, names, reduce), out_shape=...  152 us
    pallas_call x1, Pallas kernels, finish(): pl.pallas_call(finish_kernel, out_shape=[low, low] + [jax.ShapeDtypeStruc...  3.9 us

profile of v4, /device:TPU:0, one launch (start us, length us, event | category | flops | bytes accessed | tf_op | source)
XLA Modules:
  0.0 156.7 jit_solution(12661026609890668854)
XLA Ops:
  0.7 152.0 %layer.1 = (bf16[2,128,768]{2,1,0:T(8,128)(2,1)}, bf16[2,128,768]{2,1,0:T(8,128)(2,1)}, bf16[1248,768]{1,0:T(8,128)(2,1)}, f32[8,768]{1,0:T(8,128)}) custom-call(s32[2]{0:T(128)} %bitcast.13, bf16[2,128,768]{2,1,0:T(8,128)(2,1)} %bitcast.10, bf16[2,128,768]{2,1,0:T(8,128)(2,1)} %bitcast.11, s32[2,2,128]{2,1,0:T(2,128)} %bitcast.12, ...), custom_call_target="tpu_custom_call" | custom-call | tf_op jit(solution)/shard_map/layer/pallas_call | solution.py:859
  152.7 3.9 %finish.1 = (bf16[2,128,768]{2,1,0:T(8,128)(2,1)}, bf16[2,128,768]{2,1,0:T(8,128)(2,1)}, f32[96,768]{1,0:T(8,128)}, f32[96,768]{1,0:T(8,128)}, f32[96,768]{1,0:T...) custom-call(bf16[1248,768]{1,0:T(8,128)(2,1)} %get-tuple-element.32., ...), custom_call_target="tpu_custom_call" | custom-call | tf_op jit(solution)/shard_map/finish/pallas_call | solution.py:893

commit v5 on v4

--- a/solution.py
+++ b/solution.py
@@ -155,14 +155,20 @@
 
 CHUNKS = (
     ("g", 384, 128, 384),
-    ("g", 512, 256, 512),
-    ("g", 0, 192, 0),
-    ("g", 192, 192, 192),
-    ("pool", 0, 192, 768),
+    ("g", 512, 128, 512),
+    ("g", 640, 128, 640),
+    ("g", 0, 96, 0),
+    ("g", 96, 96, 96),
+    ("g", 192, 96, 192),
+    ("g", 288, 96, 288),
+    ("pool", 0, 96, 768),
+    ("pool", 96, 96, 864),
     ("pool", 192, 96, 960),
     ("pool", 288, 96, 1056),
-    ("pool", 384, 96, 1152),
+    ("pool", 384, 64, 1152),
+    ("pool", 448, 32, 1216),
 )
+C, F, S, T, M, N, V = range(7)
 STAGES = ("core", "xa", "xb", "ya", "yb", "z1", "z2", "z3")
 BLOCKS = ("x", "m", "c", "f", "o", "d")
 SENDS = tuple(k + str(i) for k in BLOCKS for i in range(4)) + ("dx0",)
@@ -233,7 +239,7 @@
 
 
 def add_rows(count, body):
-    size = 48 if count % 48 == 0 else 32
+    size = 48 if count % 48 == 0 else 32 if count % 32 == 0 else 16
 
     def step(i, carry):
         body(pl.multiple_of(size * i, 16), size)
@@ -384,25 +390,27 @@
     def run(*steps):
         if not reduce:
             return
-        for step in steps:
-            kind, u = step[0], int(step[1:])
-            if kind == "C":
+        for kind, u in steps:
+            if kind == C:
                 red.core(u)
-            elif kind == "F":
+            elif kind == F:
                 red.first(u)
-            elif kind == "S":
+            elif kind == S:
                 red.second(u)
-            elif kind == "T":
-                pl.when(is_end)(lambda: red.third(u, False))
-            elif kind == "M":
-                pl.when(is_mid)(lambda: red.third(u, True))
-            elif kind == "N":
-                pl.when(is_mid)(lambda: red.fourth(u))
-            elif kind == "s":
+            elif kind == T:
+                pl.when(is_end)(functools.partial(red.third, u, False))
+            elif kind == M:
+                pl.when(is_mid)(functools.partial(red.third, u, True))
+            elif kind == N:
+                pl.when(is_mid)(functools.partial(red.fourth, u))
+            else:
                 red.small(u)
 
-    def run_at(index, plan):
-        for at, steps in plan.items():
+    def run_plan(place):
+        run(*PLAN.get(place, ()))
+
+    def run_at(index, place):
+        for at, steps in PLAN[place].items():
             pl.when(index == at)(functools.partial(run, *steps))
 
     loads = {}
@@ -617,10 +625,9 @@
         ).astype(BF)
         return carry
 
-    lax.fori_loop(0, 8, functools.partial(grad_down, 0, 128), 0)
-    run("C0")
-    lax.fori_loop(0, 8, functools.partial(grad_down, 128, 256), 0)
-    run("C1")
+    for third in range(3):
+        lax.fori_loop(0, 8, functools.partial(grad_down, 128 * third, 128), 0)
+        run_plan("down%d" % third)
     stores = {}
 
     def store(name, src, dst):
@@ -660,7 +667,7 @@
         low = push.astype(BF)
         r.act[:, cols] = low
         r.sm[0, pl.ds(tile // 3, 1), part] = jnp.sum(low.astype(F32), axis=0, keepdims=True)
-        run_at(tile, PLAN["up_back"])
+        run_at(tile, "up_back")
         return carry
 
     lax.fori_loop(0, 12, up_back, 0)
@@ -669,7 +676,7 @@
         cols = pl.ds(pl.multiple_of(256 * tile, 256), 256)
         _, _, dest = up_tile(tile)
         put_shares(r.g, pl.multiple_of(96 * (tile // 3), 32), dest, tn(r.low[...], r.act[:, cols]))
-        run_at(tile, PLAN["grad_up"])
+        run_at(tile, "grad_up")
         return carry
 
     lax.fori_loop(0, 12, grad_up, 0)
@@ -689,33 +696,34 @@
         r.dlow[rows, :] = dres.astype(BF)
     for row in range(4):
         r.sm[0, 4 + row : 5 + row, :] = sums[row]
-    run(*PLAN["norm"])
+    run_plan("norm")
     for tile in range(3):
         cols = slice(256 * tile, 256 * tile + 256)
         put_shares(r.pool, 0, cols, tn(r.att[...], r.dlow[:, cols]))
+    run_plan("out")
     for tile in range(3):
         cols = slice(256 * tile, 256 * tile + 256)
         r.att[:, cols] = nt(r.dlow[...], r.wo[cols, :]).astype(BF)
+    run_plan("datt")
 
     def attend_back(pair, carry):
         attend_pair_back(pair, r)
-        run_at(pair, PLAN["pairs"])
+        run_at(pair, "pairs")
         return carry
 
     lax.fori_loop(0, PAIRS, attend_back, 0)
-    run("C4")
     for tile in range(3):
         cols = slice(256 * tile, 256 * tile + 256)
         put_shares(r.pool, 192, cols, tn(r.x[0:256, :], r.q[:, cols]))
-    run("C5", *PLAN["query"])
+    run_plan("query")
     for tile in range(3):
         cols = slice(256 * tile, 256 * tile + 256)
         put_shares(r.pool, 288, cols, tn(r.x[...], r.k[:, cols]))
-    run("C6", *PLAN["key"])
+    run_plan("key")
     for tile in range(3):
         cols = slice(256 * tile, 256 * tile + 256)
         put_shares(r.pool, 384, cols, tn(r.x[...], r.v[:, cols]))
-    run("C7", *PLAN["value"])
+    run_plan("value")
 
     for tile in range(3):
         cols = slice(256 * tile, 256 * tile + 256)
@@ -725,13 +733,13 @@
             tail[0:256] + r.res[:, cols] + nt(r.q[...], r.wq[cols, :])
         ).astype(BF)
     net.post("dx", "dx", 0, lambda: (r.relq.at[256:512, 0:768], r.dxr, pair))
-    run(*PLAN["input"])
+    run_plan("input")
     net.came("dx", 0, lambda: (r.relq.at[256:512, 0:768], r.dxr, pair))
     r.din[...] = (r.relq[0:256, 0:768].astype(F32) + r.dxr[...].astype(F32)).astype(BF)
     give_back("d", r.din, r.input_grad)
     pl.when(own)(lambda: store("din", lambda: r.din.at[0:64], lambda: r.input_grad.at[micro, half]))
-    run(*PLAN["tail"])
-    run(*PLAN["last"])
+    run_plan("dxdone")
+    run_plan("tail")
     if reduce:
         store("small", lambda: r.sm.at[5], lambda: r.small)
 
@@ -766,17 +774,44 @@
 
 
 PLAN = {
-    "up_back": {4: ("F0",), 9: ("F1",)},
-    "grad_up": {5: ("C2",), 11: ("C3",)},
-    "norm": ("S0", "F2", "s0"),
-    "pairs": {2: ("S1", "F3", "s1"), 3: ("T0",), 5: ("s2",)},
-    "query": ("S2", "F4"),
-    "key": ("M0", "T1"),
-    "value": ("F5",),
-    "input": ("s3",),
-    "tail": ("M1", "T2", "S3", "N0", "F6", "M2", "N1", "S4", "F7", "s4", "T3", "N2", "S5", "M3"),
-    "last": ("T4", "S6", "N3", "M4", "T5", "s5", "S7", "N4", "M5", "T6", "N5", "M6", "T7")
-    + ("N6", "M7", "N7"),
+    "down0": ((C, 0),),
+    "down1": ((C, 1),),
+    "down2": ((C, 2), (F, 0),),
+    "up_back": {
+        1: ((F, 1),),
+    },
+    "grad_up": {
+        2: ((C, 3),),
+        3: ((S, 0),),
+        5: ((C, 4),),
+        6: ((F, 2),),
+        8: ((C, 5),),
+        11: ((C, 6),),
+    },
+    "norm": ((V, 0),),
+    "out": ((C, 7), (S, 1), (T, 0),),
+    "datt": ((F, 3),),
+    "pairs": {
+        0: ((V, 1),),
+        1: ((S, 2), (T, 1),),
+        2: ((F, 4),),
+        3: ((M, 0), (S, 3), (T, 2), (F, 5),),
+        4: ((M, 1), (S, 4), (V, 2),),
+        5: ((C, 8), (N, 0), (T, 3),),
+    },
+    "query": ((C, 9), (F, 6), (M, 2),),
+    "key": ((C, 10), (T, 4), (S, 5), (F, 8), (N, 1),),
+    "value": ((C, 11), (C, 12), (M, 3), (V, 3),),
+    "input": ((M, 4), (T, 5), (N, 2), (F, 7), (S, 6),),
+    "dxdone": (
+        (N, 4), (N, 3), (S, 8), (S, 7), (M, 5), (F, 9), (T, 6), (F, 10), (T, 7), (T, 8),
+        (M, 6), (N, 5),
+    ),
+    "tail": (
+        (M, 7), (S, 9), (S, 10), (N, 6), (M, 8), (T, 9), (F, 11), (V, 4), (F, 12), (T, 10),
+        (N, 7), (M, 9), (S, 11), (N, 8), (T, 11), (M, 10), (S, 12), (T, 12), (N, 9), (M, 11),
+        (N, 10), (M, 12), (N, 11), (N, 12), (V, 5),
+    ),
 }
 
 

time: 157 us -> 131 us (0.83)
  Pallas kernels: 156 us -> 130 us
    pallas_call x1, Pallas kernels: 152 us -> 126 us  [layer(): pl.pallas_call(functools.partial(layer_kernel, names, reduce), out_shape=...]
where the time goes in v5:
time: 131 us
  Pallas kernels  130 us (99%)
    pallas_call x1, Pallas kernels, layer(): pl.pallas_call(functools.partial(layer_kernel, names, reduce), out_shape=...  126 us
    pallas_call x1, Pallas kernels, finish(): pl.pallas_call(finish_kernel, out_shape=[low, low] + [jax.ShapeDtypeStruc...  3.9 us

profile of v5, /device:TPU:0, one launch (start us, length us, event | category | flops | bytes accessed | tf_op | source)
XLA Modules:
  0.0 131.1 jit_solution(13554002774992240881)
XLA Ops:
  0.7 126.4 %layer.1 = (bf16[2,128,768]{2,1,0:T(8,128)(2,1)}, bf16[2,128,768]{2,1,0:T(8,128)(2,1)}, bf16[1248,768]{1,0:T(8,128)(2,1)}, f32[8,768]{1,0:T(8,128)}) custom-call(s32[2]{0:T(128)} %bitcast.13, bf16[2,128,768]{2,1,0:T(8,128)(2,1)} %bitcast.10, bf16[2,128,768]{2,1,0:T(8,128)(2,1)} %bitcast.11, s32[2,2,128]{2,1,0:T(2,128)} %bitcast.12, ...), custom_call_target="tpu_custom_call" | custom-call | tf_op jit(solution)/shard_map/layer/pallas_call | solution.py:894
  127.1 3.9 %finish.1 = (bf16[2,128,768]{2,1,0:T(8,128)(2,1)}, bf16[2,128,768]{2,1,0:T(8,128)(2,1)}, f32[96,768]{1,0:T(8,128)}, f32[96,768]{1,0:T(8,128)}, f32[96,768]{1,0:T...) custom-call(bf16[1248,768]{1,0:T(8,128)(2,1)} %get-tuple-element.32., ...), custom_call_target="tpu_custom_call" | custom-call | tf_op jit(solution)/shard_map/finish/pallas_call | solution.py:928

commit v6 on v5

--- a/solution.py
+++ b/solution.py
@@ -387,6 +387,14 @@
         r.r1 = tuple(getattr(r, "r1_%d" % u) for u in range(len(CHUNKS)))
         red = Reduction(r, net, dp, z)
 
+    def kept(u):
+        rows = pl.ds(CHUNKS[u][3], CHUNKS[u][2])
+        return pltpu.make_async_copy(r.sums.at[rows], r.share.at[rows], r.keep_sem.at[u])
+
+    def whole(u):
+        red.fourth(u)
+        kept(u).start()
+
     def run(*steps):
         if not reduce:
             return
@@ -402,7 +410,7 @@
             elif kind == M:
                 pl.when(is_mid)(functools.partial(red.third, u, True))
             elif kind == N:
-                pl.when(is_mid)(functools.partial(red.fourth, u))
+                pl.when(is_mid)(functools.partial(whole, u))
             else:
                 red.small(u)
 
@@ -582,12 +590,10 @@
         bias = r.vectors[pl.ds(tile // 3, 1), part]
         value = nn(r.low[...], r.pool[0, y, x, :, part]) + bias
         below = 0.5 * (1.0 + lax.erf(value * np.float32(np.sqrt(0.5))))
-        dense = jnp.exp(value * value * -0.5) * np.float32(1.0 / np.sqrt(2.0 * np.pi))
         r.act[:, cols] = (value * below).astype(BF)
-        slope = below + value * dense
-        top = slope.astype(BF)
+        top = value.astype(BF)
         r.g[0, y, x, 0:256, part] = top
-        r.g[1, y, x, 0:256, part] = (slope - top.astype(F32)).astype(BF)
+        r.g[1, y, x, 0:256, part] = (value - top.astype(F32)).astype(BF)
         return carry
 
     lax.fori_loop(0, 12, up, 0)
@@ -618,15 +624,18 @@
         r.res[rows, :] = dres
         r.dlow[rows, :] = dres.astype(BF)
 
-    def grad_down(offset, size, share, carry):
-        cols = pl.ds(pl.multiple_of(384 * share + offset, 128), size)
-        r.g[share % 2, share // 4, share // 2 % 2, 384 + offset : 384 + offset + size, :] = tn(
-            r.act[:, cols], r.dlow[...]
-        ).astype(BF)
-        return carry
+    def grad_down(offset):
+        for quad in range(2):
+            shares = range(4 * quad, 4 * quad + 4)
+            starts = [384 * share + offset for share in shares]
+            left = jnp.concatenate([r.act[:, at : at + 128] for at in starts], axis=1)
+            part = tn(left, r.dlow[...]).astype(BF)
+            for i, share in enumerate(shares):
+                place = (share % 2, share // 4, share // 2 % 2, pl.ds(384 + offset, 128))
+                r.g[place] = part[128 * i : 128 * i + 128]
 
     for third in range(3):
-        lax.fori_loop(0, 8, functools.partial(grad_down, 128 * third, 128), 0)
+        grad_down(128 * third)
         run_plan("down%d" % third)
     stores = {}
 
@@ -662,7 +671,10 @@
     def up_back(tile, carry):
         cols = pl.ds(pl.multiple_of(256 * tile, 256), 256)
         y, x, part = up_tile(tile)
-        slope = r.g[0, y, x, 0:256, part].astype(F32) + r.g[1, y, x, 0:256, part].astype(F32)
+        value = r.g[0, y, x, 0:256, part].astype(F32) + r.g[1, y, x, 0:256, part].astype(F32)
+        below = 0.5 * (1.0 + lax.erf(value * np.float32(np.sqrt(0.5))))
+        dense = jnp.exp(value * value * -0.5) * np.float32(1.0 / np.sqrt(2.0 * np.pi))
+        slope = below + value * dense
         push = nt(r.dlow[...], r.pool[1, y, x, part, :]) * slope
         low = push.astype(BF)
         r.act[:, cols] = low
@@ -747,8 +759,7 @@
         def _():
             for u in range(len(CHUNKS)):
                 net.got("z3%d" % u)
-
-        store("share", lambda: r.sums, lambda: r.share)
+                kept(u).start()
     else:
         store("small", lambda: r.sm.at[0], lambda: r.small)
         store("share", lambda: r.g, lambda: r.share.at[0])
@@ -758,7 +769,11 @@
     given_back("o", r.hidden_out)
     given_back("d", r.input_grad)
     stored("small")
-    stored("share")
+    if reduce:
+        for u in range(len(CHUNKS)):
+            kept(u).wait()
+    else:
+        stored("share")
 
     @pl.when(own)
     def _():
@@ -887,7 +902,7 @@
         ("small", (8, 768), F32),
     )
     shapes = scratch(reduce)
-    sems = ("send_sem", "recv_sem", "post_sem", "load_sem", "store_sem")
+    sems = ("send_sem", "recv_sem", "post_sem", "load_sem", "store_sem", "keep_sem")
     names = tuple(i[0] for i in ins) + tuple(o[0] for o in outs)
     names += tuple(s[0] for s in shapes) + sems
     dma = pltpu.SemaphoreType.DMA
@@ -897,7 +912,7 @@
         in_specs=[i[2] for i in ins],
         out_specs=[any_space] * len(outs),
         scratch_shapes=[pltpu.VMEM(s[1], s[2]) for s in shapes]
-        + [dma((len(i),)) for i in (SENDS, SENDS, POSTS, LOADS, STORES)],
+        + [dma((len(i),)) for i in (SENDS, SENDS, POSTS, LOADS, STORES, CHUNKS)],
         compiler_params=pltpu.CompilerParams(
             vmem_limit_bytes=VMEM_LIMIT, collective_id=0, has_side_effects=True
         ),

time: 131 us -> 128 us (0.977)
  Pallas kernels: 130 us -> 127 us
    pallas_call x1, Pallas kernels: 126 us -> 123 us  [layer(): pl.pallas_call(functools.partial(layer_kernel, names, reduce), out_shape=...]
where the time goes in v6:
time: 128 us
  Pallas kernels  127 us (99%)
    pallas_call x1, Pallas kernels, layer(): pl.pallas_call(functools.partial(layer_kernel, names, reduce), out_shape=...  123 us
    pallas_call x1, Pallas kernels, finish(): pl.pallas_call(finish_kernel, out_shape=[low, low] + [jax.ShapeDtypeStruc...  3.9 us

profile of v6, /device:TPU:0, one launch (start us, length us, event | category | flops | bytes accessed | tf_op | source)
XLA Modules:
  0.0 128.2 jit_solution(16165948135158249774)
XLA Ops:
  0.7 123.5 %layer.1 = (bf16[2,128,768]{2,1,0:T(8,128)(2,1)}, bf16[2,128,768]{2,1,0:T(8,128)(2,1)}, bf16[1248,768]{1,0:T(8,128)(2,1)}, f32[8,768]{1,0:T(8,128)}) custom-call(s32[2]{0:T(128)} %bitcast.13, bf16[2,128,768]{2,1,0:T(8,128)(2,1)} %bitcast.10, bf16[2,128,768]{2,1,0:T(8,128)(2,1)} %bitcast.11, s32[2,2,128]{2,1,0:T(2,128)} %bitcast.12, ...), custom_call_target="tpu_custom_call" | custom-call | tf_op jit(solution)/shard_map/layer/pallas_call | solution.py:909
  124.2 3.9 %finish.1 = (bf16[2,128,768]{2,1,0:T(8,128)(2,1)}, bf16[2,128,768]{2,1,0:T(8,128)(2,1)}, f32[96,768]{1,0:T(8,128)}, f32[96,768]{1,0:T(8,128)}, f32[96,768]{1,0:T...) custom-call(bf16[1248,768]{1,0:T(8,128)(2,1)} %get-tuple-element.32., ...), custom_call_target="tpu_custom_call" | custom-call | tf_op jit(solution)/shard_map/finish/pallas_call | solution.py:943

commit v7 on v6

--- a/solution.py
+++ b/solution.py
@@ -555,7 +555,7 @@
         attend_pair(pair, live, r)
         return carry
 
-    lax.fori_loop(0, PAIRS, attend, 0)
+    lax.fori_loop(0, PAIRS, attend, 0, unroll=6)
 
     loaded("out")
     for tile in range(3):
@@ -596,7 +596,7 @@
         r.g[1, y, x, 0:256, part] = (value - top.astype(F32)).astype(BF)
         return carry
 
-    lax.fori_loop(0, 12, up, 0)
+    lax.fori_loop(0, 12, up, 0, unroll=12)
     for tile in range(3):
         cols = slice(256 * tile, 256 * tile + 256)
         r.res[:, cols] = r.res[:, cols] + sum(

time: 128 us -> 123 us (0.961)
  Pallas kernels: 127 us -> 122 us
    pallas_call x1, Pallas kernels: 123 us -> 119 us  [layer(): pl.pallas_call(functools.partial(layer_kernel, names, reduce), out_shape=...]
where the time goes in v7:
time: 123 us
  Pallas kernels  122 us (99%)
    pallas_call x1, Pallas kernels, layer(): pl.pallas_call(functools.partial(layer_kernel, names, reduce), out_shape=...  119 us
    pallas_call x1, Pallas kernels, finish(): pl.pallas_call(finish_kernel, out_shape=[low, low] + [jax.ShapeDtypeStruc...  3.9 us

profile of v7, /device:TPU:0, one launch (start us, length us, event | category | flops | bytes accessed | tf_op | source)
XLA Modules:
  0.0 123.3 jit_solution(12691545176134764383)
XLA Ops:
  0.7 118.5 %layer.1 = (bf16[2,128,768]{2,1,0:T(8,128)(2,1)}, bf16[2,128,768]{2,1,0:T(8,128)(2,1)}, bf16[1248,768]{1,0:T(8,128)(2,1)}, f32[8,768]{1,0:T(8,128)}) custom-call(s32[2]{0:T(128)} %bitcast.13, bf16[2,128,768]{2,1,0:T(8,128)(2,1)} %bitcast.10, bf16[2,128,768]{2,1,0:T(8,128)(2,1)} %bitcast.11, s32[2,2,128]{2,1,0:T(2,128)} %bitcast.12, ...), custom_call_target="tpu_custom_call" | custom-call | tf_op jit(solution)/shard_map/layer/pallas_call | solution.py:909
  119.2 3.9 %finish.1 = (bf16[2,128,768]{2,1,0:T(8,128)(2,1)}, bf16[2,128,768]{2,1,0:T(8,128)(2,1)}, f32[96,768]{1,0:T(8,128)}, f32[96,768]{1,0:T(8,128)}, f32[96,768]{1,0:T...) custom-call(bf16[1248,768]{1,0:T(8,128)(2,1)} %get-tuple-element.32., ...), custom_call_target="tpu_custom_call" | custom-call | tf_op jit(solution)/shard_map/finish/pallas_call | solution.py:943

commit v8 on v7

--- a/solution.py
+++ b/solution.py
@@ -87,10 +87,11 @@
 def attend_pair(pair, live, r):
     cols = pl.ds(pl.multiple_of(128 * pair, 128), 128)
     stack = head_stack(r.q[:, cols].astype(F32) * 0.125).astype(BF)
+    both_left = nt(stack, r.wr[0:384, cols])
+    both_right = nt(stack, r.wr[384:768, cols])
     for head in range(2):
         rows = slice(256 * head, 256 * head + 256)
-        left = nt(stack[rows], r.wr[0:384, cols])
-        right = nt(stack[rows], r.wr[384:768, cols])
+        left, right = both_left[rows], both_right[rows]
         sin, cos = r.sine[...], r.cosine[...]
         r.relq[rows, 0:384] = (left * sin + right * cos).astype(BF)
         r.relq[rows, 384:768] = (right * sin - left * cos).astype(BF)

time: 123 us -> 123 us (level)
  no operation moved by 1% of the time
where the time goes in v8:
time: 123 us
  Pallas kernels  122 us (99%)
    pallas_call x1, Pallas kernels, layer(): pl.pallas_call(functools.partial(layer_kernel, names, reduce), out_shape=...  118 us
    pallas_call x1, Pallas kernels, finish(): pl.pallas_call(finish_kernel, out_shape=[low, low] + [jax.ShapeDtypeStruc...  3.9 us

profile of v8, /device:TPU:0, one launch (start us, length us, event | category | flops | bytes accessed | tf_op | source)
XLA Modules:
  0.0 122.9 jit_solution(4471160871520876830)
XLA Ops:
  0.7 118.2 %layer.1 = (bf16[2,128,768]{2,1,0:T(8,128)(2,1)}, bf16[2,128,768]{2,1,0:T(8,128)(2,1)}, bf16[1248,768]{1,0:T(8,128)(2,1)}, f32[8,768]{1,0:T(8,128)}) custom-call(s32[2]{0:T(128)} %bitcast.13, bf16[2,128,768]{2,1,0:T(8,128)(2,1)} %bitcast.10, bf16[2,128,768]{2,1,0:T(8,128)(2,1)} %bitcast.11, s32[2,2,128]{2,1,0:T(2,128)} %bitcast.12, ...), custom_call_target="tpu_custom_call" | custom-call | tf_op jit(solution)/shard_map/layer/pallas_call | solution.py:910
  118.8 3.9 %finish.1 = (bf16[2,128,768]{2,1,0:T(8,128)(2,1)}, bf16[2,128,768]{2,1,0:T(8,128)(2,1)}, f32[96,768]{1,0:T(8,128)}, f32[96,768]{1,0:T(8,128)}, f32[96,768]{1,0:T...) custom-call(bf16[1248,768]{1,0:T(8,128)(2,1)} %get-tuple-element.32., ...), custom_call_target="tpu_custom_call" | custom-call | tf_op jit(solution)/shard_map/finish/pallas_call | solution.py:944
